TPU v7x, 32 devices: a whole 2x2x4 slice. The times are simulated.
32 devices in a mesh: groups: 2 (over x), row: 16 (over z, y, core).
Axes of the slice: x: 2, y: 2, z: 4, core: 2. Of those that a mesh axis runs over, the one named last changes fastest.
Arguments:
- coupling: bfloat16 [32768, 896], P(('groups', 'row')), parts along dimension 0, may hold values from -6 to 6
- column_block: bfloat16 [32768, 1536], P(('groups', 'row')), parts along dimension 0, may hold values from -6 to 6
- pivot_inverse: bfloat16 [3072, 1536], P(('groups', 'row')), parts along dimension 0, may hold values from -0.15625 to 0.15625
- row_panel: bfloat16 [1536, 1792], P(None, ('groups', 'row')), parts along dimension 1, may hold values from -0.15625 to 0.15625
Outputs:
- lower_panel: bfloat16 [32768, 1536], P(('groups', 'row')), parts along dimension 0
- schur: bfloat16 [32768, 896], P(('groups', 'row')), parts along dimension 0
There are 2 independent parts, one for each index of `groups`. A program takes and returns all parts, laid end to end along the dimension named above; each array names one. Nothing has to cross between parts.
All inputs are finite; a program needn't handle non-finite values.
Results may differ from a plain program's by a relative error of at most 0.0039.
Values may be sent and summed in bfloat16 or wider, within the bound.
No kernel may reach another device: no remote copies, remote signals or barrier semaphores. Data moves between devices by JAX's collectives and lax.ppermute only.
A program may use at most 64 MiB of HBM per device.

v0:
```python
import jax
import jax.numpy as jnp
from jax import lax
from jax.sharding import PartitionSpec as P


def on_device(coupling, column_block, pivot_inverse, row_panel):
    whole_inverse = lax.all_gather(pivot_inverse, "row", axis=0, tiled=True)
    lower_panel = jnp.dot(column_block, whole_inverse, preferred_element_type=jnp.float32).astype(
        jnp.bfloat16
    )
    product = jnp.dot(
        lower_panel,
        lax.all_gather(row_panel, "row", axis=1, tiled=True),
        preferred_element_type=jnp.float32,
    )
    schur = (coupling.astype(jnp.float32) - product).astype(jnp.bfloat16)
    return (lower_panel, schur)


def solution(mesh):
    placed = (
        P(("groups", "row"), None),
        P(("groups", "row"), None),
        P(("groups", "row"), None),
        P(None, ("groups", "row")),
    )
    return jax.shard_map(
        on_device,
        mesh=mesh,
        in_specs=placed,
        out_specs=(P(("groups", "row"), None), P(("groups", "row"), None)),
        check_vma=False,
    )
```

profile of v0, /device:TPU:0, one launch (start us, length us, event | category | flops | bytes accessed | tf_op | source)
XLA Modules:
  0.0 125.8 jit_solution(16534755584395549889)
XLA Ops:
  7.2 0.0 copy-start
  7.2 0.0 all-gather.3.cloned.1.call-start
  7.2 0.7 all-gather.3.cloned.1.call-update
  7.9 0.0 all-gather.5.cloned.1.call-start
  8.0 0.7 all-gather.5.cloned.1.call-update
  8.7 57.8 %all-gather.3.cloned.1.call-done = bf16[1536,1536]{1,0:T(8,128)(2,1)} async-done(((bf16[96,1536]{1,0:T(8,128)(2,1)}), bf16[1536,1536]{1,0:T(8,128)(2,1)}) %all-gather.3.cloned.1.call-update) | async-done | bytes 4718608 | tf_op jit(solution)/shard_map/all_gather | solution.py:8
  66.4 0.0 copy-done
  66.4 8.7 %convolution_convert_fusion = bf16[1024,1536]{1,0:T(8,128)(2,1)} fusion(bf16[1024,1536]{1,0:T(8,128)(2,1)S(1)} %copy-done, bf16[1536,1536]{1,0:T(8,128)(2,1)} %all-gather.3.cloned.1.call-done), kind=kOutput, calls=%fused_computation | convolution fusion | flops 4833411072 | bytes 11010048 | tf_op jit(solution)/shard_map/dot_general | solution.py:9
  75.1 35.9 %all-gather.5.cloned.1.call-done = bf16[1536,896]{0,1:T(8,128)(2,1)} async-done(((bf16[1536,56]{0,1:T(8,128)(2,1)}), bf16[1536,896]{0,1:T(8,128)(2,1)}) %all-gather.5.cloned.1.call-update) | async-done | bytes 2752528 | tf_op jit(solution)/shard_map/all_gather | solution.py:14
  111.0 7.9 %subtract_convert_fusion = bf16[1024,896]{1,0:T(8,128)(2,1)} fusion(bf16[1024,896]{1,0:T(8,128)(2,1)} %param.4, bf16[1024,1536]{1,0:T(8,128)(2,1)} %convolution_convert_fusion, bf16[1536,896]{0,1:T(8,128)(2,1)} %all-gather.5.cloned.1.call-done), kind=kOutput, calls=%fused_computation.1 | convolution fusion | flops 2821324800 | bytes 9568256 | tf_op jit(solution)/shard_map/dot_general | solution.py:12
Async XLA Ops:
  7.2 59.3 %copy-start = (bf16[1024,1536]{1,0:T(8,128)(2,1)S(1)}, bf16[1024,1536]{1,0:T(8,128)(2,1)}, u32[]{:S(2)}) copy-start(bf16[1024,1536]{1,0:T(8,128)(2,1)} %param.5) | copy-start | bytes 9437188
  7.2 59.2 %all-gather.3.cloned.1.call-start = ((), (), s32[]{:S(2)}) async-start(), calls=%async_computation | async-start | bytes 5013504 | tf_op jit(solution)/shard_map/all_gather | solution.py:8
  7.9 103.1 %all-gather.5.cloned.1.call-start = ((), (), s32[]{:S(2)}) async-start(), calls=%async_computation.1 | async-start | bytes 2924544 | tf_op jit(solution)/shard_map/all_gather | solution.py:14
Sparse Core Ops, SparseCore 0:
  10.3 56.0 all-gather.2
  68.7 42.2 all-gather.4
where the time goes:
time: 126 us
  waiting for transfers between devices  95 us (75%)
  matrix products  16.6 us (13%)
  between operations  14 us (11%)
    all_gather x1, waiting for transfers between devices, on_device(): whole_inverse = lax.all_gather(pivot_inverse, 'row', axis=0, tiled=True)  57.8 us
    all_gather x1, waiting for transfers between devices, on_device(): lax.all_gather(row_panel, 'row', axis=1, tiled=True)  35.9 us
    dot_general x1, matrix products, on_device(): jnp.dot(column_block, whole_inverse, preferred_element_type=jnp.float32)  8.69 us
    dot_general x1, matrix products, on_device(): jnp.dot(lower_panel, lax.all_gather(row_panel, 'row', axis=1, tiled=True)...  7.92 us
  transfers between devices with their start and end apart: 2, of which 2 were waited for; matrix products, arithmetic and copies ran while one was open for 7% of the time, Pallas kernels for 0%

commit v1 on v0

v1 whole, which is shorter than its diff:
```python
import functools

import jax
import jax.numpy as jnp
from jax import lax
from jax.experimental import pallas as pl
from jax.experimental.pallas import tpu as pltpu
from jax.sharding import PartitionSpec as P

F32, BF16 = jnp.float32, jnp.bfloat16
ON_CHIP = pl.BlockSpec(memory_space=pltpu.VMEM)
IN_PLACE = pl.BlockSpec(memory_space=pl.ANY)
PARAMS = pltpu.CompilerParams(vmem_limit_bytes=40 << 20)


def shape(*dims):
    return jax.ShapeDtypeStruct(dims, BF16)


def cost(flops, nbytes):
    return pl.CostEstimate(flops=flops, bytes_accessed=nbytes, transcendentals=0)


def ring_of(chips):
    if chips > 8:
        return list(range(chips))
    return list(range(0, chips, 2)) + list(range(chips - 1, 0, -2))


def distances(chips):
    near = [0]
    for k in range(1, (chips + 1) // 2):
        near += [-k, k]
    return near + ([chips // 2] if chips % 2 == 0 else [])


def chip_at(distance, chips):
    chip = lax.axis_index("row") // 2
    if chips > 8:
        return lax.rem(chip + distance + chips, chips)
    place = jnp.where(lax.rem(chip, 2) == 0, chip // 2, chips - 1 - chip // 2)
    place = lax.rem(place + distance + chips, chips)
    return jnp.where(place < chips // 2, 2 * place, 2 * (chips - 1 - place) + 1)


def my_core():
    return lax.rem(lax.axis_index("row"), 2)


def split_kernel(shard, mine, theirs):
    half = mine.shape[1]
    first = my_core() == 0
    left, right = shard[:, :half], shard[:, half:]
    mine[...] = jnp.where(first, left, right)
    theirs[...] = jnp.where(first, right, left)


def split(shard):
    rows, cols = shard.shape
    return pl.pallas_call(
        split_kernel,
        out_shape=(shape(rows, cols // 2),) * 2,
        in_specs=[ON_CHIP],
        out_specs=(ON_CHIP, ON_CHIP),
        compiler_params=PARAMS,
        name="split",
    )(shard)


def place_kernel(chips, *refs):
    pieces, whole, sems = refs[:-2], refs[-2], refs[-1]
    rows = pieces[0].shape[0]
    copies = []
    for i, distance in enumerate(distances(chips)):
        chip = chip_at(distance, chips)
        for stream in range(2):
            core = my_core() if stream == 0 else 1 - my_core()
            at = pl.multiple_of((2 * chip + core) * rows, 8)
            j = 2 * i + stream
            copies.append(pltpu.make_async_copy(pieces[j], whole.at[pl.ds(at, rows)], sems.at[j]))
    for copy in copies:
        copy.start()
    for copy in copies:
        copy.wait()


def place(pieces, chips, name):
    rows, cols = pieces[0].shape
    return pl.pallas_call(
        functools.partial(place_kernel, chips),
        out_shape=shape(rows * len(pieces), cols),
        in_specs=[ON_CHIP] * len(pieces),
        out_specs=ON_CHIP,
        scratch_shapes=[pltpu.SemaphoreType.DMA((len(pieces),))],
        compiler_params=PARAMS,
        cost_estimate=cost(0, 4 * rows * len(pieces) * cols),
        name=name,
    )(*pieces)


def lower_kernel(own, *refs):
    column, panel = refs[:2]
    out, kept, sems = refs[-3:]
    half = panel.shape[1]
    core = my_core() if own else 1 - my_core()
    cols = pl.ds(pl.multiple_of(core * half, 128), half)
    rows = column.shape[0] // 4
    copies = []
    for i in range(4):
        at = pl.ds(i * rows, rows)
        kept[at] = jnp.dot(column[at], panel[...], preferred_element_type=F32).astype(BF16)
        copies.append(pltpu.make_async_copy(kept.at[at], out.at[at, cols], sems.at[i]))
        copies[-1].start()
    for copy in copies:
        copy.wait()


def lower(column_block, panel, so_far):
    own = so_far is None
    n, k = column_block.shape
    half = panel.shape[1]
    return pl.pallas_call(
        functools.partial(lower_kernel, own),
        out_shape=(shape(n, 2 * half), shape(n, half)),
        in_specs=[ON_CHIP, ON_CHIP] + ([] if own else [IN_PLACE]),
        out_specs=(IN_PLACE, ON_CHIP),
        scratch_shapes=[pltpu.SemaphoreType.DMA((4,))],
        input_output_aliases={} if own else {2: 0},
        compiler_params=PARAMS,
        cost_estimate=cost(2 * n * k * half, 2 * (n * k + k * half + n * half)),
        name="lower_own" if own else "lower_other",
    )(column_block, panel, *([] if own else [so_far]))


def schur_kernel(own_lower, own_panel, other_lower, other_panel, coupling, out, done, sems):
    rows = coupling.shape[0] // 4
    contract = (((1,), (1,)), ((), ()))
    copies = []
    for i in range(4):
        at = pl.ds(i * rows, rows)
        product = lax.dot_general(own_lower[at], own_panel[...], contract, preferred_element_type=F32)
        product += lax.dot_general(other_lower[at], other_panel[...], contract, preferred_element_type=F32)
        done[at] = (coupling[at].astype(F32) - product).astype(BF16)
        copies.append(pltpu.make_async_copy(done.at[at], out.at[at], sems.at[i]))
        copies[-1].start()
    for copy in copies:
        copy.wait()


def schur(own_lower, own_panel, other_lower, other_panel, coupling):
    n, cols = coupling.shape
    k = 2 * own_lower.shape[1]
    return pl.pallas_call(
        schur_kernel,
        out_shape=shape(n, cols),
        in_specs=[ON_CHIP] * 5,
        out_specs=IN_PLACE,
        scratch_shapes=[pltpu.VMEM((n, cols), BF16), pltpu.SemaphoreType.DMA((4,))],
        compiler_params=PARAMS,
        cost_estimate=cost(2 * n * k * cols, 2 * (n * k + k * cols + 2 * n * cols)),
        name="schur",
    )(own_lower, own_panel, other_lower, other_panel, coupling)


def gather_half(shard, chips, up, down, swap):
    mine, theirs = split(shard)
    rising = [mine, lax.ppermute(theirs, "row", swap)]
    falling = list(rising)
    got = {(s, 0): rising[s] for s in range(2)}
    for k in range(1, chips // 2 + 1):
        last = 2 * k == chips
        for s in range(2):
            if not (last and s == 1):
                rising[s] = lax.ppermute(rising[s], "row", up)
                got[s, k if last else -k] = rising[s]
            if not (last and s == 0):
                falling[s] = lax.ppermute(falling[s], "row", down)
                got[s, k] = falling[s]
    return [got[s, d] for d in distances(chips) for s in range(2)]


def on_device(devices, coupling, column_block, pivot_inverse, row_panel):
    chips = devices // 2
    ring = ring_of(chips)
    swap = [(i, i ^ 1) for i in range(devices)]
    up = [(2 * ring[i] + c, 2 * ring[(i + 1) % chips] + c) for i in range(chips) for c in range(2)]
    down = [(to, at) for at, to in up]
    pieces = gather_half(pivot_inverse, chips, up, down, swap)
    own_p = place(pieces, chips, "place_p")
    shard, gate = lax.optimization_barrier((row_panel.T, pieces[2 * (chips - 4)]))
    own_r = place(gather_half(shard, chips, up, down, swap), chips, "place_r")
    other_p = lax.ppermute(own_p, "row", swap)
    other_r = lax.ppermute(own_r, "row", swap)
    lower_panel, own_lower = lower(column_block, own_p, None)
    lower_panel, other_lower = lower(column_block, other_p, lower_panel)
    return lower_panel, schur(own_lower, own_r, other_lower, other_r, coupling)


def by_all_gather(coupling, column_block, pivot_inverse, row_panel):
    whole_inverse = lax.all_gather(pivot_inverse, "row", axis=0, tiled=True)
    whole_panel = lax.all_gather(row_panel, "row", axis=1, tiled=True)
    lower_panel = jnp.dot(column_block, whole_inverse, preferred_element_type=F32).astype(BF16)
    product = jnp.dot(lower_panel, whole_panel, preferred_element_type=F32)
    return lower_panel, (coupling.astype(F32) - product).astype(BF16)


def solution(mesh):
    devices = mesh.shape["row"]
    parts = mesh.shape["groups"]

    def step(coupling, column_block, pivot_inverse, row_panel):
        aligned = row_panel.shape[1] // (parts * devices) % 8 == 0
        aligned &= pivot_inverse.shape[0] // (parts * devices) % 8 == 0
        body = functools.partial(on_device, devices) if aligned else by_all_gather
        rows = P(("groups", "row"), None)
        return jax.shard_map(
            body,
            mesh=mesh,
            in_specs=(rows, rows, rows, P(None, ("groups", "row"))),
            out_specs=(rows, rows),
            check_vma=False,
        )(coupling, column_block, pivot_inverse, row_panel)

    return step
```

time: 126 us -> 71.8 us (0.57)
  waiting for transfers between devices: 95 us -> 16.6 us
  starting transfers between devices: 0.08 us -> 36.3 us
  Pallas kernels: 0 us -> 17 us
  matrix products: 16.6 us -> 0 us
  between operations: 14 us -> 0.78 us
    all_gather x2 -> x0, waiting for transfers between devices: 93.7 us -> none  [the longest x1 57.8 us: on_device(): whole_inverse = lax.all_gather(pivot_inverse, 'row', axis=0, tiled=True)]
    ppermute x0 -> x32, starting transfers between devices: none -> 36.3 us  [the longest x14 18.3 us: gather_half(): falling[s] = lax.ppermute(falling[s], 'row', down)]
    pallas_call x0 -> x7, Pallas kernels: none -> 17 us  [the longest x2 6.77 us: lower(): pl.pallas_call(functools.partial(lower_kernel, own), out_shape=(shape(n,...]
    ppermute x0 -> x32, waiting for transfers between devices: none -> 16.6 us  [the longest x14 9.81 us: gather_half(): falling[s] = lax.ppermute(falling[s], 'row', down)]
    dot_general x2 -> x0, matrix products: 16.6 us -> none  [the longest x1 8.69 us: on_device(): jnp.dot(column_block, whole_inverse, preferred_element_type=jnp.float32)]
    unnamed x2 -> x0, waiting for transfers between devices: 1.38 us -> none
  transfers between devices with their start and end apart: 2 -> 32, of which waited for: 2 -> 14; matrix products, arithmetic and copies ran while one was open for 7% -> 0% of each run, Pallas kernels for 0% -> 13%
where the time goes in v1:
time: 71.8 us; the launch traced here: 71.6 us
  starting transfers between devices  36.3 us (51%)
  Pallas kernels  17 us (24%)
  waiting for transfers between devices  16.6 us (23%)
  local copies, waits for them, and re-layouts  0.97 us (1%)
  between operations  0.78 us (1%)
    ppermute x14, starting transfers between devices, gather_half(): falling[s] = lax.ppermute(falling[s], 'row', down)  18.3 us
    ppermute x14, starting transfers between devices, gather_half(): rising[s] = lax.ppermute(rising[s], 'row', up)  16.7 us
    ppermute x14, waiting for transfers between devices, gather_half(): falling[s] = lax.ppermute(falling[s], 'row', down)  9.81 us
    pallas_call x2, Pallas kernels, lower(): pl.pallas_call(functools.partial(lower_kernel, own), out_shape=(shape(n,...  6.77 us
    pallas_call x2, Pallas kernels, place(): pl.pallas_call(functools.partial(place_kernel, chips), out_shape=shape(ro...  5.88 us
    ppermute x14, waiting for transfers between devices, gather_half(): rising[s] = lax.ppermute(rising[s], 'row', up)  4.34 us
    pallas_call x1, Pallas kernels, schur(): pl.pallas_call(schur_kernel, out_shape=shape(n, cols), in_specs=[ON_CHIP]...  4.25 us
    ppermute x2, waiting for transfers between devices, gather_half(): rising = [mine, lax.ppermute(theirs, 'row', swap)]  2.47 us
  transfers between devices with their start and end apart: 32, of which 14 were waited for; matrix products, arithmetic and copies ran while one was open for 0% of the time, Pallas kernels for 13%

profile of v1, /device:TPU:0, one launch (start us, length us, event | category | flops | bytes accessed | tf_op | source)
XLA Modules:
  0.0 71.6 jit_solution(4415975156185436477)
XLA Ops:
  2.1 2.6 %collective-permute-start.1 = (bf16[96,768]{1,0:T(8,128)(2,1)S(1)}, bf16[96,768]{1,0:T(8,128)(2,1)S(1)}, u32[]{:S(2)}, u32[]{:S(2)}) collective-permute-start(bf16[96,768]{1,0:T(8,128)(2,1)S(1)} %get-tuple-element.11.refs_0_), channel_id=1, source_target_pairs={{0,4},{1,5},{4,8},{5,9},{8,12},{9,13},{12,14},{13,15},{14,10},{15,... | collective-permute-start | bytes 442376 | tf_op jit(solution)/shard_map/ppermute | solution.py:174
  4.8 1.2 %collective-permute-start.4 = (bf16[96,768]{1,0:T(8,128)(2,1)S(1)}, bf16[96,768]{1,0:T(8,128)(2,1)S(1)}, u32[]{:S(2)}, u32[]{:S(2)}) collective-permute-start(bf16[96,768]{1,0:T(8,128)(2,1)S(1)} %collective-permute-done.refs_1_), channel_id=1, source_target_pairs={{4,0},{5,1},{8,4},{9,5},{12,8},{13,9},{14,12},{15,13},{10,14},{11,... | collective-permute-start | bytes 442376 | tf_op jit(solution)/shard_map/ppermute | solution.py:177
  6.0 1.6 %collective-permute-start.3 = (bf16[96,768]{1,0:T(8,128)(2,1)S(1)}, bf16[96,768]{1,0:T(8,128)(2,1)S(1)}, u32[]{:S(2)}, u32[]{:S(2)}) collective-permute-start(bf16[96,768]{1,0:T(8,128)(2,1)S(1)} %get-tuple-element.11.refs_0_), channel_id=1, source_target_pairs={{4,0},{5,1},{8,4},{9,5},{12,8},{13,9},{14,12},{15,13},{10,14},{11,... | collective-permute-start | bytes 442376 | tf_op jit(solution)/shard_map/ppermute | solution.py:177
  8.1 1.1 %collective-permute-done.1.refs_2_ = bf16[96,768]{1,0:T(8,128)(2,1)S(1)} collective-permute-done((bf16[96,768]{1,0:T(8,128)(2,1)S(1)}, bf16[96,768]{1,0:T(8,128)(2,1)S(1)}, u32[]{:S(2)}, u32[]{:S(2)}) %collective-permute-start.1) | collective-permute-done | bytes 147488 | tf_op jit(solution)/shard_map/ppermute | solution.py:174
  9.2 2.3 %collective-permute-start.5 = (bf16[96,768]{1,0:T(8,128)(2,1)S(1)}, bf16[96,768]{1,0:T(8,128)(2,1)S(1)}, u32[]{:S(2)}, u32[]{:S(2)}) collective-permute-start(bf16[96,768]{1,0:T(8,128)(2,1)S(1)} %collective-permute-done.1.refs_2_), channel_id=1, source_target_pairs={{0,4},{1,5},{4,8},{5,9},{8,12},{9,13},{12,14},{13,15},{14,10},{15,... | collective-permute-start | bytes 442376 | tf_op jit(solution)/shard_map/ppermute | solution.py:174
  11.5 1.2 %collective-permute-start.8 = (bf16[96,768]{1,0:T(8,128)(2,1)S(1)}, bf16[96,768]{1,0:T(8,128)(2,1)S(1)}, u32[]{:S(2)}, u32[]{:S(2)}) collective-permute-start(bf16[96,768]{1,0:T(8,128)(2,1)S(1)} %collective-permute-done.4.refs_5_), channel_id=1, source_target_pairs={{4,0},{5,1},{8,4},{9,5},{12,8},{13,9},{14,12},{15,13},{10,14},{11,... | collective-permute-start | bytes 442376 | tf_op jit(solution)/shard_map/ppermute | solution.py:177
  12.7 1.9 %collective-permute-done.3.refs_4_ = bf16[96,768]{1,0:T(8,128)(2,1)S(1)} collective-permute-done((bf16[96,768]{1,0:T(8,128)(2,1)S(1)}, bf16[96,768]{1,0:T(8,128)(2,1)S(1)}, u32[]{:S(2)}, u32[]{:S(2)}) %collective-permute-start.3) | collective-permute-done | bytes 147488 | tf_op jit(solution)/shard_map/ppermute | solution.py:177
  14.7 1.2 %collective-permute-start.7 = (bf16[96,768]{1,0:T(8,128)(2,1)S(1)}, bf16[96,768]{1,0:T(8,128)(2,1)S(1)}, u32[]{:S(2)}, u32[]{:S(2)}) collective-permute-start(bf16[96,768]{1,0:T(8,128)(2,1)S(1)} %collective-permute-done.3.refs_4_), channel_id=1, source_target_pairs={{4,0},{5,1},{8,4},{9,5},{12,8},{13,9},{14,12},{15,13},{10,14},{11,... | collective-permute-start | bytes 442376 | tf_op jit(solution)/shard_map/ppermute | solution.py:177
  16.7 1.6 %collective-permute-start.9 = (bf16[96,768]{1,0:T(8,128)(2,1)S(1)}, bf16[96,768]{1,0:T(8,128)(2,1)S(1)}, u32[]{:S(2)}, u32[]{:S(2)}) collective-permute-start(bf16[96,768]{1,0:T(8,128)(2,1)S(1)} %collective-permute-done.5.refs_6_), channel_id=1, source_target_pairs={{0,4},{1,5},{4,8},{5,9},{8,12},{9,13},{12,14},{13,15},{14,10},{15,... | collective-permute-start | bytes 442376 | tf_op jit(solution)/shard_map/ppermute | solution.py:174
  18.3 1.2 %collective-permute-start.12 = (bf16[96,768]{1,0:T(8,128)(2,1)S(1)}, bf16[96,768]{1,0:T(8,128)(2,1)S(1)}, u32[]{:S(2)}, u32[]{:S(2)}) collective-permute-start(bf16[96,768]{1,0:T(8,128)(2,1)S(1)} %collective-permute-done.8.refs_9_), channel_id=1, source_target_pairs={{4,0},{5,1},{8,4},{9,5},{12,8},{13,9},{14,12},{15,13},{10,14},{11,... | collective-permute-start | bytes 442376 | tf_op jit(solution)/shard_map/ppermute | solution.py:177
  19.5 1.9 %collective-permute-done.7.refs_8_ = bf16[96,768]{1,0:T(8,128)(2,1)S(1)} collective-permute-done((bf16[96,768]{1,0:T(8,128)(2,1)S(1)}, bf16[96,768]{1,0:T(8,128)(2,1)S(1)}, u32[]{:S(2)}, u32[]{:S(2)}) %collective-permute-start.7) | collective-permute-done | bytes 147488 | tf_op jit(solution)/shard_map/ppermute | solution.py:177
  21.4 1.2 %collective-permute-start.11 = (bf16[96,768]{1,0:T(8,128)(2,1)S(1)}, bf16[96,768]{1,0:T(8,128)(2,1)S(1)}, u32[]{:S(2)}, u32[]{:S(2)}) collective-permute-start(bf16[96,768]{1,0:T(8,128)(2,1)S(1)} %collective-permute-done.7.refs_8_), channel_id=1, source_target_pairs={{4,0},{5,1},{8,4},{9,5},{12,8},{13,9},{14,12},{15,13},{10,14},{11,... | collective-permute-start | bytes 442376 | tf_op jit(solution)/shard_map/ppermute | solution.py:177
  23.5 1.6 %collective-permute-start.13 = (bf16[96,768]{1,0:T(8,128)(2,1)S(1)}, bf16[96,768]{1,0:T(8,128)(2,1)S(1)}, u32[]{:S(2)}, u32[]{:S(2)}) collective-permute-start(bf16[96,768]{1,0:T(8,128)(2,1)S(1)} %collective-permute-done.9.refs_10_), channel_id=1, source_target_pairs={{0,4},{1,5},{4,8},{5,9},{8,12},{9,13},{12,14},{13,15},{14,10},{15,... | collective-permute-start | bytes 442376 | tf_op jit(solution)/shard_map/ppermute | solution.py:174
  25.1 1.2 %collective-permute-start.14 = (bf16[96,768]{1,0:T(8,128)(2,1)S(1)}, bf16[96,768]{1,0:T(8,128)(2,1)S(1)}, u32[]{:S(2)}, u32[]{:S(2)}) collective-permute-start(bf16[96,768]{1,0:T(8,128)(2,1)S(1)} %collective-permute-done.12.refs_13_), channel_id=1, source_target_pairs={{4,0},{5,1},{8,4},{9,5},{12,8},{13,9},{14,12},{15,13},{10,14},{11,... | collective-permute-start | bytes 442376 | tf_op jit(solution)/shard_map/ppermute | solution.py:177
  26.3 1.8 %collective-permute-done.11.refs_12_ = bf16[96,768]{1,0:T(8,128)(2,1)S(1)} collective-permute-done((bf16[96,768]{1,0:T(8,128)(2,1)S(1)}, bf16[96,768]{1,0:T(8,128)(2,1)S(1)}, u32[]{:S(2)}, u32[]{:S(2)}) %collective-permute-start.11) | collective-permute-done | bytes 147488 | tf_op jit(solution)/shard_map/ppermute | solution.py:177
  28.1 1.3 %collective-permute-done.13.refs_14_ = bf16[96,768]{1,0:T(8,128)(2,1)S(1)} collective-permute-done((bf16[96,768]{1,0:T(8,128)(2,1)S(1)}, bf16[96,768]{1,0:T(8,128)(2,1)S(1)}, u32[]{:S(2)}, u32[]{:S(2)}) %collective-permute-start.13) | collective-permute-done | bytes 147488 | tf_op jit(solution)/shard_map/ppermute | solution.py:174
  30.2 3.7 %place_p.1.refs_1_ = bf16[1536,768]{1,0:T(8,128)(2,1)S(1)} custom-call(bf16[96,768]{1,0:T(8,128)(2,1)S(1)} %get-tuple-element.11.refs_0_, bf16[96,768]{1,0:T(8,128)(2,1)S(1)} %collective-permute-done.refs_1_, bf16[96,768]{1,0:T(8,128)(2,1)S(1)} %collective-permute-done.1.refs_2_, bf16[96,768]{1,0:T(8,128)(2,1)S(1)} %collective-permute-done.2.refs_3_, ...), custom_call_target="tpu_custom_call" | custom-call | bytes 4718592 | tf_op jit(solution)/shard_map/place_p/pallas_call | solution.py:89
  34.6 1.6 %collective-permute-start.17 = (bf16[56,768]{1,0:T(8,128)(2,1)S(1)}, bf16[56,768]{1,0:T(8,128)(2,1)S(1)}, u32[]{:S(2)}, u32[]{:S(2)}) collective-permute-start(bf16[56,768]{1,0:T(8,128)(2,1)S(1)} %get-tuple-element.17.refs_0_), channel_id=1, source_target_pairs={{0,4},{1,5},{4,8},{5,9},{8,12},{9,13},{12,14},{13,15},{14,10},{15,... | collective-permute-start | bytes 258056 | tf_op jit(solution)/shard_map/ppermute | solution.py:174
  36.2 2.5 %collective-permute-done.16.refs_1_ = bf16[56,768]{1,0:T(8,128)(2,1)S(1)} collective-permute-done((bf16[56,768]{1,0:T(8,128)(2,1)S(1)}, bf16[56,768]{1,0:T(8,128)(2,1)S(1)}, u32[]{:S(2)}, u32[]{:S(2)}) %collective-permute-start.16) | collective-permute-done | bytes 86048 | tf_op jit(solution)/shard_map/ppermute | solution.py:167
  38.6 1.2 %collective-permute-start.20 = (bf16[56,768]{1,0:T(8,128)(2,1)S(1)}, bf16[56,768]{1,0:T(8,128)(2,1)S(1)}, u32[]{:S(2)}, u32[]{:S(2)}) collective-permute-start(bf16[56,768]{1,0:T(8,128)(2,1)S(1)} %collective-permute-done.16.refs_1_), channel_id=1, source_target_pairs={{4,0},{5,1},{8,4},{9,5},{12,8},{13,9},{14,12},{15,13},{10,14},{11,... | collective-permute-start | bytes 258056 | tf_op jit(solution)/shard_map/ppermute | solution.py:177
  39.8 1.6 %collective-permute-start.19 = (bf16[56,768]{1,0:T(8,128)(2,1)S(1)}, bf16[56,768]{1,0:T(8,128)(2,1)S(1)}, u32[]{:S(2)}, u32[]{:S(2)}) collective-permute-start(bf16[56,768]{1,0:T(8,128)(2,1)S(1)} %get-tuple-element.17.refs_0_), channel_id=1, source_target_pairs={{4,0},{5,1},{8,4},{9,5},{12,8},{13,9},{14,12},{15,13},{10,14},{11,... | collective-permute-start | bytes 258056 | tf_op jit(solution)/shard_map/ppermute | solution.py:177
  42.7 1.3 %collective-permute-done.20.refs_5_ = bf16[56,768]{1,0:T(8,128)(2,1)S(1)} collective-permute-done((bf16[56,768]{1,0:T(8,128)(2,1)S(1)}, bf16[56,768]{1,0:T(8,128)(2,1)S(1)}, u32[]{:S(2)}, u32[]{:S(2)}) %collective-permute-start.20) | collective-permute-done | bytes 86048 | tf_op jit(solution)/shard_map/ppermute | solution.py:177
  44.0 1.0 %collective-permute-start.24 = (bf16[56,768]{1,0:T(8,128)(2,1)S(1)}, bf16[56,768]{1,0:T(8,128)(2,1)S(1)}, u32[]{:S(2)}, u32[]{:S(2)}) collective-permute-start(bf16[56,768]{1,0:T(8,128)(2,1)S(1)} %collective-permute-done.20.refs_5_), channel_id=1, source_target_pairs={{4,0},{5,1},{8,4},{9,5},{12,8},{13,9},{14,12},{15,13},{10,14},{11,... | collective-permute-start | bytes 258056 | tf_op jit(solution)/shard_map/ppermute | solution.py:177
  45.1 1.6 %collective-permute-start.23 = (bf16[56,768]{1,0:T(8,128)(2,1)S(1)}, bf16[56,768]{1,0:T(8,128)(2,1)S(1)}, u32[]{:S(2)}, u32[]{:S(2)}) collective-permute-start(bf16[56,768]{1,0:T(8,128)(2,1)S(1)} %collective-permute-done.19.refs_4_), channel_id=1, source_target_pairs={{4,0},{5,1},{8,4},{9,5},{12,8},{13,9},{14,12},{15,13},{10,14},{11,... | collective-permute-start | bytes 258056 | tf_op jit(solution)/shard_map/ppermute | solution.py:177
  47.3 1.4 %collective-permute-start.25 = (bf16[56,768]{1,0:T(8,128)(2,1)S(1)}, bf16[56,768]{1,0:T(8,128)(2,1)S(1)}, u32[]{:S(2)}, u32[]{:S(2)}) collective-permute-start(bf16[56,768]{1,0:T(8,128)(2,1)S(1)} %collective-permute-done.21.refs_6_), channel_id=1, source_target_pairs={{0,4},{1,5},{4,8},{5,9},{8,12},{9,13},{12,14},{13,15},{14,10},{15,... | collective-permute-start | bytes 258056 | tf_op jit(solution)/shard_map/ppermute | solution.py:174
  48.8 1.4 %collective-permute-start.28 = (bf16[56,768]{1,0:T(8,128)(2,1)S(1)}, bf16[56,768]{1,0:T(8,128)(2,1)S(1)}, u32[]{:S(2)}, u32[]{:S(2)}) collective-permute-start(bf16[56,768]{1,0:T(8,128)(2,1)S(1)} %collective-permute-done.24.refs_9_), channel_id=1, source_target_pairs={{4,0},{5,1},{8,4},{9,5},{12,8},{13,9},{14,12},{15,13},{10,14},{11,... | collective-permute-start | bytes 258056 | tf_op jit(solution)/shard_map/ppermute | solution.py:177
  50.2 1.7 %collective-permute-start.27 = (bf16[56,768]{1,0:T(8,128)(2,1)S(1)}, bf16[56,768]{1,0:T(8,128)(2,1)S(1)}, u32[]{:S(2)}, u32[]{:S(2)}) collective-permute-start(bf16[56,768]{1,0:T(8,128)(2,1)S(1)} %collective-permute-done.23.refs_8_), channel_id=1, source_target_pairs={{4,0},{5,1},{8,4},{9,5},{12,8},{13,9},{14,12},{15,13},{10,14},{11,... | collective-permute-start | bytes 258056 | tf_op jit(solution)/shard_map/ppermute | solution.py:177
  52.2 1.5 %collective-permute-start.29 = (bf16[56,768]{1,0:T(8,128)(2,1)S(1)}, bf16[56,768]{1,0:T(8,128)(2,1)S(1)}, u32[]{:S(2)}, u32[]{:S(2)}) collective-permute-start(bf16[56,768]{1,0:T(8,128)(2,1)S(1)} %collective-permute-done.25.refs_10_), channel_id=1, source_target_pairs={{0,4},{1,5},{4,8},{5,9},{8,12},{9,13},{12,14},{13,15},{14,10},{15,... | collective-permute-start | bytes 258056 | tf_op jit(solution)/shard_map/ppermute | solution.py:174
  58.2 2.2 %place_r.1.own_panel = bf16[896,768]{1,0:T(8,128)(2,1)S(1)} custom-call(bf16[56,768]{1,0:T(8,128)(2,1)S(1)} %get-tuple-element.17.refs_0_, bf16[56,768]{1,0:T(8,128)(2,1)S(1)} %collective-permute-done.16.refs_1_, bf16[56,768]{1,0:T(8,128)(2,1)S(1)} %collective-permute-done.17.refs_2_, bf16[56,768]{1,0:T(8,128)(2,1)S(1)} %collective-permute-done.18.refs_3_, ...), custom_call_target="tpu_custom_call" | custom-call | bytes 2752512 | tf_op jit(solution)/shard_map/place_r/pallas_call | solution.py:89
  60.5 3.4 %lower_own.1 = (bf16[1024,1536]{1,0:T(8,128)(2,1)}, bf16[1024,768]{1,0:T(8,128)(2,1)S(1)}) custom-call(bf16[1024,1536]{1,0:T(8,128)(2,1)S(1)} %copy-done.2, bf16[1536,768]{1,0:T(8,128)(2,1)S(1)} %place_p.1.refs_1_), custom_call_target="tpu_custom_call" | custom-call | flops 2415919104 | bytes 7077888 | tf_op jit(solution)/shard_map/lower_own/pallas_call | solution.py:122
  63.9 3.4 %lower_other.1 = (bf16[1024,1536]{1,0:T(8,128)(2,1)}, bf16[1024,768]{1,0:T(8,128)(2,1)S(1)}) custom-call(bf16[1024,1536]{1,0:T(8,128)(2,1)S(1)} %copy-done.2, bf16[1536,768]{1,0:T(8,128)(2,1)S(1)} %collective-permute-done.15.refs_1_, bf16[1024,1536]{1,0:T(8,128)(2,1)} %get-tuple-element.13.refs_2_), custom_call_target="tpu_custom_call", output_to_operand_aliasing={{0}: (2, {})} | custom-call | flops 2415919104 | bytes 7077888 | tf_op jit(solution)/shard_map/lower_other/pallas_call | solution.py:122
  67.3 4.2 %schur.1 = bf16[1024,896]{1,0:T(8,128)(2,1)} custom-call(bf16[1024,768]{1,0:T(8,128)(2,1)S(1)} %get-tuple-element.15.own_lower, bf16[896,768]{1,0:T(8,128)(2,1)S(1)} %place_r.1.own_panel, bf16[1024,768]{1,0:T(8,128)(2,1)S(1)} %get-tuple-element.19.other_lower, bf16[896,768]{1,0:T(8,128)(2,1)S(1)} %collective-permute-done.31.other_panel, ...), custom_call_target="tpu_custom_call" | custom-call | flops 2818572288 | bytes 9568256 | tf_op jit(solution)/shard_map/schur/pallas_call | solution.py:153
  (47 shorter events, 12.1 us)
Async XLA Ops:
  1.6 3.2 %collective-permute-start = (bf16[96,768]{1,0:T(8,128)(2,1)S(1)}, bf16[96,768]{1,0:T(8,128)(2,1)S(1)}, u32[]{:S(2)}, u32[]{:S(2)}) collective-permute-start(bf16[96,768]{1,0:T(8,128)(2,1)S(1)} %get-tuple-element.12), channel_id=1, source_target_pairs={{0,1},{1,0},{2,3},{3,2},{4,5},{5,4},{6,7},{7,6},{8,9},{9,8},{10,11... | collective-permute-start | bytes 442376 | tf_op jit(solution)/shard_map/ppermute | solution.py:167
  2.1 7.0 %collective-permute-start.1 = (bf16[96,768]{1,0:T(8,128)(2,1)S(1)}, bf16[96,768]{1,0:T(8,128)(2,1)S(1)}, u32[]{:S(2)}, u32[]{:S(2)}) collective-permute-start(bf16[96,768]{1,0:T(8,128)(2,1)S(1)} %get-tuple-element.11.refs_0_), channel_id=1, source_target_pairs={{0,4},{1,5},{4,8},{5,9},{8,12},{9,13},{12,14},{13,15},{14,10},{15,... | collective-permute-start | bytes 442376 | tf_op jit(solution)/shard_map/ppermute | solution.py:174
  4.8 6.7 %collective-permute-start.4 = (bf16[96,768]{1,0:T(8,128)(2,1)S(1)}, bf16[96,768]{1,0:T(8,128)(2,1)S(1)}, u32[]{:S(2)}, u32[]{:S(2)}) collective-permute-start(bf16[96,768]{1,0:T(8,128)(2,1)S(1)} %collective-permute-done.refs_1_), channel_id=1, source_target_pairs={{4,0},{5,1},{8,4},{9,5},{12,8},{13,9},{14,12},{15,13},{10,14},{11,... | collective-permute-start | bytes 442376 | tf_op jit(solution)/shard_map/ppermute | solution.py:177
  6.0 8.6 %collective-permute-start.3 = (bf16[96,768]{1,0:T(8,128)(2,1)S(1)}, bf16[96,768]{1,0:T(8,128)(2,1)S(1)}, u32[]{:S(2)}, u32[]{:S(2)}) collective-permute-start(bf16[96,768]{1,0:T(8,128)(2,1)S(1)} %get-tuple-element.11.refs_0_), channel_id=1, source_target_pairs={{4,0},{5,1},{8,4},{9,5},{12,8},{13,9},{14,12},{15,13},{10,14},{11,... | collective-permute-start | bytes 442376 | tf_op jit(solution)/shard_map/ppermute | solution.py:177
  7.6 8.3 %collective-permute-start.2 = (bf16[96,768]{1,0:T(8,128)(2,1)S(1)}, bf16[96,768]{1,0:T(8,128)(2,1)S(1)}, u32[]{:S(2)}, u32[]{:S(2)}) collective-permute-start(bf16[96,768]{1,0:T(8,128)(2,1)S(1)} %collective-permute-done.refs_1_), channel_id=1, source_target_pairs={{0,4},{1,5},{4,8},{5,9},{8,12},{9,13},{12,14},{13,15},{14,10},{15,... | collective-permute-start | bytes 442376 | tf_op jit(solution)/shard_map/ppermute | solution.py:174
  9.2 7.5 %collective-permute-start.5 = (bf16[96,768]{1,0:T(8,128)(2,1)S(1)}, bf16[96,768]{1,0:T(8,128)(2,1)S(1)}, u32[]{:S(2)}, u32[]{:S(2)}) collective-permute-start(bf16[96,768]{1,0:T(8,128)(2,1)S(1)} %collective-permute-done.1.refs_2_), channel_id=1, source_target_pairs={{0,4},{1,5},{4,8},{5,9},{8,12},{9,13},{12,14},{13,15},{14,10},{15,... | collective-permute-start | bytes 442376 | tf_op jit(solution)/shard_map/ppermute | solution.py:174
  11.5 6.8 %collective-permute-start.8 = (bf16[96,768]{1,0:T(8,128)(2,1)S(1)}, bf16[96,768]{1,0:T(8,128)(2,1)S(1)}, u32[]{:S(2)}, u32[]{:S(2)}) collective-permute-start(bf16[96,768]{1,0:T(8,128)(2,1)S(1)} %collective-permute-done.4.refs_5_), channel_id=1, source_target_pairs={{4,0},{5,1},{8,4},{9,5},{12,8},{13,9},{14,12},{15,13},{10,14},{11,... | collective-permute-start | bytes 442376 | tf_op jit(solution)/shard_map/ppermute | solution.py:177
  14.7 6.8 %collective-permute-start.7 = (bf16[96,768]{1,0:T(8,128)(2,1)S(1)}, bf16[96,768]{1,0:T(8,128)(2,1)S(1)}, u32[]{:S(2)}, u32[]{:S(2)}) collective-permute-start(bf16[96,768]{1,0:T(8,128)(2,1)S(1)} %collective-permute-done.3.refs_4_), channel_id=1, source_target_pairs={{4,0},{5,1},{8,4},{9,5},{12,8},{13,9},{14,12},{15,13},{10,14},{11,... | collective-permute-start | bytes 442376 | tf_op jit(solution)/shard_map/ppermute | solution.py:177
  15.9 6.8 %collective-permute-start.6 = (bf16[96,768]{1,0:T(8,128)(2,1)S(1)}, bf16[96,768]{1,0:T(8,128)(2,1)S(1)}, u32[]{:S(2)}, u32[]{:S(2)}) collective-permute-start(bf16[96,768]{1,0:T(8,128)(2,1)S(1)} %collective-permute-done.2.refs_3_), channel_id=1, source_target_pairs={{0,4},{1,5},{4,8},{5,9},{8,12},{9,13},{12,14},{13,15},{14,10},{15,... | collective-permute-start | bytes 442376 | tf_op jit(solution)/shard_map/ppermute | solution.py:174
  16.7 6.8 %collective-permute-start.9 = (bf16[96,768]{1,0:T(8,128)(2,1)S(1)}, bf16[96,768]{1,0:T(8,128)(2,1)S(1)}, u32[]{:S(2)}, u32[]{:S(2)}) collective-permute-start(bf16[96,768]{1,0:T(8,128)(2,1)S(1)} %collective-permute-done.5.refs_6_), channel_id=1, source_target_pairs={{0,4},{1,5},{4,8},{5,9},{8,12},{9,13},{12,14},{13,15},{14,10},{15,... | collective-permute-start | bytes 442376 | tf_op jit(solution)/shard_map/ppermute | solution.py:174
  18.3 6.8 %collective-permute-start.12 = (bf16[96,768]{1,0:T(8,128)(2,1)S(1)}, bf16[96,768]{1,0:T(8,128)(2,1)S(1)}, u32[]{:S(2)}, u32[]{:S(2)}) collective-permute-start(bf16[96,768]{1,0:T(8,128)(2,1)S(1)} %collective-permute-done.8.refs_9_), channel_id=1, source_target_pairs={{4,0},{5,1},{8,4},{9,5},{12,8},{13,9},{14,12},{15,13},{10,14},{11,... | collective-permute-start | bytes 442376 | tf_op jit(solution)/shard_map/ppermute | solution.py:177
  21.4 6.7 %collective-permute-start.11 = (bf16[96,768]{1,0:T(8,128)(2,1)S(1)}, bf16[96,768]{1,0:T(8,128)(2,1)S(1)}, u32[]{:S(2)}, u32[]{:S(2)}) collective-permute-start(bf16[96,768]{1,0:T(8,128)(2,1)S(1)} %collective-permute-done.7.refs_8_), channel_id=1, source_target_pairs={{4,0},{5,1},{8,4},{9,5},{12,8},{13,9},{14,12},{15,13},{10,14},{11,... | collective-permute-start | bytes 442376 | tf_op jit(solution)/shard_map/ppermute | solution.py:177
  22.7 5.4 %collective-permute-start.10 = (bf16[96,768]{1,0:T(8,128)(2,1)S(1)}, bf16[96,768]{1,0:T(8,128)(2,1)S(1)}, u32[]{:S(2)}, u32[]{:S(2)}) collective-permute-start(bf16[96,768]{1,0:T(8,128)(2,1)S(1)} %collective-permute-done.6.refs_7_), channel_id=1, source_target_pairs={{0,4},{1,5},{4,8},{5,9},{8,12},{9,13},{12,14},{13,15},{14,10},{15,... | collective-permute-start | bytes 442376 | tf_op jit(solution)/shard_map/ppermute | solution.py:174
  23.5 5.9 %collective-permute-start.13 = (bf16[96,768]{1,0:T(8,128)(2,1)S(1)}, bf16[96,768]{1,0:T(8,128)(2,1)S(1)}, u32[]{:S(2)}, u32[]{:S(2)}) collective-permute-start(bf16[96,768]{1,0:T(8,128)(2,1)S(1)} %collective-permute-done.9.refs_10_), channel_id=1, source_target_pairs={{0,4},{1,5},{4,8},{5,9},{8,12},{9,13},{12,14},{13,15},{14,10},{15,... | collective-permute-start | bytes 442376 | tf_op jit(solution)/shard_map/ppermute | solution.py:174
  25.1 5.1 %collective-permute-start.14 = (bf16[96,768]{1,0:T(8,128)(2,1)S(1)}, bf16[96,768]{1,0:T(8,128)(2,1)S(1)}, u32[]{:S(2)}, u32[]{:S(2)}) collective-permute-start(bf16[96,768]{1,0:T(8,128)(2,1)S(1)} %collective-permute-done.12.refs_13_), channel_id=1, source_target_pairs={{4,0},{5,1},{8,4},{9,5},{12,8},{13,9},{14,12},{15,13},{10,14},{11,... | collective-permute-start | bytes 442376 | tf_op jit(solution)/shard_map/ppermute | solution.py:177
  33.9 30.0 %collective-permute-start.15 = (bf16[1536,768]{1,0:T(8,128)(2,1)S(1)}, bf16[1536,768]{1,0:T(8,128)(2,1)S(1)}, u32[]{:S(2)}, u32[]{:S(2)}) collective-permute-start(bf16[1536,768]{1,0:T(8,128)(2,1)S(1)} %place_p.1.refs_1_), channel_id=1, source_target_pairs={{0,1},{1,0},{2,3},{3,2},{4,5},{5,4},{6,7},{7,6},{8,9},{9,8},{10,11... | collective-permute-start | bytes 7077896 | tf_op jit(solution)/shard_map/ppermute | solution.py:192
  34.0 4.6 %collective-permute-start.16 = (bf16[56,768]{1,0:T(8,128)(2,1)S(1)}, bf16[56,768]{1,0:T(8,128)(2,1)S(1)}, u32[]{:S(2)}, u32[]{:S(2)}) collective-permute-start(bf16[56,768]{1,0:T(8,128)(2,1)S(1)} %get-tuple-element.18), channel_id=1, source_target_pairs={{0,1},{1,0},{2,3},{3,2},{4,5},{5,4},{6,7},{7,6},{8,9},{9,8},{10,11... | collective-permute-start | bytes 258056 | tf_op jit(solution)/shard_map/ppermute | solution.py:167
  34.6 7.3 %collective-permute-start.17 = (bf16[56,768]{1,0:T(8,128)(2,1)S(1)}, bf16[56,768]{1,0:T(8,128)(2,1)S(1)}, u32[]{:S(2)}, u32[]{:S(2)}) collective-permute-start(bf16[56,768]{1,0:T(8,128)(2,1)S(1)} %get-tuple-element.17.refs_0_), channel_id=1, source_target_pairs={{0,4},{1,5},{4,8},{5,9},{8,12},{9,13},{12,14},{13,15},{14,10},{15,... | collective-permute-start | bytes 258056 | tf_op jit(solution)/shard_map/ppermute | solution.py:174
  38.6 5.4 %collective-permute-start.20 = (bf16[56,768]{1,0:T(8,128)(2,1)S(1)}, bf16[56,768]{1,0:T(8,128)(2,1)S(1)}, u32[]{:S(2)}, u32[]{:S(2)}) collective-permute-start(bf16[56,768]{1,0:T(8,128)(2,1)S(1)} %collective-permute-done.16.refs_1_), channel_id=1, source_target_pairs={{4,0},{5,1},{8,4},{9,5},{12,8},{13,9},{14,12},{15,13},{10,14},{11,... | collective-permute-start | bytes 258056 | tf_op jit(solution)/shard_map/ppermute | solution.py:177
  39.8 5.2 %collective-permute-start.19 = (bf16[56,768]{1,0:T(8,128)(2,1)S(1)}, bf16[56,768]{1,0:T(8,128)(2,1)S(1)}, u32[]{:S(2)}, u32[]{:S(2)}) collective-permute-start(bf16[56,768]{1,0:T(8,128)(2,1)S(1)} %get-tuple-element.17.refs_0_), channel_id=1, source_target_pairs={{4,0},{5,1},{8,4},{9,5},{12,8},{13,9},{14,12},{15,13},{10,14},{11,... | collective-permute-start | bytes 258056 | tf_op jit(solution)/shard_map/ppermute | solution.py:177
  41.4 5.2 %collective-permute-start.18 = (bf16[56,768]{1,0:T(8,128)(2,1)S(1)}, bf16[56,768]{1,0:T(8,128)(2,1)S(1)}, u32[]{:S(2)}, u32[]{:S(2)}) collective-permute-start(bf16[56,768]{1,0:T(8,128)(2,1)S(1)} %collective-permute-done.16.refs_1_), channel_id=1, source_target_pairs={{0,4},{1,5},{4,8},{5,9},{8,12},{9,13},{12,14},{13,15},{14,10},{15,... | collective-permute-start | bytes 258056 | tf_op jit(solution)/shard_map/ppermute | solution.py:174
  41.9 5.4 %collective-permute-start.21 = (bf16[56,768]{1,0:T(8,128)(2,1)S(1)}, bf16[56,768]{1,0:T(8,128)(2,1)S(1)}, u32[]{:S(2)}, u32[]{:S(2)}) collective-permute-start(bf16[56,768]{1,0:T(8,128)(2,1)S(1)} %collective-permute-done.17.refs_2_), channel_id=1, source_target_pairs={{0,4},{1,5},{4,8},{5,9},{8,12},{9,13},{12,14},{13,15},{14,10},{15,... | collective-permute-start | bytes 258056 | tf_op jit(solution)/shard_map/ppermute | solution.py:174
  44.0 4.8 %collective-permute-start.24 = (bf16[56,768]{1,0:T(8,128)(2,1)S(1)}, bf16[56,768]{1,0:T(8,128)(2,1)S(1)}, u32[]{:S(2)}, u32[]{:S(2)}) collective-permute-start(bf16[56,768]{1,0:T(8,128)(2,1)S(1)} %collective-permute-done.20.refs_5_), channel_id=1, source_target_pairs={{4,0},{5,1},{8,4},{9,5},{12,8},{13,9},{14,12},{15,13},{10,14},{11,... | collective-permute-start | bytes 258056 | tf_op jit(solution)/shard_map/ppermute | solution.py:177
  45.1 5.1 %collective-permute-start.23 = (bf16[56,768]{1,0:T(8,128)(2,1)S(1)}, bf16[56,768]{1,0:T(8,128)(2,1)S(1)}, u32[]{:S(2)}, u32[]{:S(2)}) collective-permute-start(bf16[56,768]{1,0:T(8,128)(2,1)S(1)} %collective-permute-done.19.refs_4_), channel_id=1, source_target_pairs={{4,0},{5,1},{8,4},{9,5},{12,8},{13,9},{14,12},{15,13},{10,14},{11,... | collective-permute-start | bytes 258056 | tf_op jit(solution)/shard_map/ppermute | solution.py:177
  46.6 5.2 %collective-permute-start.22 = (bf16[56,768]{1,0:T(8,128)(2,1)S(1)}, bf16[56,768]{1,0:T(8,128)(2,1)S(1)}, u32[]{:S(2)}, u32[]{:S(2)}) collective-permute-start(bf16[56,768]{1,0:T(8,128)(2,1)S(1)} %collective-permute-done.18.refs_3_), channel_id=1, source_target_pairs={{0,4},{1,5},{4,8},{5,9},{8,12},{9,13},{12,14},{13,15},{14,10},{15,... | collective-permute-start | bytes 258056 | tf_op jit(solution)/shard_map/ppermute | solution.py:174
  47.3 4.9 %collective-permute-start.25 = (bf16[56,768]{1,0:T(8,128)(2,1)S(1)}, bf16[56,768]{1,0:T(8,128)(2,1)S(1)}, u32[]{:S(2)}, u32[]{:S(2)}) collective-permute-start(bf16[56,768]{1,0:T(8,128)(2,1)S(1)} %collective-permute-done.21.refs_6_), channel_id=1, source_target_pairs={{0,4},{1,5},{4,8},{5,9},{8,12},{9,13},{12,14},{13,15},{14,10},{15,... | collective-permute-start | bytes 258056 | tf_op jit(solution)/shard_map/ppermute | solution.py:174
  48.8 4.9 %collective-permute-start.28 = (bf16[56,768]{1,0:T(8,128)(2,1)S(1)}, bf16[56,768]{1,0:T(8,128)(2,1)S(1)}, u32[]{:S(2)}, u32[]{:S(2)}) collective-permute-start(bf16[56,768]{1,0:T(8,128)(2,1)S(1)} %collective-permute-done.24.refs_9_), channel_id=1, source_target_pairs={{4,0},{5,1},{8,4},{9,5},{12,8},{13,9},{14,12},{15,13},{10,14},{11,... | collective-permute-start | bytes 258056 | tf_op jit(solution)/shard_map/ppermute | solution.py:177
  50.2 5.4 %collective-permute-start.27 = (bf16[56,768]{1,0:T(8,128)(2,1)S(1)}, bf16[56,768]{1,0:T(8,128)(2,1)S(1)}, u32[]{:S(2)}, u32[]{:S(2)}) collective-permute-start(bf16[56,768]{1,0:T(8,128)(2,1)S(1)} %collective-permute-done.23.refs_8_), channel_id=1, source_target_pairs={{4,0},{5,1},{8,4},{9,5},{12,8},{13,9},{14,12},{15,13},{10,14},{11,... | collective-permute-start | bytes 258056 | tf_op jit(solution)/shard_map/ppermute | solution.py:177
  51.9 4.5 %collective-permute-start.26 = (bf16[56,768]{1,0:T(8,128)(2,1)S(1)}, bf16[56,768]{1,0:T(8,128)(2,1)S(1)}, u32[]{:S(2)}, u32[]{:S(2)}) collective-permute-start(bf16[56,768]{1,0:T(8,128)(2,1)S(1)} %collective-permute-done.22.refs_7_), channel_id=1, source_target_pairs={{0,4},{1,5},{4,8},{5,9},{8,12},{9,13},{12,14},{13,15},{14,10},{15,... | collective-permute-start | bytes 258056 | tf_op jit(solution)/shard_map/ppermute | solution.py:174
  52.2 5.0 %collective-permute-start.29 = (bf16[56,768]{1,0:T(8,128)(2,1)S(1)}, bf16[56,768]{1,0:T(8,128)(2,1)S(1)}, u32[]{:S(2)}, u32[]{:S(2)}) collective-permute-start(bf16[56,768]{1,0:T(8,128)(2,1)S(1)} %collective-permute-done.25.refs_10_), channel_id=1, source_target_pairs={{0,4},{1,5},{4,8},{5,9},{8,12},{9,13},{12,14},{13,15},{14,10},{15,... | collective-permute-start | bytes 258056 | tf_op jit(solution)/shard_map/ppermute | solution.py:174
  53.7 4.5 %collective-permute-start.30 = (bf16[56,768]{1,0:T(8,128)(2,1)S(1)}, bf16[56,768]{1,0:T(8,128)(2,1)S(1)}, u32[]{:S(2)}, u32[]{:S(2)}) collective-permute-start(bf16[56,768]{1,0:T(8,128)(2,1)S(1)} %collective-permute-done.28.refs_13_), channel_id=1, source_target_pairs={{4,0},{5,1},{8,4},{9,5},{12,8},{13,9},{14,12},{15,13},{10,14},{11,... | collective-permute-start | bytes 258056 | tf_op jit(solution)/shard_map/ppermute | solution.py:177
  60.4 6.9 %collective-permute-start.31 = (bf16[896,768]{1,0:T(8,128)(2,1)S(1)}, bf16[896,768]{1,0:T(8,128)(2,1)S(1)}, u32[]{:S(2)}, u32[]{:S(2)}) collective-permute-start(bf16[896,768]{1,0:T(8,128)(2,1)S(1)} %place_r.1.own_panel), channel_id=1, source_target_pairs={{0,1},{1,0},{2,3},{3,2},{4,5},{5,4},{6,7},{7,6},{8,9},{9,8},{10,11... | collective-permute-start | bytes 4128776 | tf_op jit(solution)/shard_map/ppermute | solution.py:193
  (4 other events, 66.5 us)

commit v2 on v0

v2 whole, which is shorter than its diff:
```python
import functools

import jax
import jax.numpy as jnp
from jax import lax
from jax.experimental import pallas as pl
from jax.experimental.pallas import tpu as pltpu
from jax.sharding import PartitionSpec as P

F32, BF16 = jnp.float32, jnp.bfloat16
ON_CHIP = pl.BlockSpec(memory_space=pltpu.VMEM)
IN_HBM = pl.BlockSpec(memory_space=pltpu.HBM)
PARAMS = pltpu.CompilerParams(vmem_limit_bytes=16 << 20)
CHUNKS = 4
WEIGHT = 20


def shape(*dims):
    return jax.ShapeDtypeStruct(dims, BF16)


def cost(flops, nbytes):
    return pl.CostEstimate(flops=flops, bytes_accessed=nbytes, transcendentals=0)


def small(kernel, out_shape, operands, name):
    return pl.pallas_call(
        kernel,
        out_shape=out_shape,
        in_specs=[ON_CHIP] * len(operands),
        out_specs=jax.tree.map(lambda _: ON_CHIP, out_shape),
        compiler_params=PARAMS,
        name=name,
    )(*operands)


def in_hbm(x):
    return pltpu.with_memory_space_constraint(x, pltpu.HBM)


def after(value, *others):
    return lax.optimization_barrier((value, *others))[0]


def ring_of(chips):
    if chips > 8:
        return list(range(chips))
    return list(range(0, chips, 2)) + list(range(chips - 1, 0, -2))


def chip_at(distance, chips):
    chip = lax.axis_index("row") // 2
    if chips > 8:
        return lax.rem(chip + distance + chips, chips)
    place = jnp.where(lax.rem(chip, 2) == 0, chip // 2, chips - 1 - chip // 2)
    place = lax.rem(place + distance + chips, chips)
    return jnp.where(place < chips // 2, 2 * place, 2 * (chips - 1 - place) + 1)


def my_core():
    return lax.rem(lax.axis_index("row"), 2)


def split_kernel(inverse, panel, mine, theirs, sems):
    rows, half = inverse.shape[0], mine.shape[1]
    copies = []
    for i, (ref, at) in enumerate(((inverse, pl.ds(0, rows)), (panel, pl.ds(rows, panel.shape[0])))):
        for j, (out, core) in enumerate(((mine, my_core()), (theirs, 1 - my_core()))):
            cols = pl.ds(pl.multiple_of(core * half, 128), half)
            copies.append(pltpu.make_async_copy(ref.at[:, cols], out.at[at], sems.at[2 * j + i]))
            copies[-1].start()
    for copy in copies:
        copy.wait()


def split(inverse, panel):
    out = shape(inverse.shape[0] + panel.shape[0], inverse.shape[1] // 2)
    return pl.pallas_call(
        split_kernel,
        out_shape=(out, out),
        in_specs=[IN_HBM, IN_HBM],
        out_specs=(ON_CHIP, ON_CHIP),
        scratch_shapes=[pltpu.SemaphoreType.DMA((4,))],
        compiler_params=PARAMS,
        name="split",
    )(in_hbm(inverse), in_hbm(panel))


def fetch_kernel(*refs):
    count = len(refs) // 2
    copies = [pltpu.make_async_copy(refs[i], refs[count + i], refs[-1].at[i]) for i in range(count)]
    for copy in copies:
        copy.start()
    for copy in copies:
        copy.wait()


def fetch(*arrays):
    return pl.pallas_call(
        fetch_kernel,
        out_shape=tuple(shape(*x.shape) for x in arrays),
        in_specs=[IN_HBM] * len(arrays),
        out_specs=(ON_CHIP,) * len(arrays),
        scratch_shapes=[pltpu.SemaphoreType.DMA((len(arrays),))],
        compiler_params=PARAMS,
        name="fetch",
    )(*map(in_hbm, arrays))


def stack(parts, name):
    def kernel(*refs):
        to = 0
        for ref, (_, start, rows) in zip(refs, parts):
            refs[-1][to : to + rows] = ref[start : start + rows]
            to += rows

    rows, cols = sum(part[2] for part in parts), parts[0][0].shape[1]
    return small(kernel, shape(rows, cols), [part[0] for part in parts], name)


def place(parts, rows, chips, flip, name):
    def kernel(*refs):
        for ref, (_, start, distance, stream) in zip(refs, parts):
            core = my_core() if stream == flip else 1 - my_core()
            at = pl.multiple_of((2 * chip_at(distance, chips) + core) * rows, 8)
            refs[-1][pl.ds(at, rows), :] = ref[start : start + rows]

    cols = parts[0][0].shape[1]
    return small(kernel, shape(2 * chips * rows, cols), [part[0] for part in parts], name)


def lower_kernel(column, panel, *refs):
    if len(refs) > 1:
        kept, out, lower_out, sem = refs
        half = kept.shape[1]
        cols = pl.ds(pl.multiple_of(my_core() * half, 128), half)
        copy = pltpu.make_async_copy(kept, lower_out.at[:, cols], sem)
        copy.start()
    else:
        out, copy = refs[0], None
    rows = column.shape[0] // CHUNKS
    for i in range(CHUNKS):
        at = pl.ds(i * rows, rows)
        out[at] = jnp.dot(column[at], panel[...], preferred_element_type=F32).astype(BF16)
    if copy:
        copy.wait()


def lower(column_block, panel, kept=None):
    n, k = column_block.shape
    half = panel.shape[1]
    first = kept is None
    return pl.pallas_call(
        lower_kernel,
        out_shape=(shape(n, half),) + (() if first else (shape(n, 2 * half),)),
        in_specs=[ON_CHIP] * (2 if first else 3),
        out_specs=(ON_CHIP,) + (() if first else (IN_HBM,)),
        scratch_shapes=[] if first else [pltpu.SemaphoreType.DMA],
        compiler_params=PARAMS,
        cost_estimate=cost(WEIGHT * 2 * n * k * half, 2 * (n * k + k * half + n * half)),
        name="lower_own" if first else "lower_other",
    )(column_block, panel, *(() if first else (kept,)))


def schur_kernel(own_lower, own_panel, other_lower, other_panel, coupling, _, lower_out, out, done, out_sems, lower_sem):
    half = own_lower.shape[1]
    cols = pl.ds(pl.multiple_of((1 - my_core()) * half, 128), half)
    copies = [pltpu.make_async_copy(other_lower, lower_out.at[:, cols], lower_sem)]
    copies[-1].start()
    contract = (((1,), (1,)), ((), ()))
    start = 0
    for i, rows in enumerate(schur_chunks(coupling.shape[0])):
        at = pl.ds(start, rows)
        product = lax.dot_general(own_lower[at], own_panel[...], contract, preferred_element_type=F32)
        product += lax.dot_general(other_lower[at], other_panel[...], contract, preferred_element_type=F32)
        done[at] = (coupling[at].astype(F32) - product).astype(BF16)
        copies.append(pltpu.make_async_copy(done.at[at], out.at[at], out_sems.at[i]))
        copies[-1].start()
        start += rows
    for copy in copies:
        copy.wait()


def schur_chunks(rows):
    quarter = rows // 4
    return [quarter, quarter, quarter, quarter // 2, quarter // 2]


def schur(own_lower, own_panel, other_lower, other_panel, coupling, so_far):
    n, cols = coupling.shape
    k = 2 * own_lower.shape[1]
    return pl.pallas_call(
        schur_kernel,
        out_shape=(shape(n, k), shape(n, cols)),
        in_specs=[ON_CHIP] * 5 + [IN_HBM],
        out_specs=(IN_HBM, IN_HBM),
        scratch_shapes=[
            pltpu.VMEM((n, cols), BF16),
            pltpu.SemaphoreType.DMA((len(schur_chunks(n)),)),
            pltpu.SemaphoreType.DMA,
        ],
        input_output_aliases={5: 0},
        compiler_params=PARAMS,
        cost_estimate=cost(2 * n * k * cols, 2 * (n * k + k * cols + 2 * n * cols)),
        name="schur",
    )(own_lower, own_panel, other_lower, other_panel, coupling, so_far)


def on_device(devices, coupling, column_block, pivot_inverse, row_panel):
    chips = devices // 2
    steps = chips // 2
    ring = ring_of(chips)
    over = [(i, i ^ 1) for i in range(devices)]
    up = [(2 * ring[i] + c, 2 * ring[(i + 1) % chips] + c) for i in range(chips) for c in range(2)]
    down = [(to, at) for at, to in up]
    send = lambda x, to: lax.ppermute(x, "row", to)
    p_rows, r_rows = pivot_inverse.shape[0], row_panel.shape[1]

    mine, theirs = split(pivot_inverse, row_panel.T)
    rising = [mine, send(theirs, over)]
    falling = list(rising)
    pieces = [(rising[s], 0, s) for s in range(2)]
    for k in range(1, steps):
        for s in range(2):
            rising[s], falling[s] = send(rising[s], up), send(falling[s], down)
            pieces += [(rising[s], -k, s), (falling[s], k, s)]
        if k == 1:
            column_block, coupling = fetch(after(column_block, rising[0]), coupling)
    last = [send(rising[0], up), send(falling[1], down)]
    rows = p_rows + r_rows
    early = send(stack([(x, 0, rows) for x, _, _ in pieces], "early"), over)
    late = send(stack([(x, 0, rows) for x in last], "late"), over)
    own = [(x, 0, d, s) for x, d, s in pieces] + [(last[s], 0, steps, s) for s in range(2)]
    other = [(early, i * rows, d, s) for i, (_, d, s) in enumerate(pieces)]
    other += [(late, s * rows, steps, s) for s in range(2)]
    below = lambda parts: [(x, start + p_rows, d, s) for x, start, d, s in parts]

    own_p = place(own, p_rows, chips, 0, "place_own_p")
    (own_lower,) = lower(column_block, own_p)
    other_p = place(other, p_rows, chips, 1, "place_other_p")
    other_lower, lower_panel = lower(column_block, other_p, own_lower)
    own_r = place(below(own), r_rows, chips, 0, "place_own_r")
    other_r = place(below(other), r_rows, chips, 1, "place_other_r")
    return schur(own_lower, own_r, other_lower, other_r, coupling, lower_panel)


def by_all_gather(coupling, column_block, pivot_inverse, row_panel):
    whole_inverse = lax.all_gather(pivot_inverse, "row", axis=0, tiled=True)
    whole_panel = lax.all_gather(row_panel, "row", axis=1, tiled=True)
    lower_panel = jnp.dot(column_block, whole_inverse, preferred_element_type=F32).astype(BF16)
    product = jnp.dot(lower_panel, whole_panel, preferred_element_type=F32)
    return lower_panel, (coupling.astype(F32) - product).astype(BF16)


def solution(mesh):
    devices = mesh.shape["row"]
    parts = mesh.shape["groups"]

    def step(coupling, column_block, pivot_inverse, row_panel):
        fits = devices % 4 == 0 and devices >= 8
        fits &= row_panel.shape[1] // (parts * devices) % 8 == 0
        fits &= pivot_inverse.shape[0] // (parts * devices) % 8 == 0
        body = functools.partial(on_device, devices) if fits else by_all_gather
        rows = P(("groups", "row"), None)
        return jax.shard_map(
            body,
            mesh=mesh,
            in_specs=(rows, rows, rows, P(None, ("groups", "row"))),
            out_specs=(rows, rows),
            check_vma=False,
        )(coupling, column_block, pivot_inverse, row_panel)

    return step
```

time: 126 us -> 55.2 us (0.44)
  waiting for transfers between devices: 95 us -> 17.7 us
  starting transfers between devices: 0.08 us -> 20.6 us
  matrix products: 16.6 us -> 0 us
  Pallas kernels: 0 us -> 16 us
  between operations: 14 us -> 0.75 us
    all_gather x2 -> x0, waiting for transfers between devices: 93.7 us -> none  [the longest x1 57.8 us: on_device(): whole_inverse = lax.all_gather(pivot_inverse, 'row', axis=0, tiled=True)]
    ppermute x0 -> x17, starting transfers between devices: none -> 20.6 us  [on_device(): send = lambda x, to: lax.ppermute(x, 'row', to)]
    ppermute x0 -> x17, waiting for transfers between devices: none -> 17.7 us  [on_device(): send = lambda x, to: lax.ppermute(x, 'row', to)]
    dot_general x2 -> x0, matrix products: 16.6 us -> none  [the longest x1 8.69 us: on_device(): jnp.dot(column_block, whole_inverse, preferred_element_type=jnp.float32)]
    pallas_call x0 -> x11, Pallas kernels: none -> 16 us  [the longest x2 6.14 us: lower(): pl.pallas_call(lower_kernel, out_shape=(shape(n, half),) + (() if first e...]
    unnamed x2 -> x0, waiting for transfers between devices: 1.38 us -> none
  transfers between devices with their start and end apart: 2 -> 17, of which waited for: 2 -> 8; matrix products, arithmetic and copies ran while one was open for 7% -> 0% of each run, Pallas kernels for 0% -> 10%
where the time goes in v2:
time: 55.2 us; the launch traced here: 55.1 us
  starting transfers between devices  20.6 us (37%)
  waiting for transfers between devices  17.7 us (32%)
  Pallas kernels  16 us (29%)
  between operations  0.75 us (1%)
    ppermute x17, starting transfers between devices, on_device(): send = lambda x, to: lax.ppermute(x, 'row', to)  20.6 us
    ppermute x17, waiting for transfers between devices, on_device(): send = lambda x, to: lax.ppermute(x, 'row', to)  17.7 us
    pallas_call x2, Pallas kernels, lower(): pl.pallas_call(lower_kernel, out_shape=(shape(n, half),) + (() if first e...  6.14 us
    pallas_call x1, Pallas kernels, schur(): pl.pallas_call(schur_kernel, out_shape=(shape(n, k), shape(n, cols)), in_...  5.38 us
    pallas_call x1, Pallas kernels, fetch(): pl.pallas_call(fetch_kernel, out_shape=tuple((shape(*x.shape) for x in ar...  2.46 us
    pallas_call x1, Pallas kernels, split(): pl.pallas_call(split_kernel, out_shape=(out, out), in_specs=[IN_HBM, IN_H...  1.12 us
  transfers between devices with their start and end apart: 17, of which 8 were waited for; matrix products, arithmetic and copies ran while one was open for 0% of the time, Pallas kernels for 10%

profile of v2, /device:TPU:0, one launch (start us, length us, event | category | flops | bytes accessed | tf_op | source)
XLA Modules:
  0.0 55.1 jit_solution(5748967749966812471)
XLA Ops:
  0.6 1.1 %split.1 = (bf16[152,768]{1,0:T(8,128)(2,1)S(1)}, bf16[152,768]{1,0:T(8,128)(2,1)S(1)}) custom-call(bf16[96,1536]{1,0:T(8,128)(2,1)} %inverse.1, bf16[56,1536]{1,0:T(8,128)(2,1)} %bitcast.1), custom_call_target="tpu_custom_call" | custom-call | tf_op jit(solution)/shard_map/split/pallas_call | solution.py:78
  1.8 0.5 collective-permute-start.1
  2.3 2.6 %collective-permute-start = (bf16[152,768]{1,0:T(8,128)(2,1)S(1)}, bf16[152,768]{1,0:T(8,128)(2,1)S(1)}, u32[]{:S(2)}, u32[]{:S(2)}) collective-permute-start(bf16[152,768]{1,0:T(8,128)(2,1)S(1)} %get-tuple-element.9.refs_0_), channel_id=1, source_target_pairs={{0,4},{1,5},{4,8},{5,9},{8,12},{9,13},{12,14},{13,15},{14,10},{15,... | collective-permute-start | bytes 700424 | tf_op jit(solution)/shard_map/ppermute | solution.py:216
  4.9 1.4 %collective-permute-start.4 = (bf16[152,768]{1,0:T(8,128)(2,1)S(1)}, bf16[152,768]{1,0:T(8,128)(2,1)S(1)}, u32[]{:S(2)}, u32[]{:S(2)}) collective-permute-start(bf16[152,768]{1,0:T(8,128)(2,1)S(1)} %collective-permute-done.1.refs_1_), channel_id=1, source_target_pairs={{4,0},{5,1},{8,4},{9,5},{12,8},{13,9},{14,12},{15,13},{10,14},{11,... | collective-permute-start | bytes 700424 | tf_op jit(solution)/shard_map/ppermute | solution.py:216
  6.3 1.6 %collective-permute-start.2 = (bf16[152,768]{1,0:T(8,128)(2,1)S(1)}, bf16[152,768]{1,0:T(8,128)(2,1)S(1)}, u32[]{:S(2)}, u32[]{:S(2)}) collective-permute-start(bf16[152,768]{1,0:T(8,128)(2,1)S(1)} %get-tuple-element.9.refs_0_), channel_id=1, source_target_pairs={{4,0},{5,1},{8,4},{9,5},{12,8},{13,9},{14,12},{15,13},{10,14},{11,... | collective-permute-start | bytes 700424 | tf_op jit(solution)/shard_map/ppermute | solution.py:216
  7.9 0.4 collective-permute-start.3
  8.3 3.1 %collective-permute-done.refs_2_ = bf16[152,768]{1,0:T(8,128)(2,1)S(1)} collective-permute-done((bf16[152,768]{1,0:T(8,128)(2,1)S(1)}, bf16[152,768]{1,0:T(8,128)(2,1)S(1)}, u32[]{:S(2)}, u32[]{:S(2)}) %collective-permute-start) | collective-permute-done | bytes 233504 | tf_op jit(solution)/shard_map/ppermute | solution.py:216
  11.4 2.0 %collective-permute-start.5 = (bf16[152,768]{1,0:T(8,128)(2,1)S(1)}, bf16[152,768]{1,0:T(8,128)(2,1)S(1)}, u32[]{:S(2)}, u32[]{:S(2)}) collective-permute-start(bf16[152,768]{1,0:T(8,128)(2,1)S(1)} %collective-permute-done.refs_2_), channel_id=1, source_target_pairs={{0,4},{1,5},{4,8},{5,9},{8,12},{9,13},{12,14},{13,15},{14,10},{15,... | collective-permute-start | bytes 700424 | tf_op jit(solution)/shard_map/ppermute | solution.py:216
  13.5 1.4 %collective-permute-start.8 = (bf16[152,768]{1,0:T(8,128)(2,1)S(1)}, bf16[152,768]{1,0:T(8,128)(2,1)S(1)}, u32[]{:S(2)}, u32[]{:S(2)}) collective-permute-start(bf16[152,768]{1,0:T(8,128)(2,1)S(1)} %collective-permute-done.4.refs_5_), channel_id=1, source_target_pairs={{4,0},{5,1},{8,4},{9,5},{12,8},{13,9},{14,12},{15,13},{10,14},{11,... | collective-permute-start | bytes 700424 | tf_op jit(solution)/shard_map/ppermute | solution.py:216
  14.8 3.6 %collective-permute-done.2.refs_3_ = bf16[152,768]{1,0:T(8,128)(2,1)S(1)} collective-permute-done((bf16[152,768]{1,0:T(8,128)(2,1)S(1)}, bf16[152,768]{1,0:T(8,128)(2,1)S(1)}, u32[]{:S(2)}, u32[]{:S(2)}) %collective-permute-start.2) | collective-permute-done | bytes 233504 | tf_op jit(solution)/shard_map/ppermute | solution.py:216
  18.5 1.4 %collective-permute-start.6 = (bf16[152,768]{1,0:T(8,128)(2,1)S(1)}, bf16[152,768]{1,0:T(8,128)(2,1)S(1)}, u32[]{:S(2)}, u32[]{:S(2)}) collective-permute-start(bf16[152,768]{1,0:T(8,128)(2,1)S(1)} %collective-permute-done.2.refs_3_), channel_id=1, source_target_pairs={{4,0},{5,1},{8,4},{9,5},{12,8},{13,9},{14,12},{15,13},{10,14},{11,... | collective-permute-start | bytes 700424 | tf_op jit(solution)/shard_map/ppermute | solution.py:216
  19.8 0.7 %collective-permute-start.7 = (bf16[152,768]{1,0:T(8,128)(2,1)S(1)}, bf16[152,768]{1,0:T(8,128)(2,1)S(1)}, u32[]{:S(2)}, u32[]{:S(2)}) collective-permute-start(bf16[152,768]{1,0:T(8,128)(2,1)S(1)} %collective-permute-done.3.refs_4_), channel_id=1, source_target_pairs={{0,4},{1,5},{4,8},{5,9},{8,12},{9,13},{12,14},{13,15},{14,10},{15,... | collective-permute-start | bytes 700424 | tf_op jit(solution)/shard_map/ppermute | solution.py:216
  20.5 1.0 %collective-permute-done.5.refs_6_ = bf16[152,768]{1,0:T(8,128)(2,1)S(1)} collective-permute-done((bf16[152,768]{1,0:T(8,128)(2,1)S(1)}, bf16[152,768]{1,0:T(8,128)(2,1)S(1)}, u32[]{:S(2)}, u32[]{:S(2)}) %collective-permute-start.5) | collective-permute-done | bytes 233504 | tf_op jit(solution)/shard_map/ppermute | solution.py:216
  21.5 1.9 %collective-permute-start.9 = (bf16[152,768]{1,0:T(8,128)(2,1)S(1)}, bf16[152,768]{1,0:T(8,128)(2,1)S(1)}, u32[]{:S(2)}, u32[]{:S(2)}) collective-permute-start(bf16[152,768]{1,0:T(8,128)(2,1)S(1)} %collective-permute-done.5.refs_6_), channel_id=1, source_target_pairs={{0,4},{1,5},{4,8},{5,9},{8,12},{9,13},{12,14},{13,15},{14,10},{15,... | collective-permute-start | bytes 700424 | tf_op jit(solution)/shard_map/ppermute | solution.py:216
  23.5 1.4 %collective-permute-start.12 = (bf16[152,768]{1,0:T(8,128)(2,1)S(1)}, bf16[152,768]{1,0:T(8,128)(2,1)S(1)}, u32[]{:S(2)}, u32[]{:S(2)}) collective-permute-start(bf16[152,768]{1,0:T(8,128)(2,1)S(1)} %collective-permute-done.8.refs_9_), channel_id=1, source_target_pairs={{4,0},{5,1},{8,4},{9,5},{12,8},{13,9},{14,12},{15,13},{10,14},{11,... | collective-permute-start | bytes 700424 | tf_op jit(solution)/shard_map/ppermute | solution.py:216
  24.8 3.6 %collective-permute-done.6.refs_7_ = bf16[152,768]{1,0:T(8,128)(2,1)S(1)} collective-permute-done((bf16[152,768]{1,0:T(8,128)(2,1)S(1)}, bf16[152,768]{1,0:T(8,128)(2,1)S(1)}, u32[]{:S(2)}, u32[]{:S(2)}) %collective-permute-start.6) | collective-permute-done | bytes 233504 | tf_op jit(solution)/shard_map/ppermute | solution.py:216
  28.5 1.4 %collective-permute-start.10 = (bf16[152,768]{1,0:T(8,128)(2,1)S(1)}, bf16[152,768]{1,0:T(8,128)(2,1)S(1)}, u32[]{:S(2)}, u32[]{:S(2)}) collective-permute-start(bf16[152,768]{1,0:T(8,128)(2,1)S(1)} %collective-permute-done.6.refs_7_), channel_id=1, source_target_pairs={{4,0},{5,1},{8,4},{9,5},{12,8},{13,9},{14,12},{15,13},{10,14},{11,... | collective-permute-start | bytes 700424 | tf_op jit(solution)/shard_map/ppermute | solution.py:216
  29.8 0.7 %collective-permute-start.11 = (bf16[152,768]{1,0:T(8,128)(2,1)S(1)}, bf16[152,768]{1,0:T(8,128)(2,1)S(1)}, u32[]{:S(2)}, u32[]{:S(2)}) collective-permute-start(bf16[152,768]{1,0:T(8,128)(2,1)S(1)} %collective-permute-done.7.refs_8_), channel_id=1, source_target_pairs={{0,4},{1,5},{4,8},{5,9},{8,12},{9,13},{12,14},{13,15},{14,10},{15,... | collective-permute-start | bytes 700424 | tf_op jit(solution)/shard_map/ppermute | solution.py:216
  30.5 1.1 %collective-permute-done.9.refs_10_ = bf16[152,768]{1,0:T(8,128)(2,1)S(1)} collective-permute-done((bf16[152,768]{1,0:T(8,128)(2,1)S(1)}, bf16[152,768]{1,0:T(8,128)(2,1)S(1)}, u32[]{:S(2)}, u32[]{:S(2)}) %collective-permute-start.9) | collective-permute-done | bytes 233504 | tf_op jit(solution)/shard_map/ppermute | solution.py:216
  31.6 2.5 %collective-permute-start.13 = (bf16[152,768]{1,0:T(8,128)(2,1)S(1)}, bf16[152,768]{1,0:T(8,128)(2,1)S(1)}, u32[]{:S(2)}, u32[]{:S(2)}) collective-permute-start(bf16[152,768]{1,0:T(8,128)(2,1)S(1)} %collective-permute-done.9.refs_10_), channel_id=1, source_target_pairs={{0,4},{1,5},{4,8},{5,9},{8,12},{9,13},{12,14},{13,15},{14,10},{15,... | collective-permute-start | bytes 700424 | tf_op jit(solution)/shard_map/ppermute | solution.py:216
  34.1 0.7 %collective-permute-start.14 = (bf16[152,768]{1,0:T(8,128)(2,1)S(1)}, bf16[152,768]{1,0:T(8,128)(2,1)S(1)}, u32[]{:S(2)}, u32[]{:S(2)}) collective-permute-start(bf16[152,768]{1,0:T(8,128)(2,1)S(1)} %collective-permute-done.12.refs_13_), channel_id=1, source_target_pairs={{4,0},{5,1},{8,4},{9,5},{12,8},{13,9},{14,12},{15,13},{10,14},{11,... | collective-permute-start | bytes 700424 | tf_op jit(solution)/shard_map/ppermute | solution.py:216
  34.8 2.5 %fetch.1 = (bf16[1024,1536]{1,0:T(8,128)(2,1)S(1)}, bf16[1024,896]{1,0:T(8,128)(2,1)S(1)}) custom-call(bf16[1024,1536]{1,0:T(8,128)(2,1)} %refs_0_, bf16[1024,896]{1,0:T(8,128)(2,1)} %refs_1_.1), custom_call_target="tpu_custom_call" | custom-call | tf_op jit(solution)/shard_map/fetch/pallas_call | solution.py:99
  37.3 1.2 %collective-permute-done.10.refs_11_ = bf16[152,768]{1,0:T(8,128)(2,1)S(1)} collective-permute-done((bf16[152,768]{1,0:T(8,128)(2,1)S(1)}, bf16[152,768]{1,0:T(8,128)(2,1)S(1)}, u32[]{:S(2)}, u32[]{:S(2)}) %collective-permute-start.10) | collective-permute-done | bytes 233504 | tf_op jit(solution)/shard_map/ppermute | solution.py:216
  38.5 0.2 early.1
  38.8 2.4 %collective-permute-done.13.refs_14_.refs_0_ = bf16[152,768]{1,0:T(8,128)(2,1)S(1)} collective-permute-done((bf16[152,768]{1,0:T(8,128)(2,1)S(1)}, bf16[152,768]{1,0:T(8,128)(2,1)S(1)}, u32[]{:S(2)}, u32[]{:S(2)}) %collective-permute-start.13) | collective-permute-done | bytes 233504 | tf_op jit(solution)/shard_map/ppermute | solution.py:216
  41.2 1.5 %collective-permute-done.14.refs_15_.refs_1_ = bf16[152,768]{1,0:T(8,128)(2,1)S(1)} collective-permute-done((bf16[152,768]{1,0:T(8,128)(2,1)S(1)}, bf16[152,768]{1,0:T(8,128)(2,1)S(1)}, u32[]{:S(2)}, u32[]{:S(2)}) %collective-permute-start.14) | collective-permute-done | bytes 233504 | tf_op jit(solution)/shard_map/ppermute | solution.py:216
  42.8 0.2 place_own_p.1.panel
  43.0 2.6 %lower_own.1.refs_0_.own_lower = bf16[1024,768]{1,0:T(8,128)(2,1)S(1)} custom-call(bf16[1024,1536]{1,0:T(8,128)(2,1)S(1)} %get-tuple-element.11.column, bf16[1536,768]{1,0:T(8,128)(2,1)S(1)} %place_own_p.1.panel), custom_call_target="tpu_custom_call" | custom-call | flops 48318382080 | bytes 7077888 | tf_op jit(solution)/shard_map/lower_own/pallas_call | solution.py:153
  45.8 0.2 place_other_p.1.panel
  46.0 3.5 %lower_other.1 = (bf16[1024,768]{1,0:T(8,128)(2,1)S(1)}, bf16[1024,1536]{1,0:T(8,128)(2,1)}) custom-call(bf16[1024,1536]{1,0:T(8,128)(2,1)S(1)} %get-tuple-element.11.column, bf16[1536,768]{1,0:T(8,128)(2,1)S(1)} %place_other_p.1.panel, bf16[1024,768]{1,0:T(8,128)(2,1)S(1)} %lower_own.1.refs_0_.own_lower), custom_call_target="tpu_custom_call" | custom-call | flops 48318382080 | bytes 7077888 | tf_op jit(solution)/shard_map/lower_other/pallas_call | solution.py:153
  49.6 0.1 place_other_r.1.other_panel
  49.7 5.4 %schur.1 = (bf16[1024,1536]{1,0:T(8,128)(2,1)}, bf16[1024,896]{1,0:T(8,128)(2,1)}) custom-call(bf16[1024,768]{1,0:T(8,128)(2,1)S(1)} %lower_own.1.refs_0_.own_lower, bf16[896,768]{1,0:T(8,128)(2,1)S(1)} %place_own_r.1.own_panel, bf16[1024,768]{1,0:T(8,128)(2,1)S(1)} %get-tuple-element.13.other_lower, ...), custom_call_target="tpu_custom_call", output_to_operand_aliasing={{0}: (5, {})} | custom-call | flops 2818572288 | bytes 9568256 | tf_op jit(solution)/shard_map/schur/pallas_call | solution.py:192
  (13 shorter events, 0.4 us)
Async XLA Ops:
  1.8 3.2 %collective-permute-start.1 = (bf16[152,768]{1,0:T(8,128)(2,1)S(1)}, bf16[152,768]{1,0:T(8,128)(2,1)S(1)}, u32[]{:S(2)}, u32[]{:S(2)}) collective-permute-start(bf16[152,768]{1,0:T(8,128)(2,1)S(1)} %get-tuple-element.12), channel_id=1, source_target_pairs={{0,1},{1,0},{2,3},{3,2},{4,5},{5,4},{6,7},{7,6},{8,9},{9,8},{10,11... | collective-permute-start | bytes 700424 | tf_op jit(solution)/shard_map/ppermute | solution.py:216
  2.3 9.1 %collective-permute-start = (bf16[152,768]{1,0:T(8,128)(2,1)S(1)}, bf16[152,768]{1,0:T(8,128)(2,1)S(1)}, u32[]{:S(2)}, u32[]{:S(2)}) collective-permute-start(bf16[152,768]{1,0:T(8,128)(2,1)S(1)} %get-tuple-element.9.refs_0_), channel_id=1, source_target_pairs={{0,4},{1,5},{4,8},{5,9},{8,12},{9,13},{12,14},{13,15},{14,10},{15,... | collective-permute-start | bytes 700424 | tf_op jit(solution)/shard_map/ppermute | solution.py:216
  4.9 8.5 %collective-permute-start.4 = (bf16[152,768]{1,0:T(8,128)(2,1)S(1)}, bf16[152,768]{1,0:T(8,128)(2,1)S(1)}, u32[]{:S(2)}, u32[]{:S(2)}) collective-permute-start(bf16[152,768]{1,0:T(8,128)(2,1)S(1)} %collective-permute-done.1.refs_1_), channel_id=1, source_target_pairs={{4,0},{5,1},{8,4},{9,5},{12,8},{13,9},{14,12},{15,13},{10,14},{11,... | collective-permute-start | bytes 700424 | tf_op jit(solution)/shard_map/ppermute | solution.py:216
  6.3 12.2 %collective-permute-start.2 = (bf16[152,768]{1,0:T(8,128)(2,1)S(1)}, bf16[152,768]{1,0:T(8,128)(2,1)S(1)}, u32[]{:S(2)}, u32[]{:S(2)}) collective-permute-start(bf16[152,768]{1,0:T(8,128)(2,1)S(1)} %get-tuple-element.9.refs_0_), channel_id=1, source_target_pairs={{4,0},{5,1},{8,4},{9,5},{12,8},{13,9},{14,12},{15,13},{10,14},{11,... | collective-permute-start | bytes 700424 | tf_op jit(solution)/shard_map/ppermute | solution.py:216
  7.9 12.0 %collective-permute-start.3 = (bf16[152,768]{1,0:T(8,128)(2,1)S(1)}, bf16[152,768]{1,0:T(8,128)(2,1)S(1)}, u32[]{:S(2)}, u32[]{:S(2)}) collective-permute-start(bf16[152,768]{1,0:T(8,128)(2,1)S(1)} %collective-permute-done.1.refs_1_), channel_id=1, source_target_pairs={{0,4},{1,5},{4,8},{5,9},{8,12},{9,13},{12,14},{13,15},{14,10},{15,... | collective-permute-start | bytes 700424 | tf_op jit(solution)/shard_map/ppermute | solution.py:216
  11.4 10.1 %collective-permute-start.5 = (bf16[152,768]{1,0:T(8,128)(2,1)S(1)}, bf16[152,768]{1,0:T(8,128)(2,1)S(1)}, u32[]{:S(2)}, u32[]{:S(2)}) collective-permute-start(bf16[152,768]{1,0:T(8,128)(2,1)S(1)} %collective-permute-done.refs_2_), channel_id=1, source_target_pairs={{0,4},{1,5},{4,8},{5,9},{8,12},{9,13},{12,14},{13,15},{14,10},{15,... | collective-permute-start | bytes 700424 | tf_op jit(solution)/shard_map/ppermute | solution.py:216
  13.5 10.0 %collective-permute-start.8 = (bf16[152,768]{1,0:T(8,128)(2,1)S(1)}, bf16[152,768]{1,0:T(8,128)(2,1)S(1)}, u32[]{:S(2)}, u32[]{:S(2)}) collective-permute-start(bf16[152,768]{1,0:T(8,128)(2,1)S(1)} %collective-permute-done.4.refs_5_), channel_id=1, source_target_pairs={{4,0},{5,1},{8,4},{9,5},{12,8},{13,9},{14,12},{15,13},{10,14},{11,... | collective-permute-start | bytes 700424 | tf_op jit(solution)/shard_map/ppermute | solution.py:216
  18.5 10.0 %collective-permute-start.6 = (bf16[152,768]{1,0:T(8,128)(2,1)S(1)}, bf16[152,768]{1,0:T(8,128)(2,1)S(1)}, u32[]{:S(2)}, u32[]{:S(2)}) collective-permute-start(bf16[152,768]{1,0:T(8,128)(2,1)S(1)} %collective-permute-done.2.refs_3_), channel_id=1, source_target_pairs={{4,0},{5,1},{8,4},{9,5},{12,8},{13,9},{14,12},{15,13},{10,14},{11,... | collective-permute-start | bytes 700424 | tf_op jit(solution)/shard_map/ppermute | solution.py:216
  19.8 10.0 %collective-permute-start.7 = (bf16[152,768]{1,0:T(8,128)(2,1)S(1)}, bf16[152,768]{1,0:T(8,128)(2,1)S(1)}, u32[]{:S(2)}, u32[]{:S(2)}) collective-permute-start(bf16[152,768]{1,0:T(8,128)(2,1)S(1)} %collective-permute-done.3.refs_4_), channel_id=1, source_target_pairs={{0,4},{1,5},{4,8},{5,9},{8,12},{9,13},{12,14},{13,15},{14,10},{15,... | collective-permute-start | bytes 700424 | tf_op jit(solution)/shard_map/ppermute | solution.py:216
  21.5 10.1 %collective-permute-start.9 = (bf16[152,768]{1,0:T(8,128)(2,1)S(1)}, bf16[152,768]{1,0:T(8,128)(2,1)S(1)}, u32[]{:S(2)}, u32[]{:S(2)}) collective-permute-start(bf16[152,768]{1,0:T(8,128)(2,1)S(1)} %collective-permute-done.5.refs_6_), channel_id=1, source_target_pairs={{0,4},{1,5},{4,8},{5,9},{8,12},{9,13},{12,14},{13,15},{14,10},{15,... | collective-permute-start | bytes 700424 | tf_op jit(solution)/shard_map/ppermute | solution.py:216
  23.5 10.7 %collective-permute-start.12 = (bf16[152,768]{1,0:T(8,128)(2,1)S(1)}, bf16[152,768]{1,0:T(8,128)(2,1)S(1)}, u32[]{:S(2)}, u32[]{:S(2)}) collective-permute-start(bf16[152,768]{1,0:T(8,128)(2,1)S(1)} %collective-permute-done.8.refs_9_), channel_id=1, source_target_pairs={{4,0},{5,1},{8,4},{9,5},{12,8},{13,9},{14,12},{15,13},{10,14},{11,... | collective-permute-start | bytes 700424 | tf_op jit(solution)/shard_map/ppermute | solution.py:216
  28.5 10.0 %collective-permute-start.10 = (bf16[152,768]{1,0:T(8,128)(2,1)S(1)}, bf16[152,768]{1,0:T(8,128)(2,1)S(1)}, u32[]{:S(2)}, u32[]{:S(2)}) collective-permute-start(bf16[152,768]{1,0:T(8,128)(2,1)S(1)} %collective-permute-done.6.refs_7_), channel_id=1, source_target_pairs={{4,0},{5,1},{8,4},{9,5},{12,8},{13,9},{14,12},{15,13},{10,14},{11,... | collective-permute-start | bytes 700424 | tf_op jit(solution)/shard_map/ppermute | solution.py:216
  29.8 8.6 %collective-permute-start.11 = (bf16[152,768]{1,0:T(8,128)(2,1)S(1)}, bf16[152,768]{1,0:T(8,128)(2,1)S(1)}, u32[]{:S(2)}, u32[]{:S(2)}) collective-permute-start(bf16[152,768]{1,0:T(8,128)(2,1)S(1)} %collective-permute-done.7.refs_8_), channel_id=1, source_target_pairs={{0,4},{1,5},{4,8},{5,9},{8,12},{9,13},{12,14},{13,15},{14,10},{15,... | collective-permute-start | bytes 700424 | tf_op jit(solution)/shard_map/ppermute | solution.py:216
  31.6 9.5 %collective-permute-start.13 = (bf16[152,768]{1,0:T(8,128)(2,1)S(1)}, bf16[152,768]{1,0:T(8,128)(2,1)S(1)}, u32[]{:S(2)}, u32[]{:S(2)}) collective-permute-start(bf16[152,768]{1,0:T(8,128)(2,1)S(1)} %collective-permute-done.9.refs_10_), channel_id=1, source_target_pairs={{0,4},{1,5},{4,8},{5,9},{8,12},{9,13},{12,14},{13,15},{14,10},{15,... | collective-permute-start | bytes 700424 | tf_op jit(solution)/shard_map/ppermute | solution.py:216
  34.1 8.6 %collective-permute-start.14 = (bf16[152,768]{1,0:T(8,128)(2,1)S(1)}, bf16[152,768]{1,0:T(8,128)(2,1)S(1)}, u32[]{:S(2)}, u32[]{:S(2)}) collective-permute-start(bf16[152,768]{1,0:T(8,128)(2,1)S(1)} %collective-permute-done.12.refs_13_), channel_id=1, source_target_pairs={{4,0},{5,1},{8,4},{9,5},{12,8},{13,9},{14,12},{15,13},{10,14},{11,... | collective-permute-start | bytes 700424 | tf_op jit(solution)/shard_map/ppermute | solution.py:216
  38.7 7.1 %collective-permute-start.15 = (bf16[2128,768]{1,0:T(8,128)(2,1)S(1)}, bf16[2128,768]{1,0:T(8,128)(2,1)S(1)}, u32[]{:S(2)}, u32[]{:S(2)}) collective-permute-start(bf16[2128,768]{1,0:T(8,128)(2,1)S(1)} %early.1), channel_id=1, source_target_pairs={{0,1},{1,0},{2,3},{3,2},{4,5},{5,4},{6,7},{7,6},{8,9},{9,8},{10,11... | collective-permute-start | bytes 9805832 | tf_op jit(solution)/shard_map/ppermute | solution.py:216
  42.7 3.0 %collective-permute-start.16 = (bf16[304,768]{1,0:T(8,128)(2,1)S(1)}, bf16[304,768]{1,0:T(8,128)(2,1)S(1)}, u32[]{:S(2)}, u32[]{:S(2)}) collective-permute-start(bf16[304,768]{1,0:T(8,128)(2,1)S(1)} %late.1), channel_id=1, source_target_pairs={{0,1},{1,0},{2,3},{3,2},{4,5},{5,4},{6,7},{7,6},{8,9},{9,8},{10,11... | collective-permute-start | bytes 1400840 | tf_op jit(solution)/shard_map/ppermute | solution.py:216

commit v3 on v2

v3 whole, which is shorter than its diff:
```python
import functools

import jax
import jax.numpy as jnp
from jax import lax
from jax.experimental import pallas as pl
from jax.experimental.pallas import tpu as pltpu
from jax.sharding import PartitionSpec as P

F32, BF16 = jnp.float32, jnp.bfloat16
ON_CHIP = pl.BlockSpec(memory_space=pltpu.VMEM)
IN_HBM = pl.BlockSpec(memory_space=pltpu.HBM)
PARAMS = pltpu.CompilerParams(vmem_limit_bytes=16 << 20)
CHUNKS = 4
WEIGHT = 20
FETCH_AT = 2
MARK = 10_000_000_000


def shape(*dims):
    return jax.ShapeDtypeStruct(dims, BF16)


def cost(flops, nbytes):
    return pl.CostEstimate(flops=flops, bytes_accessed=nbytes, transcendentals=0)


def small(kernel, out_shape, operands, name):
    return pl.pallas_call(
        kernel,
        out_shape=out_shape,
        in_specs=[ON_CHIP] * len(operands),
        out_specs=jax.tree.map(lambda _: ON_CHIP, out_shape),
        compiler_params=PARAMS,
        name=name,
    )(*operands)


def in_hbm(x):
    return pltpu.with_memory_space_constraint(x, pltpu.HBM)


def after(value, *others):
    return lax.optimization_barrier((value, *others))[0]


def ring_of(chips):
    if chips > 8:
        return list(range(chips))
    return list(range(0, chips, 2)) + list(range(chips - 1, 0, -2))


def chip_at(distance, chips):
    chip = lax.axis_index("row") // 2
    if chips > 8:
        return lax.rem(chip + distance + chips, chips)
    place = jnp.where(lax.rem(chip, 2) == 0, chip // 2, chips - 1 - chip // 2)
    place = lax.rem(place + distance + chips, chips)
    return jnp.where(place < chips // 2, 2 * place, 2 * (chips - 1 - place) + 1)


def my_core():
    return lax.rem(lax.axis_index("row"), 2)


def part_of(rows):
    return -(-rows // 16) * 8


def stack(parts, name):
    sizes = [part_of(rows) if mine else rows for _, _, rows, mine in parts]

    def kernel(*refs):
        to = 0
        for ref, (_, start, rows, mine), size in zip(refs, parts, sizes):
            taken = ref[start : start + size]
            if mine:
                taken = jnp.where(my_core() == 0, taken, ref[start + rows - size : start + rows])
            refs[-1][to : to + size] = taken
            to += size

    return small(kernel, shape(sum(sizes), parts[0][0].shape[1]), [part[0] for part in parts], name)


def place(parts, rows, chips, name):
    def kernel(*refs):
        core = my_core()
        for ref, (_, start, steps, stream, side) in zip(refs, parts):
            by = core if side == 0 else 1 - core
            chip = chip_at(jnp.where(by == 0, -steps, steps), chips)
            at = (2 * chip + (by if stream == 0 else 1 - by)) * rows
            size = rows
            if 2 * steps == chips:
                size = part_of(rows)
                at += by * (rows - size)
            refs[-1][pl.ds(pl.multiple_of(at, 8), size), :] = ref[start : start + size]

    cols = parts[0][0].shape[1]
    return small(kernel, shape(2 * chips * rows, cols), [part[0] for part in parts], name)


def mark(piece):
    def kernel(piece_ref, out):
        out[...] = piece_ref[:16, :128]

    return pl.pallas_call(
        kernel,
        out_shape=shape(16, 128),
        in_specs=[ON_CHIP],
        out_specs=ON_CHIP,
        compiler_params=PARAMS,
        cost_estimate=cost(MARK, 0),
        name="mark",
    )(piece)


def fetch_kernel(*refs):
    count = len(refs) // 2
    copies = [pltpu.make_async_copy(refs[i], refs[count + i], refs[-1].at[i]) for i in range(count)]
    for copy in copies:
        copy.start()
    for copy in copies:
        copy.wait()


def fetch(*arrays):
    return pl.pallas_call(
        fetch_kernel,
        out_shape=tuple(shape(*x.shape) for x in arrays),
        in_specs=[IN_HBM] * len(arrays),
        out_specs=(ON_CHIP,) * len(arrays),
        scratch_shapes=[pltpu.SemaphoreType.DMA((len(arrays),))],
        compiler_params=PARAMS,
        name="fetch",
    )(*map(in_hbm, arrays))


def lower_kernel(part, column, panel, out):
    rows, half = column.shape[0] // CHUNKS, out.shape[1]
    for i in range(CHUNKS):
        at = pl.ds(i * rows, rows)
        out[at] = jnp.dot(
            column[at], panel[:, part * half : (part + 1) * half], preferred_element_type=F32
        ).astype(BF16)


def lower(column_block, panel, part):
    n, k = column_block.shape
    half = panel.shape[1] // 2
    return pl.pallas_call(
        functools.partial(lower_kernel, part),
        out_shape=shape(n, half),
        in_specs=[ON_CHIP, ON_CHIP],
        out_specs=ON_CHIP,
        compiler_params=PARAMS,
        cost_estimate=cost(WEIGHT * 2 * n * k * half, 2 * (n * k + k * half + n * half)),
        name="lower",
    )(column_block, panel)


def schur_kernel(left, right, panel, coupling, lower_out, out, done, out_sems, lower_sems):
    half = left.shape[1]
    copies = []
    for i, ref in enumerate((left, right)):
        copies.append(pltpu.make_async_copy(ref, lower_out.at[:, pl.ds(i * half, half)], lower_sems.at[i]))
        copies[-1].start()
    contract = (((1,), (1,)), ((), ()))
    rows = coupling.shape[0] // CHUNKS
    for i in range(CHUNKS):
        at = pl.ds(i * rows, rows)
        product = lax.dot_general(left[at], panel[:, :half], contract, preferred_element_type=F32)
        product += lax.dot_general(right[at], panel[:, half:], contract, preferred_element_type=F32)
        done[at] = (coupling[at].astype(F32) - product).astype(BF16)
        copies.append(pltpu.make_async_copy(done.at[at], out.at[at], out_sems.at[i]))
        copies[-1].start()
    for copy in copies:
        copy.wait()


def schur(left, right, panel, coupling):
    n, cols = coupling.shape
    k = 2 * left.shape[1]
    return pl.pallas_call(
        schur_kernel,
        out_shape=(shape(n, k), shape(n, cols)),
        in_specs=[ON_CHIP] * 4,
        out_specs=(IN_HBM, IN_HBM),
        scratch_shapes=[
            pltpu.VMEM((n, cols), BF16),
            pltpu.SemaphoreType.DMA((CHUNKS,)),
            pltpu.SemaphoreType.DMA((2,)),
        ],
        compiler_params=PARAMS,
        cost_estimate=cost(2 * n * k * cols, 2 * (2 * n * k + k * cols + 2 * n * cols)),
        name="schur",
    )(left, right, panel, coupling)


def on_device(devices, coupling, column_block, pivot_inverse, row_panel):
    chips = devices // 2
    steps = chips // 2
    ring = ring_of(chips)
    swap = [(i, i ^ 1) for i in range(devices)]
    hops = [(ring[i], ring[(i + 1) % chips]) for i in range(chips)]
    along = [(2 * a, 2 * b) for a, b in hops] + [(2 * b + 1, 2 * a + 1) for a, b in hops]
    on = lambda x: lax.ppermute(x, "row", along)
    over = lambda x: lax.ppermute(x, "row", swap)
    p_rows, r_rows = pivot_inverse.shape[0], row_panel.shape[1]

    p_start = [pivot_inverse, over(pivot_inverse)]
    (row_panel,) = fetch(row_panel.T)
    r_start = [row_panel, over(row_panel)]
    p_parts = [(p_start[s], 0, 0, s, 0) for s in range(2)]
    r_parts = [(r_start[s], 0, 0, s, 0) for s in range(2)]

    def keep(x, k, s, p_at, r_at):
        for side, y in enumerate((x, over(x))):
            if p_at is not None:
                p_parts.append((y, p_at, k, s, side))
            if r_at is not None:
                r_parts.append((y, r_at, k - 1, s, side))

    held = p_start
    for k in range(1, steps):
        held = [on(x) for x in held]
        for s in range(2):
            keep(held[s], k, s, 0, p_rows if k > 1 else None)
        held[1] = after(held[1], mark(held[0]))
        if k == 1:
            held = [stack([(held[s], 0, p_rows, False), (r_start[s], 0, r_rows, False)], "follow") for s in range(2)]
        if k == FETCH_AT:
            column_block, coupling = fetch(after(column_block, held[0]), coupling)
            held[1] = after(held[1], column_block)
    held = [on(stack([(x, 0, p_rows, True), (x, p_rows, r_rows, False)], "opposite_p")) for x in held]
    for s in range(2):
        keep(held[s], steps, s, 0, part_of(p_rows))
    held[1] = after(held[1], mark(held[0]))
    last = on(stack([(x, part_of(p_rows), r_rows, True) for x in held], "opposite_r"))

    panel = place(p_parts, p_rows, chips, "place_p")
    left = lower(column_block, panel, 0)
    for side, x in enumerate((last, over(after(last, left)))):
        r_parts += [(x, s * part_of(r_rows), steps, s, side) for s in range(2)]
    right = lower(column_block, after(panel, last), 1)
    return schur(left, right, place(r_parts, r_rows, chips, "place_r"), coupling)


def by_all_gather(coupling, column_block, pivot_inverse, row_panel):
    whole_inverse = lax.all_gather(pivot_inverse, "row", axis=0, tiled=True)
    whole_panel = lax.all_gather(row_panel, "row", axis=1, tiled=True)
    lower_panel = jnp.dot(column_block, whole_inverse, preferred_element_type=F32).astype(BF16)
    product = jnp.dot(lower_panel, whole_panel, preferred_element_type=F32)
    return lower_panel, (coupling.astype(F32) - product).astype(BF16)


def solution(mesh):
    devices = mesh.shape["row"]
    parts = mesh.shape["groups"]

    def step(coupling, column_block, pivot_inverse, row_panel):
        fits = devices % 4 == 0 and devices >= 12
        fits &= row_panel.shape[1] // (parts * devices) % 8 == 0
        fits &= pivot_inverse.shape[0] // (parts * devices) % 8 == 0
        body = functools.partial(on_device, devices) if fits else by_all_gather
        rows = P(("groups", "row"), None)
        return jax.shard_map(
            body,
            mesh=mesh,
            in_specs=(rows, rows, rows, P(None, ("groups", "row"))),
            out_specs=(rows, rows),
            check_vma=False,
        )(coupling, column_block, pivot_inverse, row_panel)

    return step
```

time: 55.2 us -> 53.6 us (0.971)
  Pallas kernels: 16 us -> 13.6 us
    pallas_call x3 -> x2, Pallas kernels: 7.26 us -> 5.19 us  [lower(): pl.pallas_call(functools.partial(lower_kernel, part), out_shape=shape(n,...]
    pallas_call x1, Pallas kernels: 5.38 us -> 4.27 us  [schur(): pl.pallas_call(schur_kernel, out_shape=(shape(n, k), shape(n, cols)), in_...]
    pallas_call x1 -> x2, Pallas kernels: 2.46 us -> 3.39 us  [fetch(): pl.pallas_call(fetch_kernel, out_shape=tuple((shape(*x.shape) for x in ar...]
    ppermute x17 -> x20, waiting for transfers between devices: 17.7 us -> 18.1 us  [the longest x9 18.1 us: on_device(): on = lambda x: lax.ppermute(x, 'row', along)]
    ppermute x17 -> x20, starting transfers between devices: 20.6 us -> 20.9 us  [the longest x9 19.2 us: on_device(): on = lambda x: lax.ppermute(x, 'row', along)]
  transfers between devices with their start and end apart: 17 -> 20, of which waited for: 8 -> 9; matrix products, arithmetic and copies ran while one was open for 0% -> 0% of each run, Pallas kernels for 10% -> 17%
where the time goes in v3:
time: 53.6 us; the launch traced here: 53.4 us
  starting transfers between devices  20.9 us (39%)
  waiting for transfers between devices  18.1 us (34%)
  Pallas kernels  13.6 us (25%)
  between operations  0.77 us (1%)
    ppermute x9, starting transfers between devices, on_device(): on = lambda x: lax.ppermute(x, 'row', along)  19.2 us
    ppermute x9, waiting for transfers between devices, on_device(): on = lambda x: lax.ppermute(x, 'row', along)  18.1 us
    pallas_call x2, Pallas kernels, lower(): pl.pallas_call(functools.partial(lower_kernel, part), out_shape=shape(n,...  5.19 us
    pallas_call x1, Pallas kernels, schur(): pl.pallas_call(schur_kernel, out_shape=(shape(n, k), shape(n, cols)), in_...  4.27 us
    pallas_call x2, Pallas kernels, fetch(): pl.pallas_call(fetch_kernel, out_shape=tuple((shape(*x.shape) for x in ar...  3.39 us
    ppermute x11, starting transfers between devices, on_device(): over = lambda x: lax.ppermute(x, 'row', swap)  1.69 us
  transfers between devices with their start and end apart: 20, of which 9 were waited for; matrix products, arithmetic and copies ran while one was open for 0% of the time, Pallas kernels for 17%

profile of v3, /device:TPU:0, one launch (start us, length us, event | category | flops | bytes accessed | tf_op | source)
XLA Modules:
  0.0 53.4 jit_solution(347894841267881161)
XLA Ops:
  0.6 0.5 collective-permute-start.2
  1.1 2.6 %collective-permute-start = (bf16[96,1536]{1,0:T(8,128)(2,1)}, bf16[96,1536]{1,0:T(8,128)(2,1)S(1)}, u32[]{:S(2)}, u32[]{:S(2)}) collective-permute-start(bf16[96,1536]{1,0:T(8,128)(2,1)} %refs_0_.2), channel_id=1, source_target_pairs={{0,4},{4,8},{8,12},{12,14},{14,10},{10,6},{6,2},{2,0},{5,1},{9,5},... | collective-permute-start | bytes 884744 | tf_op jit(solution)/shard_map/ppermute | solution.py:206
  3.8 0.0 collective-permute-done.2.refs_1_
  3.8 1.7 %collective-permute-start.4 = (bf16[96,1536]{1,0:T(8,128)(2,1)S(1)}, bf16[96,1536]{1,0:T(8,128)(2,1)S(1)}, u32[]{:S(2)}, u32[]{:S(2)}) collective-permute-start(bf16[96,1536]{1,0:T(8,128)(2,1)S(1)} %collective-permute-done.2.refs_1_), channel_id=1, source_target_pairs={{0,4},{4,8},{8,12},{12,14},{14,10},{10,6},{6,2},{2,0},{5,1},{9,5},... | collective-permute-start | bytes 884744 | tf_op jit(solution)/shard_map/ppermute | solution.py:206
  5.5 0.9 %fetch.2.refs_1_.refs_0_ = bf16[56,1536]{1,0:T(8,128)(2,1)S(1)} custom-call(bf16[56,1536]{1,0:T(8,128)(2,1)} %bitcast.1), custom_call_target="tpu_custom_call" | custom-call | tf_op jit(solution)/shard_map/fetch/pallas_call | solution.py:127
  6.4 0.1 collective-permute-start.7
  6.5 2.1 %collective-permute-done.refs_0_.refs_2_ = bf16[96,1536]{1,0:T(8,128)(2,1)S(1)} collective-permute-done((bf16[96,1536]{1,0:T(8,128)(2,1)}, bf16[96,1536]{1,0:T(8,128)(2,1)S(1)}, u32[]{:S(2)}, u32[]{:S(2)}) %collective-permute-start) | collective-permute-done | bytes 294944 | tf_op jit(solution)/shard_map/ppermute | solution.py:206
  8.7 2.1 %collective-permute-start.1 = (bf16[152,1536]{1,0:T(8,128)(2,1)S(1)}, bf16[152,1536]{1,0:T(8,128)(2,1)S(1)}, u32[]{:S(2)}, u32[]{:S(2)}) collective-permute-start(bf16[152,1536]{1,0:T(8,128)(2,1)S(1)} %follow.2), channel_id=1, source_target_pairs={{0,4},{4,8},{8,12},{12,14},{14,10},{10,6},{6,2},{2,0},{5,1},{9,5},... | collective-permute-start | bytes 1400840 | tf_op jit(solution)/shard_map/ppermute | solution.py:206
  10.8 1.0 %collective-permute-done.4.refs_0_.refs_4_ = bf16[96,1536]{1,0:T(8,128)(2,1)S(1)} collective-permute-done((bf16[96,1536]{1,0:T(8,128)(2,1)S(1)}, bf16[96,1536]{1,0:T(8,128)(2,1)S(1)}, u32[]{:S(2)}, u32[]{:S(2)}) %collective-permute-start.4) | collective-permute-done | bytes 294944 | tf_op jit(solution)/shard_map/ppermute | solution.py:206
  11.8 2.1 %collective-permute-start.8 = (bf16[152,1536]{1,0:T(8,128)(2,1)S(1)}, bf16[152,1536]{1,0:T(8,128)(2,1)S(1)}, u32[]{:S(2)}, u32[]{:S(2)}) collective-permute-start(bf16[152,1536]{1,0:T(8,128)(2,1)S(1)} %follow.3), channel_id=1, source_target_pairs={{0,4},{4,8},{8,12},{12,14},{14,10},{10,6},{6,2},{2,0},{5,1},{9,5},... | collective-permute-start | bytes 1400840 | tf_op jit(solution)/shard_map/ppermute | solution.py:206
  14.0 3.3 %collective-permute-done.1.refs_6_.refs_2_ = bf16[152,1536]{1,0:T(8,128)(2,1)S(1)} collective-permute-done((bf16[152,1536]{1,0:T(8,128)(2,1)S(1)}, bf16[152,1536]{1,0:T(8,128)(2,1)S(1)}, u32[]{:S(2)}, u32[]{:S(2)}) %collective-permute-start.1) | collective-permute-done | bytes 466976 | tf_op jit(solution)/shard_map/ppermute | solution.py:206
  17.3 2.5 %fetch.3 = (bf16[1024,1536]{1,0:T(8,128)(2,1)S(1)}, bf16[1024,896]{1,0:T(8,128)(2,1)S(1)}) custom-call(bf16[1024,1536]{1,0:T(8,128)(2,1)} %refs_0_.1, bf16[1024,896]{1,0:T(8,128)(2,1)} %refs_1_.1), custom_call_target="tpu_custom_call" | custom-call | tf_op jit(solution)/shard_map/fetch/pallas_call | solution.py:127
  19.8 0.0 copy-start
  19.8 2.1 %collective-permute-start.10 = (bf16[152,1536]{1,0:T(8,128)(2,1)S(1)}, bf16[152,1536]{1,0:T(8,128)(2,1)S(1)}, u32[]{:S(2)}, u32[]{:S(2)}) collective-permute-start(bf16[152,1536]{1,0:T(8,128)(2,1)S(1)} %collective-permute-done.1.refs_6_.refs_2_), channel_id=1, source_target_pairs={{0,4},{4,8},{8,12},{12,14},{14,10},{10,6},{6,2},{2,0},{5,1},{9,5},... | collective-permute-start | bytes 1400840 | tf_op jit(solution)/shard_map/ppermute | solution.py:206
  21.9 0.4 collective-permute-done.8.refs_8_.refs_4_
  22.3 2.1 %collective-permute-start.12 = (bf16[152,1536]{1,0:T(8,128)(2,1)S(1)}, bf16[152,1536]{1,0:T(8,128)(2,1)S(1)}, u32[]{:S(2)}, u32[]{:S(2)}) collective-permute-start(bf16[152,1536]{1,0:T(8,128)(2,1)S(1)} %collective-permute-done.8.refs_8_.refs_4_), channel_id=1, source_target_pairs={{0,4},{4,8},{8,12},{12,14},{14,10},{10,6},{6,2},{2,0},{5,1},{9,5},... | collective-permute-start | bytes 1400840 | tf_op jit(solution)/shard_map/ppermute | solution.py:206
  24.4 0.5 collective-permute-start.3
  24.9 3.5 %collective-permute-done.10.refs_0_.refs_1_.refs_10_.refs_6_ = bf16[152,1536]{1,0:T(8,128)(2,1)S(1)} collective-permute-done((bf16[152,1536]{1,0:T(8,128)(2,1)S(1)}, bf16[152,1536]{1,0:T(8,128)(2,1)S(1)}, u32[]{:S(2)}, u32[]{:S(2)}) %collective-permute-start.10) | collective-permute-done | bytes 466976 | tf_op jit(solution)/shard_map/ppermute | solution.py:206
  28.4 2.1 %collective-permute-start.14 = (bf16[104,1536]{1,0:T(8,128)(2,1)S(1)}, bf16[104,1536]{1,0:T(8,128)(2,1)S(1)}, u32[]{:S(2)}, u32[]{:S(2)}) collective-permute-start(bf16[104,1536]{1,0:T(8,128)(2,1)S(1)} %opposite_p.2), channel_id=1, source_target_pairs={{0,4},{4,8},{8,12},{12,14},{14,10},{10,6},{6,2},{2,0},{5,1},{9,5},... | collective-permute-start | bytes 958472 | tf_op jit(solution)/shard_map/ppermute | solution.py:206
  30.6 2.8 %collective-permute-done.12.refs_0_.refs_1_.refs_12_.refs_8_ = bf16[152,1536]{1,0:T(8,128)(2,1)S(1)} collective-permute-done((bf16[152,1536]{1,0:T(8,128)(2,1)S(1)}, bf16[152,1536]{1,0:T(8,128)(2,1)S(1)}, u32[]{:S(2)}, u32[]{:S(2)}) %collective-permute-start.12) | collective-permute-done | bytes 466976 | tf_op jit(solution)/shard_map/ppermute | solution.py:206
  33.4 2.1 %collective-permute-start.16 = (bf16[104,1536]{1,0:T(8,128)(2,1)S(1)}, bf16[104,1536]{1,0:T(8,128)(2,1)S(1)}, u32[]{:S(2)}, u32[]{:S(2)}) collective-permute-start(bf16[104,1536]{1,0:T(8,128)(2,1)S(1)} %opposite_p.3), channel_id=1, source_target_pairs={{0,4},{4,8},{8,12},{12,14},{14,10},{10,6},{6,2},{2,0},{5,1},{9,5},... | collective-permute-start | bytes 958472 | tf_op jit(solution)/shard_map/ppermute | solution.py:206
  35.6 0.5 collective-permute-start.11
  36.1 0.1 collective-permute-start.13
  36.2 0.7 %collective-permute-done.14.refs_14_.refs_0_.refs_10_ = bf16[104,1536]{1,0:T(8,128)(2,1)S(1)} collective-permute-done((bf16[104,1536]{1,0:T(8,128)(2,1)S(1)}, bf16[104,1536]{1,0:T(8,128)(2,1)S(1)}, u32[]{:S(2)}, u32[]{:S(2)}) %collective-permute-start.14) | collective-permute-done | bytes 319520 | tf_op jit(solution)/shard_map/ppermute | solution.py:206
  36.8 3.6 %collective-permute-done.16.refs_16_.refs_1_.refs_12_ = bf16[104,1536]{1,0:T(8,128)(2,1)S(1)} collective-permute-done((bf16[104,1536]{1,0:T(8,128)(2,1)S(1)}, bf16[104,1536]{1,0:T(8,128)(2,1)S(1)}, u32[]{:S(2)}, u32[]{:S(2)}) %collective-permute-start.16) | collective-permute-done | bytes 319520 | tf_op jit(solution)/shard_map/ppermute | solution.py:206
  40.5 2.1 %collective-permute-start.18 = (bf16[64,1536]{1,0:T(8,128)(2,1)S(1)}, bf16[64,1536]{1,0:T(8,128)(2,1)S(1)}, u32[]{:S(2)}, u32[]{:S(2)}) collective-permute-start(bf16[64,1536]{1,0:T(8,128)(2,1)S(1)} %opposite_r.1), channel_id=1, source_target_pairs={{0,4},{4,8},{8,12},{12,14},{14,10},{10,6},{6,2},{2,0},{5,1},{9,5},... | collective-permute-start | bytes 589832 | tf_op jit(solution)/shard_map/ppermute | solution.py:206
  42.7 0.4 place_p.1.panel
  43.0 2.6 %lower.2.left = bf16[1024,768]{1,0:T(8,128)(2,1)S(1)} custom-call(bf16[1024,1536]{1,0:T(8,128)(2,1)S(1)} %get-tuple-element.9.column, bf16[1536,1536]{1,0:T(8,128)(2,1)S(1)} %place_p.1.panel), custom_call_target="tpu_custom_call" | custom-call | flops 48318382080 | bytes 7077888 | tf_op jit(solution)/shard_map/lower/pallas_call | solution.py:150
  45.7 0.6 %collective-permute-done.18.refs_14_.refs_15_ = bf16[64,1536]{1,0:T(8,128)(2,1)S(1)} collective-permute-done((bf16[64,1536]{1,0:T(8,128)(2,1)S(1)}, bf16[64,1536]{1,0:T(8,128)(2,1)S(1)}, u32[]{:S(2)}, u32[]{:S(2)}) %collective-permute-start.18) | collective-permute-done | bytes 196640 | tf_op jit(solution)/shard_map/ppermute | solution.py:206
  46.3 2.6 %lower.3.right = bf16[1024,768]{1,0:T(8,128)(2,1)S(1)} custom-call(bf16[1024,1536]{1,0:T(8,128)(2,1)S(1)} %get-tuple-element.9.column, bf16[1536,1536]{1,0:T(8,128)(2,1)S(1)} %place_p.1.panel), custom_call_target="tpu_custom_call" | custom-call | flops 48318382080 | bytes 7077888 | tf_op jit(solution)/shard_map/lower/pallas_call | solution.py:150
  48.9 0.2 place_r.1.panel
  49.1 4.3 %schur.1 = (bf16[1024,1536]{1,0:T(8,128)(2,1)}, bf16[1024,896]{1,0:T(8,128)(2,1)}) custom-call(bf16[1024,768]{1,0:T(8,128)(2,1)S(1)} %lower.2.left, bf16[1024,768]{1,0:T(8,128)(2,1)S(1)} %lower.3.right, bf16[896,1536]{1,0:T(8,128)(2,1)S(1)} %place_r.1.panel, bf16[1024,896]{1,0:T(8,128)(2,1)S(1)} %get-tuple-element.13.coupling), custom_call_target="tpu_custom_call" | custom-call | flops 2818572288 | bytes 12713984 | tf_op jit(solution)/shard_map/schur/pallas_call | solution.py:183
  (22 shorter events, 0.2 us)
Async XLA Ops:
  0.6 3.2 %collective-permute-start.2 = (bf16[96,1536]{1,0:T(8,128)(2,1)}, bf16[96,1536]{1,0:T(8,128)(2,1)S(1)}, u32[]{:S(2)}, u32[]{:S(2)}) collective-permute-start(bf16[96,1536]{1,0:T(8,128)(2,1)} %refs_0_.2), channel_id=1, source_target_pairs={{0,1},{1,0},{2,3},{3,2},{4,5},{5,4},{6,7},{7,6},{8,9},{9,8},{10,11... | collective-permute-start | bytes 884744 | tf_op jit(solution)/shard_map/ppermute | solution.py:207
  1.1 7.5 %collective-permute-start = (bf16[96,1536]{1,0:T(8,128)(2,1)}, bf16[96,1536]{1,0:T(8,128)(2,1)S(1)}, u32[]{:S(2)}, u32[]{:S(2)}) collective-permute-start(bf16[96,1536]{1,0:T(8,128)(2,1)} %refs_0_.2), channel_id=1, source_target_pairs={{0,4},{4,8},{8,12},{12,14},{14,10},{10,6},{6,2},{2,0},{5,1},{9,5},... | collective-permute-start | bytes 884744 | tf_op jit(solution)/shard_map/ppermute | solution.py:206
  3.8 8.0 %collective-permute-start.4 = (bf16[96,1536]{1,0:T(8,128)(2,1)S(1)}, bf16[96,1536]{1,0:T(8,128)(2,1)S(1)}, u32[]{:S(2)}, u32[]{:S(2)}) collective-permute-start(bf16[96,1536]{1,0:T(8,128)(2,1)S(1)} %collective-permute-done.2.refs_1_), channel_id=1, source_target_pairs={{0,4},{4,8},{8,12},{12,14},{14,10},{10,6},{6,2},{2,0},{5,1},{9,5},... | collective-permute-start | bytes 884744 | tf_op jit(solution)/shard_map/ppermute | solution.py:206
  6.4 5.4 %collective-permute-start.7 = (bf16[56,1536]{1,0:T(8,128)(2,1)S(1)}, bf16[56,1536]{1,0:T(8,128)(2,1)S(1)}, u32[]{:S(2)}, u32[]{:S(2)}) collective-permute-start(bf16[56,1536]{1,0:T(8,128)(2,1)S(1)} %fetch.2.refs_1_.refs_0_), channel_id=1, source_target_pairs={{0,1},{1,0},{2,3},{3,2},{4,5},{5,4},{6,7},{7,6},{8,9},{9,8},{10,11... | collective-permute-start | bytes 516104 | tf_op jit(solution)/shard_map/ppermute | solution.py:207
  8.7 8.6 %collective-permute-start.1 = (bf16[152,1536]{1,0:T(8,128)(2,1)S(1)}, bf16[152,1536]{1,0:T(8,128)(2,1)S(1)}, u32[]{:S(2)}, u32[]{:S(2)}) collective-permute-start(bf16[152,1536]{1,0:T(8,128)(2,1)S(1)} %follow.2), channel_id=1, source_target_pairs={{0,4},{4,8},{8,12},{12,14},{14,10},{10,6},{6,2},{2,0},{5,1},{9,5},... | collective-permute-start | bytes 1400840 | tf_op jit(solution)/shard_map/ppermute | solution.py:206
  11.8 10.5 %collective-permute-start.8 = (bf16[152,1536]{1,0:T(8,128)(2,1)S(1)}, bf16[152,1536]{1,0:T(8,128)(2,1)S(1)}, u32[]{:S(2)}, u32[]{:S(2)}) collective-permute-start(bf16[152,1536]{1,0:T(8,128)(2,1)S(1)} %follow.3), channel_id=1, source_target_pairs={{0,4},{4,8},{8,12},{12,14},{14,10},{10,6},{6,2},{2,0},{5,1},{9,5},... | collective-permute-start | bytes 1400840 | tf_op jit(solution)/shard_map/ppermute | solution.py:206
  19.8 22.9 %copy-start = (bf16[96,1536]{1,0:T(8,128)(2,1)S(1)}, bf16[96,1536]{1,0:T(8,128)(2,1)}, u32[]{:S(2)}) copy-start(bf16[96,1536]{1,0:T(8,128)(2,1)} %refs_0_.2) | copy-start | bytes 884740
  19.8 8.6 %collective-permute-start.10 = (bf16[152,1536]{1,0:T(8,128)(2,1)S(1)}, bf16[152,1536]{1,0:T(8,128)(2,1)S(1)}, u32[]{:S(2)}, u32[]{:S(2)}) collective-permute-start(bf16[152,1536]{1,0:T(8,128)(2,1)S(1)} %collective-permute-done.1.refs_6_.refs_2_), channel_id=1, source_target_pairs={{0,4},{4,8},{8,12},{12,14},{14,10},{10,6},{6,2},{2,0},{5,1},{9,5},... | collective-permute-start | bytes 1400840 | tf_op jit(solution)/shard_map/ppermute | solution.py:206
  22.3 11.1 %collective-permute-start.12 = (bf16[152,1536]{1,0:T(8,128)(2,1)S(1)}, bf16[152,1536]{1,0:T(8,128)(2,1)S(1)}, u32[]{:S(2)}, u32[]{:S(2)}) collective-permute-start(bf16[152,1536]{1,0:T(8,128)(2,1)S(1)} %collective-permute-done.8.refs_8_.refs_4_), channel_id=1, source_target_pairs={{0,4},{4,8},{8,12},{12,14},{14,10},{10,6},{6,2},{2,0},{5,1},{9,5},... | collective-permute-start | bytes 1400840 | tf_op jit(solution)/shard_map/ppermute | solution.py:206
  24.4 11.7 %collective-permute-start.6 = (bf16[152,1536]{1,0:T(8,128)(2,1)S(1)}, bf16[152,1536]{1,0:T(8,128)(2,1)S(1)}, u32[]{:S(2)}, u32[]{:S(2)}) collective-permute-start(bf16[152,1536]{1,0:T(8,128)(2,1)S(1)} %collective-permute-done.1.refs_6_.refs_2_), channel_id=1, source_target_pairs={{0,1},{1,0},{2,3},{3,2},{4,5},{5,4},{6,7},{7,6},{8,9},{9,8},{10,11... | collective-permute-start | bytes 1400840 | tf_op jit(solution)/shard_map/ppermute | solution.py:207
  24.4 11.2 %collective-permute-start.3 = (bf16[96,1536]{1,0:T(8,128)(2,1)S(1)}, bf16[96,1536]{1,0:T(8,128)(2,1)S(1)}, u32[]{:S(2)}, u32[]{:S(2)}) collective-permute-start(bf16[96,1536]{1,0:T(8,128)(2,1)S(1)} %collective-permute-done.refs_0_.refs_2_), channel_id=1, source_target_pairs={{0,1},{1,0},{2,3},{3,2},{4,5},{5,4},{6,7},{7,6},{8,9},{9,8},{10,11... | collective-permute-start | bytes 884744 | tf_op jit(solution)/shard_map/ppermute | solution.py:207
  24.9 10.7 %collective-permute-start.5 = (bf16[96,1536]{1,0:T(8,128)(2,1)S(1)}, bf16[96,1536]{1,0:T(8,128)(2,1)S(1)}, u32[]{:S(2)}, u32[]{:S(2)}) collective-permute-start(bf16[96,1536]{1,0:T(8,128)(2,1)S(1)} %collective-permute-done.4.refs_0_.refs_4_), channel_id=1, source_target_pairs={{0,1},{1,0},{2,3},{3,2},{4,5},{5,4},{6,7},{7,6},{8,9},{9,8},{10,11... | collective-permute-start | bytes 884744 | tf_op jit(solution)/shard_map/ppermute | solution.py:207
  28.4 8.4 %collective-permute-start.14 = (bf16[104,1536]{1,0:T(8,128)(2,1)S(1)}, bf16[104,1536]{1,0:T(8,128)(2,1)S(1)}, u32[]{:S(2)}, u32[]{:S(2)}) collective-permute-start(bf16[104,1536]{1,0:T(8,128)(2,1)S(1)} %opposite_p.2), channel_id=1, source_target_pairs={{0,4},{4,8},{8,12},{12,14},{14,10},{10,6},{6,2},{2,0},{5,1},{9,5},... | collective-permute-start | bytes 958472 | tf_op jit(solution)/shard_map/ppermute | solution.py:206
  33.4 7.0 %collective-permute-start.16 = (bf16[104,1536]{1,0:T(8,128)(2,1)S(1)}, bf16[104,1536]{1,0:T(8,128)(2,1)S(1)}, u32[]{:S(2)}, u32[]{:S(2)}) collective-permute-start(bf16[104,1536]{1,0:T(8,128)(2,1)S(1)} %opposite_p.3), channel_id=1, source_target_pairs={{0,4},{4,8},{8,12},{12,14},{14,10},{10,6},{6,2},{2,0},{5,1},{9,5},... | collective-permute-start | bytes 958472 | tf_op jit(solution)/shard_map/ppermute | solution.py:206
  35.6 4.9 %collective-permute-start.9 = (bf16[152,1536]{1,0:T(8,128)(2,1)S(1)}, bf16[152,1536]{1,0:T(8,128)(2,1)S(1)}, u32[]{:S(2)}, u32[]{:S(2)}) collective-permute-start(bf16[152,1536]{1,0:T(8,128)(2,1)S(1)} %collective-permute-done.8.refs_8_.refs_4_), channel_id=1, source_target_pairs={{0,1},{1,0},{2,3},{3,2},{4,5},{5,4},{6,7},{7,6},{8,9},{9,8},{10,11... | collective-permute-start | bytes 1400840 | tf_op jit(solution)/shard_map/ppermute | solution.py:207
  35.6 7.1 %collective-permute-start.11 = (bf16[152,1536]{1,0:T(8,128)(2,1)S(1)}, bf16[152,1536]{1,0:T(8,128)(2,1)S(1)}, u32[]{:S(2)}, u32[]{:S(2)}) collective-permute-start(bf16[152,1536]{1,0:T(8,128)(2,1)S(1)} %collective-permute-done.10.refs_0_.refs_1_.refs_10_.refs_6_), channel_id=1, source_target_pairs={{0,1},{1,0},{2,3},{3,2},{4,5},{5,4},{6,7},{7,6},{8,9},{9,8},{10,11... | collective-permute-start | bytes 1400840 | tf_op jit(solution)/shard_map/ppermute | solution.py:207
  36.1 6.6 %collective-permute-start.13 = (bf16[152,1536]{1,0:T(8,128)(2,1)S(1)}, bf16[152,1536]{1,0:T(8,128)(2,1)S(1)}, u32[]{:S(2)}, u32[]{:S(2)}) collective-permute-start(bf16[152,1536]{1,0:T(8,128)(2,1)S(1)} %collective-permute-done.12.refs_0_.refs_1_.refs_12_.refs_8_), channel_id=1, source_target_pairs={{0,1},{1,0},{2,3},{3,2},{4,5},{5,4},{6,7},{7,6},{8,9},{9,8},{10,11... | collective-permute-start | bytes 1400840 | tf_op jit(solution)/shard_map/ppermute | solution.py:207
  36.8 5.8 %collective-permute-start.15 = (bf16[104,1536]{1,0:T(8,128)(2,1)S(1)}, bf16[104,1536]{1,0:T(8,128)(2,1)S(1)}, u32[]{:S(2)}, u32[]{:S(2)}) collective-permute-start(bf16[104,1536]{1,0:T(8,128)(2,1)S(1)} %collective-permute-done.14.refs_14_.refs_0_.refs_10_), channel_id=1, source_target_pairs={{0,1},{1,0},{2,3},{3,2},{4,5},{5,4},{6,7},{7,6},{8,9},{9,8},{10,11... | collective-permute-start | bytes 958472 | tf_op jit(solution)/shard_map/ppermute | solution.py:207
  40.5 2.2 %collective-permute-start.17 = (bf16[104,1536]{1,0:T(8,128)(2,1)S(1)}, bf16[104,1536]{1,0:T(8,128)(2,1)S(1)}, u32[]{:S(2)}, u32[]{:S(2)}) collective-permute-start(bf16[104,1536]{1,0:T(8,128)(2,1)S(1)} %collective-permute-done.16.refs_16_.refs_1_.refs_12_), channel_id=1, source_target_pairs={{0,1},{1,0},{2,3},{3,2},{4,5},{5,4},{6,7},{7,6},{8,9},{9,8},{10,11... | collective-permute-start | bytes 958472 | tf_op jit(solution)/shard_map/ppermute | solution.py:207
  40.5 5.7 %collective-permute-start.18 = (bf16[64,1536]{1,0:T(8,128)(2,1)S(1)}, bf16[64,1536]{1,0:T(8,128)(2,1)S(1)}, u32[]{:S(2)}, u32[]{:S(2)}) collective-permute-start(bf16[64,1536]{1,0:T(8,128)(2,1)S(1)} %opposite_r.1), channel_id=1, source_target_pairs={{0,4},{4,8},{8,12},{12,14},{14,10},{10,6},{6,2},{2,0},{5,1},{9,5},... | collective-permute-start | bytes 589832 | tf_op jit(solution)/shard_map/ppermute | solution.py:206
  46.2 2.6 %collective-permute-start.19 = (bf16[64,1536]{1,0:T(8,128)(2,1)S(1)}, bf16[64,1536]{1,0:T(8,128)(2,1)S(1)}, u32[]{:S(2)}, u32[]{:S(2)}) collective-permute-start(bf16[64,1536]{1,0:T(8,128)(2,1)S(1)} %collective-permute-done.18.refs_14_.refs_15_), channel_id=1, source_target_pairs={{0,1},{1,0},{2,3},{3,2},{4,5},{5,4},{6,7},{7,6},{8,9},{9,8},{10,11... | collective-permute-start | bytes 589832 | tf_op jit(solution)/shard_map/ppermute | solution.py:207

commit v4 on v3

v4 whole, which is shorter than its diff:
```python
import functools
import math

import jax
import jax.numpy as jnp
from jax import lax
from jax.experimental import pallas as pl
from jax.experimental.pallas import tpu as pltpu
from jax.sharding import PartitionSpec as P

F32, BF16 = jnp.float32, jnp.bfloat16
ON_CHIP = pl.BlockSpec(memory_space=pltpu.VMEM)
IN_HBM = pl.BlockSpec(memory_space=pltpu.HBM)
PARAMS = pltpu.CompilerParams(vmem_limit_bytes=20 << 20)
CHUNKS = 4
WEIGHT = 20
MARK = 10_000_000_000


def shape(*dims):
    return jax.ShapeDtypeStruct(dims, BF16)


def cost(flops, nbytes):
    return pl.CostEstimate(flops=flops, bytes_accessed=nbytes, transcendentals=0)


def small(kernel, out_shape, operands, name):
    return pl.pallas_call(
        kernel,
        out_shape=out_shape,
        in_specs=[ON_CHIP] * len(operands),
        out_specs=jax.tree.map(lambda _: ON_CHIP, out_shape),
        compiler_params=PARAMS,
        name=name,
    )(*operands)


def in_hbm(x):
    return pltpu.with_memory_space_constraint(x, pltpu.HBM)


def after(value, *others):
    return lax.optimization_barrier((value, *others))[0]


def ring_of(chips):
    if chips > 8:
        return list(range(chips))
    return list(range(0, chips, 2)) + list(range(chips - 1, 0, -2))


def chip_at(distance, chips):
    chip = lax.axis_index("row") // 2
    if chips > 8:
        return lax.rem(chip + distance + chips, chips)
    place = jnp.where(lax.rem(chip, 2) == 0, chip // 2, chips - 1 - chip // 2)
    place = lax.rem(place + distance + chips, chips)
    return jnp.where(place < chips // 2, 2 * place, 2 * (chips - 1 - place) + 1)


def my_core():
    return lax.rem(lax.axis_index("row"), 2)


def owner_row(rows, chips, steps, stream, side):
    by = my_core() if side == 0 else 1 - my_core()
    chip = chip_at(jnp.where(by == 0, -steps, steps), chips)
    return (2 * chip + (by if stream == 0 else 1 - by)) * rows


def place(parts, rows, chips, zero, name):
    def kernel(*refs):
        out = refs[-1]
        for ref, (_, start, *origin) in zip(refs, parts):
            at = pl.multiple_of(owner_row(rows, chips, *origin), 8)
            out[pl.ds(at, rows), :] = ref[start : start + rows]
        if zero:
            at = pl.multiple_of(2 * chip_at(chips // 2, chips) * rows, 8)
            out[pl.ds(at, 2 * rows), :] = jnp.zeros((2 * rows, out.shape[1]), BF16)

    cols = parts[0][0].shape[1]
    return small(kernel, shape(2 * chips * rows, cols), [part[0] for part in parts], name)


def window_of(rows, chips):
    chunk, whole = 2 * rows, 2 * rows * chips
    size = min(-(-(chunk + 128 - math.gcd(chunk, 128)) // 128) * 128, whole)
    start = chip_at(chips // 2, chips) * chunk // 128 * 128
    return pl.multiple_of(jnp.minimum(start, whole - size), 128), size


def opposite(p_parts, p_rows, r_parts, r_rows, r_panel, chips):
    _, size = window_of(p_rows, chips)
    parts = p_parts + r_parts
    cols = r_panel.shape[1]

    def kernel(*refs):
        window, panel = refs[-2:]
        first, _ = window_of(p_rows, chips)
        window[...] = jnp.zeros_like(window)
        for i, (ref, (_, start, *origin)) in enumerate(zip(refs, parts)):
            rows, out = (p_rows, window) if i < len(p_parts) else (r_rows, panel)
            at = owner_row(rows, chips, *origin)
            at = at - first if i < len(p_parts) else at
            out[pl.ds(pl.multiple_of(at, 8), rows), :] = ref[start : start + rows]

    return pl.pallas_call(
        kernel,
        out_shape=(shape(size, cols), shape(*r_panel.shape)),
        in_specs=[ON_CHIP] * (len(parts) + 1),
        out_specs=(ON_CHIP, ON_CHIP),
        input_output_aliases={len(parts): 1},
        compiler_params=PARAMS,
        name="opposite",
    )(*[part[0] for part in parts], r_panel)


def load_kernel(inverse, panel, out, sems):
    rows = inverse.shape[0]
    copies = [
        pltpu.make_async_copy(inverse, out.at[pl.ds(0, rows)], sems.at[0]),
        pltpu.make_async_copy(panel, out.at[pl.ds(rows, panel.shape[0])], sems.at[1]),
    ]
    for copy in copies:
        copy.start()
    for copy in copies:
        copy.wait()


def load(inverse, panel):
    return pl.pallas_call(
        load_kernel,
        out_shape=shape(inverse.shape[0] + panel.shape[0], inverse.shape[1]),
        in_specs=[IN_HBM, IN_HBM],
        out_specs=ON_CHIP,
        scratch_shapes=[pltpu.SemaphoreType.DMA((2,))],
        compiler_params=PARAMS,
        name="load",
    )(in_hbm(inverse), in_hbm(panel))


def mark(piece):
    def kernel(piece_ref, out):
        out[...] = piece_ref[:16, :128]

    return pl.pallas_call(
        kernel,
        out_shape=shape(16, 128),
        in_specs=[ON_CHIP],
        out_specs=ON_CHIP,
        compiler_params=PARAMS,
        cost_estimate=cost(MARK, 0),
        name="mark",
    )(piece)


def lower_kernel(column, panel, out):
    rows = column.shape[0] // CHUNKS
    for i in range(CHUNKS):
        at = pl.ds(i * rows, rows)
        out[at] = jnp.dot(column[at], panel[...], preferred_element_type=F32)


def lower(column_block, panel):
    n, k = column_block.shape
    return pl.pallas_call(
        lower_kernel,
        out_shape=jax.ShapeDtypeStruct((n, panel.shape[1]), F32),
        in_specs=[ON_CHIP, ON_CHIP],
        out_specs=ON_CHIP,
        compiler_params=PARAMS,
        cost_estimate=cost(WEIGHT * 2 * n * k * k, 2 * (n * k + k * k + 2 * n * k)),
        name="lower",
    )(column_block, panel)


def finish_kernel(p_rows, chips, so_far, column, window, panel, coupling, lower_out, out, lower_done, done, sems):
    first, size = window_of(p_rows, chips)
    contract = (((1,), (1,)), ((), ()))
    rows = coupling.shape[0] // CHUNKS
    copies = []
    for i in range(CHUNKS):
        at = pl.ds(i * rows, rows)
        rest = jnp.dot(column[at, pl.ds(first, size)], window[...], preferred_element_type=F32)
        lower_done[at] = (so_far[at] + rest).astype(BF16)
        copies.append(pltpu.make_async_copy(lower_done.at[at], lower_out.at[at], sems.at[0, i]))
        copies[-1].start()
        product = lax.dot_general(lower_done[at], panel[...], contract, preferred_element_type=F32)
        done[at] = (coupling[at].astype(F32) - product).astype(BF16)
        copies.append(pltpu.make_async_copy(done.at[at], out.at[at], sems.at[1, i]))
        copies[-1].start()
    for copy in copies:
        copy.wait()


def finish(so_far, column_block, window, panel, coupling, p_rows, chips):
    n, cols = coupling.shape
    k = so_far.shape[1]
    return pl.pallas_call(
        functools.partial(finish_kernel, p_rows, chips),
        out_shape=(shape(n, k), shape(n, cols)),
        in_specs=[ON_CHIP] * 5,
        out_specs=(IN_HBM, IN_HBM),
        scratch_shapes=[
            pltpu.VMEM((n, k), BF16),
            pltpu.VMEM((n, cols), BF16),
            pltpu.SemaphoreType.DMA((2, CHUNKS)),
        ],
        compiler_params=PARAMS,
        cost_estimate=cost(2 * n * k * (cols + 256), 2 * (4 * n * k + k * cols + 2 * n * cols)),
        name="finish",
    )(so_far, column_block, window, panel, coupling)


def on_device(devices, coupling, column_block, pivot_inverse, row_panel):
    chips = devices // 2
    steps = chips // 2
    ring = ring_of(chips)
    swap = [(i, i ^ 1) for i in range(devices)]
    hops = [(ring[i], ring[(i + 1) % chips]) for i in range(chips)]
    along = [(2 * a, 2 * b) for a, b in hops] + [(2 * b + 1, 2 * a + 1) for a, b in hops]
    on = lambda x: lax.ppermute(x, "row", along)
    over = lambda x: lax.ppermute(x, "row", swap)
    p_rows, r_rows = pivot_inverse.shape[0], row_panel.shape[1]

    shards = load(pivot_inverse, row_panel.T)
    held = [shards, over(shards)]
    pieces = [(held[s], 0, s, 0) for s in range(2)]
    for k in range(1, steps):
        held = [on(x) for x in held]
        pieces += [(y, k, s, side) for s in range(2) for side, y in enumerate((held[s], over(held[s])))]
        held[1] = after(held[1], mark(held[0]))
    last = on(held[0])

    at = lambda start, some: [(x, start, *origin) for x, *origin in some]
    panel = place(at(0, pieces), p_rows, chips, True, "place_p")
    r_panel = place(at(p_rows, pieces), r_rows, chips, False, "place_r")
    so_far = lower(column_block, panel)
    parts = [(last, steps, 0, 0), (over(after(last, so_far)), steps, 0, 1)]
    p_parts, r_parts = at(0, parts), at(p_rows, parts)
    window, r_panel = opposite(p_parts, p_rows, r_parts, r_rows, r_panel, chips)
    return finish(so_far, column_block, window, r_panel, coupling, p_rows, chips)


def by_all_gather(coupling, column_block, pivot_inverse, row_panel):
    whole_inverse = lax.all_gather(pivot_inverse, "row", axis=0, tiled=True)
    whole_panel = lax.all_gather(row_panel, "row", axis=1, tiled=True)
    lower_panel = jnp.dot(column_block, whole_inverse, preferred_element_type=F32).astype(BF16)
    product = jnp.dot(lower_panel, whole_panel, preferred_element_type=F32)
    return lower_panel, (coupling.astype(F32) - product).astype(BF16)


def solution(mesh):
    devices = mesh.shape["row"]
    parts = mesh.shape["groups"]

    def step(coupling, column_block, pivot_inverse, row_panel):
        fits = devices % 4 == 0 and devices >= 12
        fits &= row_panel.shape[1] // (parts * devices) % 8 == 0
        fits &= pivot_inverse.shape[0] // (parts * devices) % 8 == 0
        body = functools.partial(on_device, devices) if fits else by_all_gather
        rows = P(("groups", "row"), None)
        return jax.shard_map(
            body,
            mesh=mesh,
            in_specs=(rows, rows, rows, P(None, ("groups", "row"))),
            out_specs=(rows, rows),
            check_vma=False,
        )(coupling, column_block, pivot_inverse, row_panel)

    return step
```

time: 53.6 us -> 52.1 us (0.972)
  waiting for transfers between devices: 18.1 us -> 23.6 us
  starting transfers between devices: 20.9 us -> 15.8 us
  Pallas kernels: 13.6 us -> 11.8 us
    ppermute x9 -> x7, starting transfers between devices: 19.2 us -> 14.8 us  [on_device(): on = lambda x: lax.ppermute(x, 'row', along)]
    ppermute x9 -> x7, waiting for transfers between devices: 18.1 us -> 22 us  [on_device(): on = lambda x: lax.ppermute(x, 'row', along)]
    ppermute x11 -> x8, waiting for transfers between devices: 0.03 us -> 1.62 us  [on_device(): over = lambda x: lax.ppermute(x, 'row', swap)]
    pallas_call x5 -> x4, Pallas kernels: 12.8 us -> 11.3 us  [the longest x1 5.1 us: finish(): pl.pallas_call(functools.partial(finish_kernel, p_rows, chips), out_shape...]
    ppermute x11 -> x8, starting transfers between devices: 1.69 us -> 1.04 us  [on_device(): over = lambda x: lax.ppermute(x, 'row', swap)]
  transfers between devices with their start and end apart: 20 -> 15, of which waited for: 9 -> 8; matrix products, arithmetic and copies ran while one was open for 0% -> 0% of each run, Pallas kernels for 17% -> 11%
where the time goes in v4:
time: 52.1 us; the launch traced here: 52 us
  waiting for transfers between devices  23.6 us (45%)
  starting transfers between devices  15.8 us (30%)
  Pallas kernels  11.8 us (23%)
  between operations  0.72 us (1%)
    ppermute x7, waiting for transfers between devices, on_device(): on = lambda x: lax.ppermute(x, 'row', along)  22 us
    ppermute x7, starting transfers between devices, on_device(): on = lambda x: lax.ppermute(x, 'row', along)  14.8 us
    pallas_call x1, Pallas kernels, finish(): pl.pallas_call(functools.partial(finish_kernel, p_rows, chips), out_shape...  5.1 us
    pallas_call x1, Pallas kernels, lower(): pl.pallas_call(lower_kernel, out_shape=jax.ShapeDtypeStruct((n, panel.sha...  5.03 us
    ppermute x8, waiting for transfers between devices, on_device(): over = lambda x: lax.ppermute(x, 'row', swap)  1.62 us
    ppermute x8, starting transfers between devices, on_device(): over = lambda x: lax.ppermute(x, 'row', swap)  1.04 us
  transfers between devices with their start and end apart: 15, of which 8 were waited for; matrix products, arithmetic and copies ran while one was open for 0% of the time, Pallas kernels for 11%

profile of v4, /device:TPU:0, one launch (start us, length us, event | category | flops | bytes accessed | tf_op | source)
XLA Modules:
  0.0 52.0 jit_solution(1712614613723182620)
XLA Ops:
  0.6 1.0 %load.1.refs_0_ = bf16[152,1536]{1,0:T(8,128)(2,1)S(1)} custom-call(bf16[96,1536]{1,0:T(8,128)(2,1)} %inverse.1, bf16[56,1536]{1,0:T(8,128)(2,1)} %bitcast.1), custom_call_target="tpu_custom_call" | custom-call | tf_op jit(solution)/shard_map/load/pallas_call | solution.py:132
  1.7 0.0 copy-start
  1.7 0.5 collective-permute-start
  2.2 2.6 %collective-permute-start.1 = (bf16[152,1536]{1,0:T(8,128)(2,1)S(1)}, bf16[152,1536]{1,0:T(8,128)(2,1)S(1)}, u32[]{:S(2)}, u32[]{:S(2)}) collective-permute-start(bf16[152,1536]{1,0:T(8,128)(2,1)S(1)} %load.1.refs_0_), channel_id=1, source_target_pairs={{0,4},{4,8},{8,12},{12,14},{14,10},{10,6},{6,2},{2,0},{5,1},{9,5},... | collective-permute-start | bytes 1400840 | tf_op jit(solution)/shard_map/ppermute | solution.py:223
  4.8 0.0 collective-permute-done.refs_1_
  4.8 1.8 %collective-permute-start.3 = (bf16[152,1536]{1,0:T(8,128)(2,1)S(1)}, bf16[152,1536]{1,0:T(8,128)(2,1)S(1)}, u32[]{:S(2)}, u32[]{:S(2)}) collective-permute-start(bf16[152,1536]{1,0:T(8,128)(2,1)S(1)} %collective-permute-done.refs_1_), channel_id=1, source_target_pairs={{0,4},{4,8},{8,12},{12,14},{14,10},{10,6},{6,2},{2,0},{5,1},{9,5},... | collective-permute-start | bytes 1400840 | tf_op jit(solution)/shard_map/ppermute | solution.py:223
  6.6 4.7 %collective-permute-done.1.refs_2_ = bf16[152,1536]{1,0:T(8,128)(2,1)S(1)} collective-permute-done((bf16[152,1536]{1,0:T(8,128)(2,1)S(1)}, bf16[152,1536]{1,0:T(8,128)(2,1)S(1)}, u32[]{:S(2)}, u32[]{:S(2)}) %collective-permute-start.1) | collective-permute-done | bytes 466976 | tf_op jit(solution)/shard_map/ppermute | solution.py:223
  11.3 2.1 %collective-permute-start.5 = (bf16[152,1536]{1,0:T(8,128)(2,1)S(1)}, bf16[152,1536]{1,0:T(8,128)(2,1)S(1)}, u32[]{:S(2)}, u32[]{:S(2)}) collective-permute-start(bf16[152,1536]{1,0:T(8,128)(2,1)S(1)} %collective-permute-done.1.refs_2_), channel_id=1, source_target_pairs={{0,4},{4,8},{8,12},{12,14},{14,10},{10,6},{6,2},{2,0},{5,1},{9,5},... | collective-permute-start | bytes 1400840 | tf_op jit(solution)/shard_map/ppermute | solution.py:223
  13.4 2.9 %collective-permute-done.3.refs_4_ = bf16[152,1536]{1,0:T(8,128)(2,1)S(1)} collective-permute-done((bf16[152,1536]{1,0:T(8,128)(2,1)S(1)}, bf16[152,1536]{1,0:T(8,128)(2,1)S(1)}, u32[]{:S(2)}, u32[]{:S(2)}) %collective-permute-start.3) | collective-permute-done | bytes 466976 | tf_op jit(solution)/shard_map/ppermute | solution.py:223
  16.3 2.1 %collective-permute-start.7 = (bf16[152,1536]{1,0:T(8,128)(2,1)S(1)}, bf16[152,1536]{1,0:T(8,128)(2,1)S(1)}, u32[]{:S(2)}, u32[]{:S(2)}) collective-permute-start(bf16[152,1536]{1,0:T(8,128)(2,1)S(1)} %collective-permute-done.3.refs_4_), channel_id=1, source_target_pairs={{0,4},{4,8},{8,12},{12,14},{14,10},{10,6},{6,2},{2,0},{5,1},{9,5},... | collective-permute-start | bytes 1400840 | tf_op jit(solution)/shard_map/ppermute | solution.py:223
  18.4 2.9 %collective-permute-done.5.refs_6_ = bf16[152,1536]{1,0:T(8,128)(2,1)S(1)} collective-permute-done((bf16[152,1536]{1,0:T(8,128)(2,1)S(1)}, bf16[152,1536]{1,0:T(8,128)(2,1)S(1)}, u32[]{:S(2)}, u32[]{:S(2)}) %collective-permute-start.5) | collective-permute-done | bytes 466976 | tf_op jit(solution)/shard_map/ppermute | solution.py:223
  21.3 2.1 %collective-permute-start.9 = (bf16[152,1536]{1,0:T(8,128)(2,1)S(1)}, bf16[152,1536]{1,0:T(8,128)(2,1)S(1)}, u32[]{:S(2)}, u32[]{:S(2)}) collective-permute-start(bf16[152,1536]{1,0:T(8,128)(2,1)S(1)} %collective-permute-done.5.refs_6_), channel_id=1, source_target_pairs={{0,4},{4,8},{8,12},{12,14},{14,10},{10,6},{6,2},{2,0},{5,1},{9,5},... | collective-permute-start | bytes 1400840 | tf_op jit(solution)/shard_map/ppermute | solution.py:223
  23.4 2.9 %collective-permute-done.7.refs_8_ = bf16[152,1536]{1,0:T(8,128)(2,1)S(1)} collective-permute-done((bf16[152,1536]{1,0:T(8,128)(2,1)S(1)}, bf16[152,1536]{1,0:T(8,128)(2,1)S(1)}, u32[]{:S(2)}, u32[]{:S(2)}) %collective-permute-start.7) | collective-permute-done | bytes 466976 | tf_op jit(solution)/shard_map/ppermute | solution.py:223
  26.3 2.1 %collective-permute-start.11 = (bf16[152,1536]{1,0:T(8,128)(2,1)S(1)}, bf16[152,1536]{1,0:T(8,128)(2,1)S(1)}, u32[]{:S(2)}, u32[]{:S(2)}) collective-permute-start(bf16[152,1536]{1,0:T(8,128)(2,1)S(1)} %collective-permute-done.7.refs_8_), channel_id=1, source_target_pairs={{0,4},{4,8},{8,12},{12,14},{14,10},{10,6},{6,2},{2,0},{5,1},{9,5},... | collective-permute-start | bytes 1400840 | tf_op jit(solution)/shard_map/ppermute | solution.py:223
  28.4 0.0 collective-permute-start.6
  28.4 0.5 collective-permute-start.4
  28.9 0.0 collective-permute-done.2.refs_3_
  28.9 0.0 collective-permute-start.8
  28.9 2.4 %collective-permute-done.9.refs_10_ = bf16[152,1536]{1,0:T(8,128)(2,1)S(1)} collective-permute-done((bf16[152,1536]{1,0:T(8,128)(2,1)S(1)}, bf16[152,1536]{1,0:T(8,128)(2,1)S(1)}, u32[]{:S(2)}, u32[]{:S(2)}) %collective-permute-start.9) | collective-permute-done | bytes 466976 | tf_op jit(solution)/shard_map/ppermute | solution.py:223
  31.3 5.0 %collective-permute-done.11.refs_12_ = bf16[152,1536]{1,0:T(8,128)(2,1)S(1)} collective-permute-done((bf16[152,1536]{1,0:T(8,128)(2,1)S(1)}, bf16[152,1536]{1,0:T(8,128)(2,1)S(1)}, u32[]{:S(2)}, u32[]{:S(2)}) %collective-permute-start.11) | collective-permute-done | bytes 466976 | tf_op jit(solution)/shard_map/ppermute | solution.py:223
  36.3 0.0 collective-permute-start.12
  36.3 0.0 collective-permute-done.6.refs_7_
  36.3 2.1 %collective-permute-start.13 = (bf16[152,1536]{1,0:T(8,128)(2,1)S(1)}, bf16[152,1536]{1,0:T(8,128)(2,1)S(1)}, u32[]{:S(2)}, u32[]{:S(2)}) collective-permute-start(bf16[152,1536]{1,0:T(8,128)(2,1)S(1)} %collective-permute-done.9.refs_10_), channel_id=1, source_target_pairs={{0,4},{4,8},{8,12},{12,14},{14,10},{10,6},{6,2},{2,0},{5,1},{9,5},... | collective-permute-start | bytes 1400840 | tf_op jit(solution)/shard_map/ppermute | solution.py:223
  38.4 0.0 collective-permute-done.4.refs_5_
  38.4 0.3 place_p.1.panel
  38.8 5.0 %lower.1.so_far = f32[1024,1536]{1,0:T(8,128)S(1)} custom-call(bf16[1024,1536]{1,0:T(8,128)(2,1)S(1)} %copy-done, bf16[1536,1536]{1,0:T(8,128)(2,1)S(1)} %place_p.1.panel), custom_call_target="tpu_custom_call" | custom-call | flops 96636764160 | bytes 14155776 | tf_op jit(solution)/shard_map/lower/pallas_call | solution.py:167
  43.8 1.1 %collective-permute-done.13.refs_0_.refs_2_ = bf16[152,1536]{1,0:T(8,128)(2,1)S(1)} collective-permute-done((bf16[152,1536]{1,0:T(8,128)(2,1)S(1)}, bf16[152,1536]{1,0:T(8,128)(2,1)S(1)}, u32[]{:S(2)}, u32[]{:S(2)}) %collective-permute-start.13) | collective-permute-done | bytes 466976 | tf_op jit(solution)/shard_map/ppermute | solution.py:223
  44.9 0.2 place_r.1.refs_4_
  45.1 0.0 copy-start.1
  45.1 1.6 %collective-permute-done.14.refs_1_.refs_3_ = bf16[152,1536]{1,0:T(8,128)(2,1)S(1)} collective-permute-done((bf16[152,1536]{1,0:T(8,128)(2,1)S(1)}, bf16[152,1536]{1,0:T(8,128)(2,1)S(1)}, u32[]{:S(2)}, u32[]{:S(2)}) %collective-permute-start.14) | collective-permute-done | bytes 466976 | tf_op jit(solution)/shard_map/ppermute | solution.py:224
  46.7 0.1 opposite.1
  46.9 5.1 %finish.1 = (bf16[1024,1536]{1,0:T(8,128)(2,1)}, bf16[1024,896]{1,0:T(8,128)(2,1)}) custom-call(f32[1024,1536]{1,0:T(8,128)S(1)} %lower.1.so_far, bf16[1024,1536]{1,0:T(8,128)(2,1)S(1)} %copy-done, bf16[256,1536]{1,0:T(8,128)(2,1)S(1)} %get-tuple-element.6.window, bf16[896,1536]{1,0:T(8,128)(2,1)S(1)} %get-tuple-element.7.panel, bf16[1024,896]{1,0:T(8,128)(2,1)S(1)} %copy-done.1), custom_call_target="tpu_custom_call" | custom-call | flops 3623878656 | bytes 19005440 | tf_op jit(solution)/shard_map/finish/pallas_call | solution.py:200
  (8 shorter events, 0.0 us)
Async XLA Ops:
  1.7 37.1 %copy-start = (bf16[1024,1536]{1,0:T(8,128)(2,1)S(1)}, bf16[1024,1536]{1,0:T(8,128)(2,1)}, u32[]{:S(2)}) copy-start(bf16[1024,1536]{1,0:T(8,128)(2,1)} %column.3) | copy-start | bytes 9437188
  1.7 3.2 %collective-permute-start = (bf16[152,1536]{1,0:T(8,128)(2,1)S(1)}, bf16[152,1536]{1,0:T(8,128)(2,1)S(1)}, u32[]{:S(2)}, u32[]{:S(2)}) collective-permute-start(bf16[152,1536]{1,0:T(8,128)(2,1)S(1)} %load.1.refs_0_), channel_id=1, source_target_pairs={{0,1},{1,0},{2,3},{3,2},{4,5},{5,4},{6,7},{7,6},{8,9},{9,8},{10,11... | collective-permute-start | bytes 1400840 | tf_op jit(solution)/shard_map/ppermute | solution.py:224
  2.2 9.1 %collective-permute-start.1 = (bf16[152,1536]{1,0:T(8,128)(2,1)S(1)}, bf16[152,1536]{1,0:T(8,128)(2,1)S(1)}, u32[]{:S(2)}, u32[]{:S(2)}) collective-permute-start(bf16[152,1536]{1,0:T(8,128)(2,1)S(1)} %load.1.refs_0_), channel_id=1, source_target_pairs={{0,4},{4,8},{8,12},{12,14},{14,10},{10,6},{6,2},{2,0},{5,1},{9,5},... | collective-permute-start | bytes 1400840 | tf_op jit(solution)/shard_map/ppermute | solution.py:223
  4.8 11.5 %collective-permute-start.3 = (bf16[152,1536]{1,0:T(8,128)(2,1)S(1)}, bf16[152,1536]{1,0:T(8,128)(2,1)S(1)}, u32[]{:S(2)}, u32[]{:S(2)}) collective-permute-start(bf16[152,1536]{1,0:T(8,128)(2,1)S(1)} %collective-permute-done.refs_1_), channel_id=1, source_target_pairs={{0,4},{4,8},{8,12},{12,14},{14,10},{10,6},{6,2},{2,0},{5,1},{9,5},... | collective-permute-start | bytes 1400840 | tf_op jit(solution)/shard_map/ppermute | solution.py:223
  11.3 10.0 %collective-permute-start.5 = (bf16[152,1536]{1,0:T(8,128)(2,1)S(1)}, bf16[152,1536]{1,0:T(8,128)(2,1)S(1)}, u32[]{:S(2)}, u32[]{:S(2)}) collective-permute-start(bf16[152,1536]{1,0:T(8,128)(2,1)S(1)} %collective-permute-done.1.refs_2_), channel_id=1, source_target_pairs={{0,4},{4,8},{8,12},{12,14},{14,10},{10,6},{6,2},{2,0},{5,1},{9,5},... | collective-permute-start | bytes 1400840 | tf_op jit(solution)/shard_map/ppermute | solution.py:223
  16.3 10.0 %collective-permute-start.7 = (bf16[152,1536]{1,0:T(8,128)(2,1)S(1)}, bf16[152,1536]{1,0:T(8,128)(2,1)S(1)}, u32[]{:S(2)}, u32[]{:S(2)}) collective-permute-start(bf16[152,1536]{1,0:T(8,128)(2,1)S(1)} %collective-permute-done.3.refs_4_), channel_id=1, source_target_pairs={{0,4},{4,8},{8,12},{12,14},{14,10},{10,6},{6,2},{2,0},{5,1},{9,5},... | collective-permute-start | bytes 1400840 | tf_op jit(solution)/shard_map/ppermute | solution.py:223
  18.4 10.5 %collective-permute-start.2 = (bf16[152,1536]{1,0:T(8,128)(2,1)S(1)}, bf16[152,1536]{1,0:T(8,128)(2,1)S(1)}, u32[]{:S(2)}, u32[]{:S(2)}) collective-permute-start(bf16[152,1536]{1,0:T(8,128)(2,1)S(1)} %collective-permute-done.1.refs_2_), channel_id=1, source_target_pairs={{0,1},{1,0},{2,3},{3,2},{4,5},{5,4},{6,7},{7,6},{8,9},{9,8},{10,11... | collective-permute-start | bytes 1400840 | tf_op jit(solution)/shard_map/ppermute | solution.py:224
  21.3 10.0 %collective-permute-start.9 = (bf16[152,1536]{1,0:T(8,128)(2,1)S(1)}, bf16[152,1536]{1,0:T(8,128)(2,1)S(1)}, u32[]{:S(2)}, u32[]{:S(2)}) collective-permute-start(bf16[152,1536]{1,0:T(8,128)(2,1)S(1)} %collective-permute-done.5.refs_6_), channel_id=1, source_target_pairs={{0,4},{4,8},{8,12},{12,14},{14,10},{10,6},{6,2},{2,0},{5,1},{9,5},... | collective-permute-start | bytes 1400840 | tf_op jit(solution)/shard_map/ppermute | solution.py:223
  26.3 10.0 %collective-permute-start.11 = (bf16[152,1536]{1,0:T(8,128)(2,1)S(1)}, bf16[152,1536]{1,0:T(8,128)(2,1)S(1)}, u32[]{:S(2)}, u32[]{:S(2)}) collective-permute-start(bf16[152,1536]{1,0:T(8,128)(2,1)S(1)} %collective-permute-done.7.refs_8_), channel_id=1, source_target_pairs={{0,4},{4,8},{8,12},{12,14},{14,10},{10,6},{6,2},{2,0},{5,1},{9,5},... | collective-permute-start | bytes 1400840 | tf_op jit(solution)/shard_map/ppermute | solution.py:223
  28.4 7.9 %collective-permute-start.6 = (bf16[152,1536]{1,0:T(8,128)(2,1)S(1)}, bf16[152,1536]{1,0:T(8,128)(2,1)S(1)}, u32[]{:S(2)}, u32[]{:S(2)}) collective-permute-start(bf16[152,1536]{1,0:T(8,128)(2,1)S(1)} %collective-permute-done.5.refs_6_), channel_id=1, source_target_pairs={{0,1},{1,0},{2,3},{3,2},{4,5},{5,4},{6,7},{7,6},{8,9},{9,8},{10,11... | collective-permute-start | bytes 1400840 | tf_op jit(solution)/shard_map/ppermute | solution.py:224
  28.4 10.0 %collective-permute-start.4 = (bf16[152,1536]{1,0:T(8,128)(2,1)S(1)}, bf16[152,1536]{1,0:T(8,128)(2,1)S(1)}, u32[]{:S(2)}, u32[]{:S(2)}) collective-permute-start(bf16[152,1536]{1,0:T(8,128)(2,1)S(1)} %collective-permute-done.3.refs_4_), channel_id=1, source_target_pairs={{0,1},{1,0},{2,3},{3,2},{4,5},{5,4},{6,7},{7,6},{8,9},{9,8},{10,11... | collective-permute-start | bytes 1400840 | tf_op jit(solution)/shard_map/ppermute | solution.py:224
  28.9 9.5 %collective-permute-start.8 = (bf16[152,1536]{1,0:T(8,128)(2,1)S(1)}, bf16[152,1536]{1,0:T(8,128)(2,1)S(1)}, u32[]{:S(2)}, u32[]{:S(2)}) collective-permute-start(bf16[152,1536]{1,0:T(8,128)(2,1)S(1)} %collective-permute-done.7.refs_8_), channel_id=1, source_target_pairs={{0,1},{1,0},{2,3},{3,2},{4,5},{5,4},{6,7},{7,6},{8,9},{9,8},{10,11... | collective-permute-start | bytes 1400840 | tf_op jit(solution)/shard_map/ppermute | solution.py:224
  31.3 7.1 %collective-permute-start.10 = (bf16[152,1536]{1,0:T(8,128)(2,1)S(1)}, bf16[152,1536]{1,0:T(8,128)(2,1)S(1)}, u32[]{:S(2)}, u32[]{:S(2)}) collective-permute-start(bf16[152,1536]{1,0:T(8,128)(2,1)S(1)} %collective-permute-done.9.refs_10_), channel_id=1, source_target_pairs={{0,1},{1,0},{2,3},{3,2},{4,5},{5,4},{6,7},{7,6},{8,9},{9,8},{10,11... | collective-permute-start | bytes 1400840 | tf_op jit(solution)/shard_map/ppermute | solution.py:224
  36.3 2.1 %collective-permute-start.12 = (bf16[152,1536]{1,0:T(8,128)(2,1)S(1)}, bf16[152,1536]{1,0:T(8,128)(2,1)S(1)}, u32[]{:S(2)}, u32[]{:S(2)}) collective-permute-start(bf16[152,1536]{1,0:T(8,128)(2,1)S(1)} %collective-permute-done.11.refs_12_), channel_id=1, source_target_pairs={{0,1},{1,0},{2,3},{3,2},{4,5},{5,4},{6,7},{7,6},{8,9},{9,8},{10,11... | collective-permute-start | bytes 1400840 | tf_op jit(solution)/shard_map/ppermute | solution.py:224
  36.3 8.6 %collective-permute-start.13 = (bf16[152,1536]{1,0:T(8,128)(2,1)S(1)}, bf16[152,1536]{1,0:T(8,128)(2,1)S(1)}, u32[]{:S(2)}, u32[]{:S(2)}) collective-permute-start(bf16[152,1536]{1,0:T(8,128)(2,1)S(1)} %collective-permute-done.9.refs_10_), channel_id=1, source_target_pairs={{0,4},{4,8},{8,12},{12,14},{14,10},{10,6},{6,2},{2,0},{5,1},{9,5},... | collective-permute-start | bytes 1400840 | tf_op jit(solution)/shard_map/ppermute | solution.py:223
  44.9 1.8 %collective-permute-start.14 = (bf16[152,1536]{1,0:T(8,128)(2,1)S(1)}, bf16[152,1536]{1,0:T(8,128)(2,1)S(1)}, u32[]{:S(2)}, u32[]{:S(2)}) collective-permute-start(bf16[152,1536]{1,0:T(8,128)(2,1)S(1)} %collective-permute-done.13.refs_0_.refs_2_), channel_id=1, source_target_pairs={{0,1},{1,0},{2,3},{3,2},{4,5},{5,4},{6,7},{7,6},{8,9},{9,8},{10,11... | collective-permute-start | bytes 1400840 | tf_op jit(solution)/shard_map/ppermute | solution.py:224
  45.1 1.8 %copy-start.1 = (bf16[1024,896]{1,0:T(8,128)(2,1)S(1)}, bf16[1024,896]{1,0:T(8,128)(2,1)}, u32[]{:S(2)}) copy-start(bf16[1024,896]{1,0:T(8,128)(2,1)} %coupling.1) | copy-start | bytes 5505028

commit v5 on v4

--- a/solution.py
+++ b/solution.py
@@ -186,10 +186,16 @@
         lower_done[at] = (so_far[at] + rest).astype(BF16)
         copies.append(pltpu.make_async_copy(lower_done.at[at], lower_out.at[at], sems.at[0, i]))
         copies[-1].start()
-        product = lax.dot_general(lower_done[at], panel[...], contract, preferred_element_type=F32)
-        done[at] = (coupling[at].astype(F32) - product).astype(BF16)
-        copies.append(pltpu.make_async_copy(done.at[at], out.at[at], sems.at[1, i]))
-        copies[-1].start()
+        cols = out.shape[1]
+        cuts = [0, (cols // 2 + 127) // 256 * 256, cols] if i == CHUNKS - 1 else [0, cols]
+        for j, (low, high) in enumerate(zip(cuts, cuts[1:])):
+            product = lax.dot_general(lower_done[at], panel[low:high], contract, preferred_element_type=F32)
+            done[at, low:high] = (coupling[at, low:high].astype(F32) - product).astype(BF16)
+            columns = pl.ds(low, high - low)
+            copies.append(
+                pltpu.make_async_copy(done.at[at, columns], out.at[at, columns], sems.at[1 + j, i])
+            )
+            copies[-1].start()
     for copy in copies:
         copy.wait()
 
@@ -205,7 +211,7 @@
         scratch_shapes=[
             pltpu.VMEM((n, k), BF16),
             pltpu.VMEM((n, cols), BF16),
-            pltpu.SemaphoreType.DMA((2, CHUNKS)),
+            pltpu.SemaphoreType.DMA((3, CHUNKS)),
         ],
         compiler_params=PARAMS,
         cost_estimate=cost(2 * n * k * (cols + 256), 2 * (4 * n * k + k * cols + 2 * n * cols)),

time: 52.1 us -> 52.1 us (level)
  no operation moved by 1% of the time
where the time goes in v5:
time: 52.1 us; the launch traced here: 51.9 us
  waiting for transfers between devices  23.6 us (45%)
  starting transfers between devices  15.8 us (30%)
  Pallas kernels  11.8 us (23%)
  between operations  0.72 us (1%)
    ppermute x7, waiting for transfers between devices, on_device(): on = lambda x: lax.ppermute(x, 'row', along)  22 us
    ppermute x7, starting transfers between devices, on_device(): on = lambda x: lax.ppermute(x, 'row', along)  14.8 us
    pallas_call x1, Pallas kernels, finish(): pl.pallas_call(functools.partial(finish_kernel, p_rows, chips), out_shape...  5.04 us
    pallas_call x1, Pallas kernels, lower(): pl.pallas_call(lower_kernel, out_shape=jax.ShapeDtypeStruct((n, panel.sha...  5.03 us
    ppermute x8, waiting for transfers between devices, on_device(): over = lambda x: lax.ppermute(x, 'row', swap)  1.62 us
    ppermute x8, starting transfers between devices, on_device(): over = lambda x: lax.ppermute(x, 'row', swap)  1.04 us
  transfers between devices with their start and end apart: 15, of which 8 were waited for; matrix products, arithmetic and copies ran while one was open for 0% of the time, Pallas kernels for 11%

profile of v5, /device:TPU:0, one launch (start us, length us, event | category | flops | bytes accessed | tf_op | source)
XLA Modules:
  0.0 51.9 jit_solution(18237610237281656889)
XLA Ops:
  0.6 1.0 %load.1.refs_0_ = bf16[152,1536]{1,0:T(8,128)(2,1)S(1)} custom-call(bf16[96,1536]{1,0:T(8,128)(2,1)} %inverse.1, bf16[56,1536]{1,0:T(8,128)(2,1)} %bitcast.1), custom_call_target="tpu_custom_call" | custom-call | tf_op jit(solution)/shard_map/load/pallas_call | solution.py:132
  1.7 0.0 copy-start
  1.7 0.5 collective-permute-start
  2.2 2.6 %collective-permute-start.1 = (bf16[152,1536]{1,0:T(8,128)(2,1)S(1)}, bf16[152,1536]{1,0:T(8,128)(2,1)S(1)}, u32[]{:S(2)}, u32[]{:S(2)}) collective-permute-start(bf16[152,1536]{1,0:T(8,128)(2,1)S(1)} %load.1.refs_0_), channel_id=1, source_target_pairs={{0,4},{4,8},{8,12},{12,14},{14,10},{10,6},{6,2},{2,0},{5,1},{9,5},... | collective-permute-start | bytes 1400840 | tf_op jit(solution)/shard_map/ppermute | solution.py:229
  4.8 0.0 collective-permute-done.refs_1_
  4.8 1.8 %collective-permute-start.3 = (bf16[152,1536]{1,0:T(8,128)(2,1)S(1)}, bf16[152,1536]{1,0:T(8,128)(2,1)S(1)}, u32[]{:S(2)}, u32[]{:S(2)}) collective-permute-start(bf16[152,1536]{1,0:T(8,128)(2,1)S(1)} %collective-permute-done.refs_1_), channel_id=1, source_target_pairs={{0,4},{4,8},{8,12},{12,14},{14,10},{10,6},{6,2},{2,0},{5,1},{9,5},... | collective-permute-start | bytes 1400840 | tf_op jit(solution)/shard_map/ppermute | solution.py:229
  6.6 4.7 %collective-permute-done.1.refs_2_ = bf16[152,1536]{1,0:T(8,128)(2,1)S(1)} collective-permute-done((bf16[152,1536]{1,0:T(8,128)(2,1)S(1)}, bf16[152,1536]{1,0:T(8,128)(2,1)S(1)}, u32[]{:S(2)}, u32[]{:S(2)}) %collective-permute-start.1) | collective-permute-done | bytes 466976 | tf_op jit(solution)/shard_map/ppermute | solution.py:229
  11.3 2.1 %collective-permute-start.5 = (bf16[152,1536]{1,0:T(8,128)(2,1)S(1)}, bf16[152,1536]{1,0:T(8,128)(2,1)S(1)}, u32[]{:S(2)}, u32[]{:S(2)}) collective-permute-start(bf16[152,1536]{1,0:T(8,128)(2,1)S(1)} %collective-permute-done.1.refs_2_), channel_id=1, source_target_pairs={{0,4},{4,8},{8,12},{12,14},{14,10},{10,6},{6,2},{2,0},{5,1},{9,5},... | collective-permute-start | bytes 1400840 | tf_op jit(solution)/shard_map/ppermute | solution.py:229
  13.4 2.9 %collective-permute-done.3.refs_4_ = bf16[152,1536]{1,0:T(8,128)(2,1)S(1)} collective-permute-done((bf16[152,1536]{1,0:T(8,128)(2,1)S(1)}, bf16[152,1536]{1,0:T(8,128)(2,1)S(1)}, u32[]{:S(2)}, u32[]{:S(2)}) %collective-permute-start.3) | collective-permute-done | bytes 466976 | tf_op jit(solution)/shard_map/ppermute | solution.py:229
  16.3 2.1 %collective-permute-start.7 = (bf16[152,1536]{1,0:T(8,128)(2,1)S(1)}, bf16[152,1536]{1,0:T(8,128)(2,1)S(1)}, u32[]{:S(2)}, u32[]{:S(2)}) collective-permute-start(bf16[152,1536]{1,0:T(8,128)(2,1)S(1)} %collective-permute-done.3.refs_4_), channel_id=1, source_target_pairs={{0,4},{4,8},{8,12},{12,14},{14,10},{10,6},{6,2},{2,0},{5,1},{9,5},... | collective-permute-start | bytes 1400840 | tf_op jit(solution)/shard_map/ppermute | solution.py:229
  18.4 2.9 %collective-permute-done.5.refs_6_ = bf16[152,1536]{1,0:T(8,128)(2,1)S(1)} collective-permute-done((bf16[152,1536]{1,0:T(8,128)(2,1)S(1)}, bf16[152,1536]{1,0:T(8,128)(2,1)S(1)}, u32[]{:S(2)}, u32[]{:S(2)}) %collective-permute-start.5) | collective-permute-done | bytes 466976 | tf_op jit(solution)/shard_map/ppermute | solution.py:229
  21.3 2.1 %collective-permute-start.9 = (bf16[152,1536]{1,0:T(8,128)(2,1)S(1)}, bf16[152,1536]{1,0:T(8,128)(2,1)S(1)}, u32[]{:S(2)}, u32[]{:S(2)}) collective-permute-start(bf16[152,1536]{1,0:T(8,128)(2,1)S(1)} %collective-permute-done.5.refs_6_), channel_id=1, source_target_pairs={{0,4},{4,8},{8,12},{12,14},{14,10},{10,6},{6,2},{2,0},{5,1},{9,5},... | collective-permute-start | bytes 1400840 | tf_op jit(solution)/shard_map/ppermute | solution.py:229
  23.4 2.9 %collective-permute-done.7.refs_8_ = bf16[152,1536]{1,0:T(8,128)(2,1)S(1)} collective-permute-done((bf16[152,1536]{1,0:T(8,128)(2,1)S(1)}, bf16[152,1536]{1,0:T(8,128)(2,1)S(1)}, u32[]{:S(2)}, u32[]{:S(2)}) %collective-permute-start.7) | collective-permute-done | bytes 466976 | tf_op jit(solution)/shard_map/ppermute | solution.py:229
  26.3 2.1 %collective-permute-start.11 = (bf16[152,1536]{1,0:T(8,128)(2,1)S(1)}, bf16[152,1536]{1,0:T(8,128)(2,1)S(1)}, u32[]{:S(2)}, u32[]{:S(2)}) collective-permute-start(bf16[152,1536]{1,0:T(8,128)(2,1)S(1)} %collective-permute-done.7.refs_8_), channel_id=1, source_target_pairs={{0,4},{4,8},{8,12},{12,14},{14,10},{10,6},{6,2},{2,0},{5,1},{9,5},... | collective-permute-start | bytes 1400840 | tf_op jit(solution)/shard_map/ppermute | solution.py:229
  28.4 0.0 collective-permute-start.6
  28.4 0.5 collective-permute-start.4
  28.9 0.0 collective-permute-done.2.refs_3_
  28.9 0.0 collective-permute-start.8
  28.9 2.4 %collective-permute-done.9.refs_10_ = bf16[152,1536]{1,0:T(8,128)(2,1)S(1)} collective-permute-done((bf16[152,1536]{1,0:T(8,128)(2,1)S(1)}, bf16[152,1536]{1,0:T(8,128)(2,1)S(1)}, u32[]{:S(2)}, u32[]{:S(2)}) %collective-permute-start.9) | collective-permute-done | bytes 466976 | tf_op jit(solution)/shard_map/ppermute | solution.py:229
  31.3 5.0 %collective-permute-done.11.refs_12_ = bf16[152,1536]{1,0:T(8,128)(2,1)S(1)} collective-permute-done((bf16[152,1536]{1,0:T(8,128)(2,1)S(1)}, bf16[152,1536]{1,0:T(8,128)(2,1)S(1)}, u32[]{:S(2)}, u32[]{:S(2)}) %collective-permute-start.11) | collective-permute-done | bytes 466976 | tf_op jit(solution)/shard_map/ppermute | solution.py:229
  36.3 0.0 collective-permute-start.12
  36.3 0.0 collective-permute-done.6.refs_7_
  36.3 2.1 %collective-permute-start.13 = (bf16[152,1536]{1,0:T(8,128)(2,1)S(1)}, bf16[152,1536]{1,0:T(8,128)(2,1)S(1)}, u32[]{:S(2)}, u32[]{:S(2)}) collective-permute-start(bf16[152,1536]{1,0:T(8,128)(2,1)S(1)} %collective-permute-done.9.refs_10_), channel_id=1, source_target_pairs={{0,4},{4,8},{8,12},{12,14},{14,10},{10,6},{6,2},{2,0},{5,1},{9,5},... | collective-permute-start | bytes 1400840 | tf_op jit(solution)/shard_map/ppermute | solution.py:229
  38.4 0.0 collective-permute-done.4.refs_5_
  38.4 0.3 place_p.1.panel
  38.8 5.0 %lower.1.so_far = f32[1024,1536]{1,0:T(8,128)S(1)} custom-call(bf16[1024,1536]{1,0:T(8,128)(2,1)S(1)} %copy-done, bf16[1536,1536]{1,0:T(8,128)(2,1)S(1)} %place_p.1.panel), custom_call_target="tpu_custom_call" | custom-call | flops 96636764160 | bytes 14155776 | tf_op jit(solution)/shard_map/lower/pallas_call | solution.py:167
  43.8 1.1 %collective-permute-done.13.refs_0_.refs_2_ = bf16[152,1536]{1,0:T(8,128)(2,1)S(1)} collective-permute-done((bf16[152,1536]{1,0:T(8,128)(2,1)S(1)}, bf16[152,1536]{1,0:T(8,128)(2,1)S(1)}, u32[]{:S(2)}, u32[]{:S(2)}) %collective-permute-start.13) | collective-permute-done | bytes 466976 | tf_op jit(solution)/shard_map/ppermute | solution.py:229
  44.9 0.2 place_r.1.refs_4_
  45.1 0.0 copy-start.1
  45.1 1.6 %collective-permute-done.14.refs_1_.refs_3_ = bf16[152,1536]{1,0:T(8,128)(2,1)S(1)} collective-permute-done((bf16[152,1536]{1,0:T(8,128)(2,1)S(1)}, bf16[152,1536]{1,0:T(8,128)(2,1)S(1)}, u32[]{:S(2)}, u32[]{:S(2)}) %collective-permute-start.14) | collective-permute-done | bytes 466976 | tf_op jit(solution)/shard_map/ppermute | solution.py:230
  46.7 0.1 opposite.1
  46.9 5.0 %finish.1 = (bf16[1024,1536]{1,0:T(8,128)(2,1)}, bf16[1024,896]{1,0:T(8,128)(2,1)}) custom-call(f32[1024,1536]{1,0:T(8,128)S(1)} %lower.1.so_far, bf16[1024,1536]{1,0:T(8,128)(2,1)S(1)} %copy-done, bf16[256,1536]{1,0:T(8,128)(2,1)S(1)} %get-tuple-element.6.window, bf16[896,1536]{1,0:T(8,128)(2,1)S(1)} %get-tuple-element.7.panel, bf16[1024,896]{1,0:T(8,128)(2,1)S(1)} %copy-done.1), custom_call_target="tpu_custom_call" | custom-call | flops 3623878656 | bytes 19005440 | tf_op jit(solution)/shard_map/finish/pallas_call | solution.py:206
  (8 shorter events, 0.0 us)
Async XLA Ops:
  1.7 37.1 %copy-start = (bf16[1024,1536]{1,0:T(8,128)(2,1)S(1)}, bf16[1024,1536]{1,0:T(8,128)(2,1)}, u32[]{:S(2)}) copy-start(bf16[1024,1536]{1,0:T(8,128)(2,1)} %column.3) | copy-start | bytes 9437188
  1.7 3.2 %collective-permute-start = (bf16[152,1536]{1,0:T(8,128)(2,1)S(1)}, bf16[152,1536]{1,0:T(8,128)(2,1)S(1)}, u32[]{:S(2)}, u32[]{:S(2)}) collective-permute-start(bf16[152,1536]{1,0:T(8,128)(2,1)S(1)} %load.1.refs_0_), channel_id=1, source_target_pairs={{0,1},{1,0},{2,3},{3,2},{4,5},{5,4},{6,7},{7,6},{8,9},{9,8},{10,11... | collective-permute-start | bytes 1400840 | tf_op jit(solution)/shard_map/ppermute | solution.py:230
  2.2 9.1 %collective-permute-start.1 = (bf16[152,1536]{1,0:T(8,128)(2,1)S(1)}, bf16[152,1536]{1,0:T(8,128)(2,1)S(1)}, u32[]{:S(2)}, u32[]{:S(2)}) collective-permute-start(bf16[152,1536]{1,0:T(8,128)(2,1)S(1)} %load.1.refs_0_), channel_id=1, source_target_pairs={{0,4},{4,8},{8,12},{12,14},{14,10},{10,6},{6,2},{2,0},{5,1},{9,5},... | collective-permute-start | bytes 1400840 | tf_op jit(solution)/shard_map/ppermute | solution.py:229
  4.8 11.5 %collective-permute-start.3 = (bf16[152,1536]{1,0:T(8,128)(2,1)S(1)}, bf16[152,1536]{1,0:T(8,128)(2,1)S(1)}, u32[]{:S(2)}, u32[]{:S(2)}) collective-permute-start(bf16[152,1536]{1,0:T(8,128)(2,1)S(1)} %collective-permute-done.refs_1_), channel_id=1, source_target_pairs={{0,4},{4,8},{8,12},{12,14},{14,10},{10,6},{6,2},{2,0},{5,1},{9,5},... | collective-permute-start | bytes 1400840 | tf_op jit(solution)/shard_map/ppermute | solution.py:229
  11.3 10.0 %collective-permute-start.5 = (bf16[152,1536]{1,0:T(8,128)(2,1)S(1)}, bf16[152,1536]{1,0:T(8,128)(2,1)S(1)}, u32[]{:S(2)}, u32[]{:S(2)}) collective-permute-start(bf16[152,1536]{1,0:T(8,128)(2,1)S(1)} %collective-permute-done.1.refs_2_), channel_id=1, source_target_pairs={{0,4},{4,8},{8,12},{12,14},{14,10},{10,6},{6,2},{2,0},{5,1},{9,5},... | collective-permute-start | bytes 1400840 | tf_op jit(solution)/shard_map/ppermute | solution.py:229
  16.3 10.0 %collective-permute-start.7 = (bf16[152,1536]{1,0:T(8,128)(2,1)S(1)}, bf16[152,1536]{1,0:T(8,128)(2,1)S(1)}, u32[]{:S(2)}, u32[]{:S(2)}) collective-permute-start(bf16[152,1536]{1,0:T(8,128)(2,1)S(1)} %collective-permute-done.3.refs_4_), channel_id=1, source_target_pairs={{0,4},{4,8},{8,12},{12,14},{14,10},{10,6},{6,2},{2,0},{5,1},{9,5},... | collective-permute-start | bytes 1400840 | tf_op jit(solution)/shard_map/ppermute | solution.py:229
  18.4 10.5 %collective-permute-start.2 = (bf16[152,1536]{1,0:T(8,128)(2,1)S(1)}, bf16[152,1536]{1,0:T(8,128)(2,1)S(1)}, u32[]{:S(2)}, u32[]{:S(2)}) collective-permute-start(bf16[152,1536]{1,0:T(8,128)(2,1)S(1)} %collective-permute-done.1.refs_2_), channel_id=1, source_target_pairs={{0,1},{1,0},{2,3},{3,2},{4,5},{5,4},{6,7},{7,6},{8,9},{9,8},{10,11... | collective-permute-start | bytes 1400840 | tf_op jit(solution)/shard_map/ppermute | solution.py:230
  21.3 10.0 %collective-permute-start.9 = (bf16[152,1536]{1,0:T(8,128)(2,1)S(1)}, bf16[152,1536]{1,0:T(8,128)(2,1)S(1)}, u32[]{:S(2)}, u32[]{:S(2)}) collective-permute-start(bf16[152,1536]{1,0:T(8,128)(2,1)S(1)} %collective-permute-done.5.refs_6_), channel_id=1, source_target_pairs={{0,4},{4,8},{8,12},{12,14},{14,10},{10,6},{6,2},{2,0},{5,1},{9,5},... | collective-permute-start | bytes 1400840 | tf_op jit(solution)/shard_map/ppermute | solution.py:229
  26.3 10.0 %collective-permute-start.11 = (bf16[152,1536]{1,0:T(8,128)(2,1)S(1)}, bf16[152,1536]{1,0:T(8,128)(2,1)S(1)}, u32[]{:S(2)}, u32[]{:S(2)}) collective-permute-start(bf16[152,1536]{1,0:T(8,128)(2,1)S(1)} %collective-permute-done.7.refs_8_), channel_id=1, source_target_pairs={{0,4},{4,8},{8,12},{12,14},{14,10},{10,6},{6,2},{2,0},{5,1},{9,5},... | collective-permute-start | bytes 1400840 | tf_op jit(solution)/shard_map/ppermute | solution.py:229
  28.4 7.9 %collective-permute-start.6 = (bf16[152,1536]{1,0:T(8,128)(2,1)S(1)}, bf16[152,1536]{1,0:T(8,128)(2,1)S(1)}, u32[]{:S(2)}, u32[]{:S(2)}) collective-permute-start(bf16[152,1536]{1,0:T(8,128)(2,1)S(1)} %collective-permute-done.5.refs_6_), channel_id=1, source_target_pairs={{0,1},{1,0},{2,3},{3,2},{4,5},{5,4},{6,7},{7,6},{8,9},{9,8},{10,11... | collective-permute-start | bytes 1400840 | tf_op jit(solution)/shard_map/ppermute | solution.py:230
  28.4 10.0 %collective-permute-start.4 = (bf16[152,1536]{1,0:T(8,128)(2,1)S(1)}, bf16[152,1536]{1,0:T(8,128)(2,1)S(1)}, u32[]{:S(2)}, u32[]{:S(2)}) collective-permute-start(bf16[152,1536]{1,0:T(8,128)(2,1)S(1)} %collective-permute-done.3.refs_4_), channel_id=1, source_target_pairs={{0,1},{1,0},{2,3},{3,2},{4,5},{5,4},{6,7},{7,6},{8,9},{9,8},{10,11... | collective-permute-start | bytes 1400840 | tf_op jit(solution)/shard_map/ppermute | solution.py:230
  28.9 9.5 %collective-permute-start.8 = (bf16[152,1536]{1,0:T(8,128)(2,1)S(1)}, bf16[152,1536]{1,0:T(8,128)(2,1)S(1)}, u32[]{:S(2)}, u32[]{:S(2)}) collective-permute-start(bf16[152,1536]{1,0:T(8,128)(2,1)S(1)} %collective-permute-done.7.refs_8_), channel_id=1, source_target_pairs={{0,1},{1,0},{2,3},{3,2},{4,5},{5,4},{6,7},{7,6},{8,9},{9,8},{10,11... | collective-permute-start | bytes 1400840 | tf_op jit(solution)/shard_map/ppermute | solution.py:230
  31.3 7.1 %collective-permute-start.10 = (bf16[152,1536]{1,0:T(8,128)(2,1)S(1)}, bf16[152,1536]{1,0:T(8,128)(2,1)S(1)}, u32[]{:S(2)}, u32[]{:S(2)}) collective-permute-start(bf16[152,1536]{1,0:T(8,128)(2,1)S(1)} %collective-permute-done.9.refs_10_), channel_id=1, source_target_pairs={{0,1},{1,0},{2,3},{3,2},{4,5},{5,4},{6,7},{7,6},{8,9},{9,8},{10,11... | collective-permute-start | bytes 1400840 | tf_op jit(solution)/shard_map/ppermute | solution.py:230
  36.3 2.1 %collective-permute-start.12 = (bf16[152,1536]{1,0:T(8,128)(2,1)S(1)}, bf16[152,1536]{1,0:T(8,128)(2,1)S(1)}, u32[]{:S(2)}, u32[]{:S(2)}) collective-permute-start(bf16[152,1536]{1,0:T(8,128)(2,1)S(1)} %collective-permute-done.11.refs_12_), channel_id=1, source_target_pairs={{0,1},{1,0},{2,3},{3,2},{4,5},{5,4},{6,7},{7,6},{8,9},{9,8},{10,11... | collective-permute-start | bytes 1400840 | tf_op jit(solution)/shard_map/ppermute | solution.py:230
  36.3 8.6 %collective-permute-start.13 = (bf16[152,1536]{1,0:T(8,128)(2,1)S(1)}, bf16[152,1536]{1,0:T(8,128)(2,1)S(1)}, u32[]{:S(2)}, u32[]{:S(2)}) collective-permute-start(bf16[152,1536]{1,0:T(8,128)(2,1)S(1)} %collective-permute-done.9.refs_10_), channel_id=1, source_target_pairs={{0,4},{4,8},{8,12},{12,14},{14,10},{10,6},{6,2},{2,0},{5,1},{9,5},... | collective-permute-start | bytes 1400840 | tf_op jit(solution)/shard_map/ppermute | solution.py:229
  44.9 1.8 %collective-permute-start.14 = (bf16[152,1536]{1,0:T(8,128)(2,1)S(1)}, bf16[152,1536]{1,0:T(8,128)(2,1)S(1)}, u32[]{:S(2)}, u32[]{:S(2)}) collective-permute-start(bf16[152,1536]{1,0:T(8,128)(2,1)S(1)} %collective-permute-done.13.refs_0_.refs_2_), channel_id=1, source_target_pairs={{0,1},{1,0},{2,3},{3,2},{4,5},{5,4},{6,7},{7,6},{8,9},{9,8},{10,11... | collective-permute-start | bytes 1400840 | tf_op jit(solution)/shard_map/ppermute | solution.py:230
  45.1 1.8 %copy-start.1 = (bf16[1024,896]{1,0:T(8,128)(2,1)S(1)}, bf16[1024,896]{1,0:T(8,128)(2,1)}, u32[]{:S(2)}) copy-start(bf16[1024,896]{1,0:T(8,128)(2,1)} %coupling.1) | copy-start | bytes 5505028

commit v6 on v5

--- a/solution.py
+++ b/solution.py
@@ -186,6 +186,8 @@
         lower_done[at] = (so_far[at] + rest).astype(BF16)
         copies.append(pltpu.make_async_copy(lower_done.at[at], lower_out.at[at], sems.at[0, i]))
         copies[-1].start()
+    for i in range(CHUNKS):
+        at = pl.ds(i * rows, rows)
         cols = out.shape[1]
         cuts = [0, (cols // 2 + 127) // 256 * 256, cols] if i == CHUNKS - 1 else [0, cols]
         for j, (low, high) in enumerate(zip(cuts, cuts[1:])):

time: 52.1 us -> 52.1 us (level)
  no operation moved by 1% of the time
where the time goes in v6:
time: 52.1 us; the launch traced here: 52 us
  waiting for transfers between devices  23.6 us (45%)
  starting transfers between devices  15.8 us (30%)
  Pallas kernels  11.8 us (23%)
  between operations  0.72 us (1%)
    ppermute x7, waiting for transfers between devices, on_device(): on = lambda x: lax.ppermute(x, 'row', along)  22 us
    ppermute x7, starting transfers between devices, on_device(): on = lambda x: lax.ppermute(x, 'row', along)  14.8 us
    pallas_call x1, Pallas kernels, finish(): pl.pallas_call(functools.partial(finish_kernel, p_rows, chips), out_shape...  5.11 us
    pallas_call x1, Pallas kernels, lower(): pl.pallas_call(lower_kernel, out_shape=jax.ShapeDtypeStruct((n, panel.sha...  5.03 us
    ppermute x8, waiting for transfers between devices, on_device(): over = lambda x: lax.ppermute(x, 'row', swap)  1.62 us
    ppermute x8, starting transfers between devices, on_device(): over = lambda x: lax.ppermute(x, 'row', swap)  1.04 us
  transfers between devices with their start and end apart: 15, of which 8 were waited for; matrix products, arithmetic and copies ran while one was open for 0% of the time, Pallas kernels for 11%

profile of v6, /device:TPU:0, one launch (start us, length us, event | category | flops | bytes accessed | tf_op | source)
XLA Modules:
  0.0 52.0 jit_solution(11633634915045388231)
XLA Ops:
  0.6 1.0 %load.1.refs_0_ = bf16[152,1536]{1,0:T(8,128)(2,1)S(1)} custom-call(bf16[96,1536]{1,0:T(8,128)(2,1)} %inverse.1, bf16[56,1536]{1,0:T(8,128)(2,1)} %bitcast.1), custom_call_target="tpu_custom_call" | custom-call | tf_op jit(solution)/shard_map/load/pallas_call | solution.py:132
  1.7 0.0 copy-start
  1.7 0.5 collective-permute-start
  2.2 2.6 %collective-permute-start.1 = (bf16[152,1536]{1,0:T(8,128)(2,1)S(1)}, bf16[152,1536]{1,0:T(8,128)(2,1)S(1)}, u32[]{:S(2)}, u32[]{:S(2)}) collective-permute-start(bf16[152,1536]{1,0:T(8,128)(2,1)S(1)} %load.1.refs_0_), channel_id=1, source_target_pairs={{0,4},{4,8},{8,12},{12,14},{14,10},{10,6},{6,2},{2,0},{5,1},{9,5},... | collective-permute-start | bytes 1400840 | tf_op jit(solution)/shard_map/ppermute | solution.py:231
  4.8 0.0 collective-permute-done.refs_1_
  4.8 1.8 %collective-permute-start.3 = (bf16[152,1536]{1,0:T(8,128)(2,1)S(1)}, bf16[152,1536]{1,0:T(8,128)(2,1)S(1)}, u32[]{:S(2)}, u32[]{:S(2)}) collective-permute-start(bf16[152,1536]{1,0:T(8,128)(2,1)S(1)} %collective-permute-done.refs_1_), channel_id=1, source_target_pairs={{0,4},{4,8},{8,12},{12,14},{14,10},{10,6},{6,2},{2,0},{5,1},{9,5},... | collective-permute-start | bytes 1400840 | tf_op jit(solution)/shard_map/ppermute | solution.py:231
  6.6 4.7 %collective-permute-done.1.refs_2_ = bf16[152,1536]{1,0:T(8,128)(2,1)S(1)} collective-permute-done((bf16[152,1536]{1,0:T(8,128)(2,1)S(1)}, bf16[152,1536]{1,0:T(8,128)(2,1)S(1)}, u32[]{:S(2)}, u32[]{:S(2)}) %collective-permute-start.1) | collective-permute-done | bytes 466976 | tf_op jit(solution)/shard_map/ppermute | solution.py:231
  11.3 2.1 %collective-permute-start.5 = (bf16[152,1536]{1,0:T(8,128)(2,1)S(1)}, bf16[152,1536]{1,0:T(8,128)(2,1)S(1)}, u32[]{:S(2)}, u32[]{:S(2)}) collective-permute-start(bf16[152,1536]{1,0:T(8,128)(2,1)S(1)} %collective-permute-done.1.refs_2_), channel_id=1, source_target_pairs={{0,4},{4,8},{8,12},{12,14},{14,10},{10,6},{6,2},{2,0},{5,1},{9,5},... | collective-permute-start | bytes 1400840 | tf_op jit(solution)/shard_map/ppermute | solution.py:231
  13.4 2.9 %collective-permute-done.3.refs_4_ = bf16[152,1536]{1,0:T(8,128)(2,1)S(1)} collective-permute-done((bf16[152,1536]{1,0:T(8,128)(2,1)S(1)}, bf16[152,1536]{1,0:T(8,128)(2,1)S(1)}, u32[]{:S(2)}, u32[]{:S(2)}) %collective-permute-start.3) | collective-permute-done | bytes 466976 | tf_op jit(solution)/shard_map/ppermute | solution.py:231
  16.3 2.1 %collective-permute-start.7 = (bf16[152,1536]{1,0:T(8,128)(2,1)S(1)}, bf16[152,1536]{1,0:T(8,128)(2,1)S(1)}, u32[]{:S(2)}, u32[]{:S(2)}) collective-permute-start(bf16[152,1536]{1,0:T(8,128)(2,1)S(1)} %collective-permute-done.3.refs_4_), channel_id=1, source_target_pairs={{0,4},{4,8},{8,12},{12,14},{14,10},{10,6},{6,2},{2,0},{5,1},{9,5},... | collective-permute-start | bytes 1400840 | tf_op jit(solution)/shard_map/ppermute | solution.py:231
  18.4 0.0 collective-permute-start.2
  18.4 2.9 %collective-permute-done.5.refs_6_ = bf16[152,1536]{1,0:T(8,128)(2,1)S(1)} collective-permute-done((bf16[152,1536]{1,0:T(8,128)(2,1)S(1)}, bf16[152,1536]{1,0:T(8,128)(2,1)S(1)}, u32[]{:S(2)}, u32[]{:S(2)}) %collective-permute-start.5) | collective-permute-done | bytes 466976 | tf_op jit(solution)/shard_map/ppermute | solution.py:231
  21.3 2.1 %collective-permute-start.9 = (bf16[152,1536]{1,0:T(8,128)(2,1)S(1)}, bf16[152,1536]{1,0:T(8,128)(2,1)S(1)}, u32[]{:S(2)}, u32[]{:S(2)}) collective-permute-start(bf16[152,1536]{1,0:T(8,128)(2,1)S(1)} %collective-permute-done.5.refs_6_), channel_id=1, source_target_pairs={{0,4},{4,8},{8,12},{12,14},{14,10},{10,6},{6,2},{2,0},{5,1},{9,5},... | collective-permute-start | bytes 1400840 | tf_op jit(solution)/shard_map/ppermute | solution.py:231
  23.4 2.9 %collective-permute-done.7.refs_8_ = bf16[152,1536]{1,0:T(8,128)(2,1)S(1)} collective-permute-done((bf16[152,1536]{1,0:T(8,128)(2,1)S(1)}, bf16[152,1536]{1,0:T(8,128)(2,1)S(1)}, u32[]{:S(2)}, u32[]{:S(2)}) %collective-permute-start.7) | collective-permute-done | bytes 466976 | tf_op jit(solution)/shard_map/ppermute | solution.py:231
  26.3 2.1 %collective-permute-start.11 = (bf16[152,1536]{1,0:T(8,128)(2,1)S(1)}, bf16[152,1536]{1,0:T(8,128)(2,1)S(1)}, u32[]{:S(2)}, u32[]{:S(2)}) collective-permute-start(bf16[152,1536]{1,0:T(8,128)(2,1)S(1)} %collective-permute-done.7.refs_8_), channel_id=1, source_target_pairs={{0,4},{4,8},{8,12},{12,14},{14,10},{10,6},{6,2},{2,0},{5,1},{9,5},... | collective-permute-start | bytes 1400840 | tf_op jit(solution)/shard_map/ppermute | solution.py:231
  28.4 0.0 collective-permute-start.6
  28.4 0.5 collective-permute-start.4
  28.9 0.0 collective-permute-start.8
  28.9 2.4 %collective-permute-done.9.refs_10_ = bf16[152,1536]{1,0:T(8,128)(2,1)S(1)} collective-permute-done((bf16[152,1536]{1,0:T(8,128)(2,1)S(1)}, bf16[152,1536]{1,0:T(8,128)(2,1)S(1)}, u32[]{:S(2)}, u32[]{:S(2)}) %collective-permute-start.9) | collective-permute-done | bytes 466976 | tf_op jit(solution)/shard_map/ppermute | solution.py:231
  31.3 5.0 %collective-permute-done.11.refs_12_ = bf16[152,1536]{1,0:T(8,128)(2,1)S(1)} collective-permute-done((bf16[152,1536]{1,0:T(8,128)(2,1)S(1)}, bf16[152,1536]{1,0:T(8,128)(2,1)S(1)}, u32[]{:S(2)}, u32[]{:S(2)}) %collective-permute-start.11) | collective-permute-done | bytes 466976 | tf_op jit(solution)/shard_map/ppermute | solution.py:231
  36.3 0.0 collective-permute-start.12
  36.3 2.1 %collective-permute-start.13 = (bf16[152,1536]{1,0:T(8,128)(2,1)S(1)}, bf16[152,1536]{1,0:T(8,128)(2,1)S(1)}, u32[]{:S(2)}, u32[]{:S(2)}) collective-permute-start(bf16[152,1536]{1,0:T(8,128)(2,1)S(1)} %collective-permute-done.9.refs_10_), channel_id=1, source_target_pairs={{0,4},{4,8},{8,12},{12,14},{14,10},{10,6},{6,2},{2,0},{5,1},{9,5},... | collective-permute-start | bytes 1400840 | tf_op jit(solution)/shard_map/ppermute | solution.py:231
  38.4 0.0 collective-permute-done.4.refs_5_
  38.4 0.0 collective-permute-done.10.refs_11_
  38.4 0.3 place_p.1.panel
  38.8 5.0 %lower.1.so_far = f32[1024,1536]{1,0:T(8,128)S(1)} custom-call(bf16[1024,1536]{1,0:T(8,128)(2,1)S(1)} %copy-done, bf16[1536,1536]{1,0:T(8,128)(2,1)S(1)} %place_p.1.panel), custom_call_target="tpu_custom_call" | custom-call | flops 96636764160 | bytes 14155776 | tf_op jit(solution)/shard_map/lower/pallas_call | solution.py:167
  43.8 1.1 %collective-permute-done.13.refs_0_.refs_2_ = bf16[152,1536]{1,0:T(8,128)(2,1)S(1)} collective-permute-done((bf16[152,1536]{1,0:T(8,128)(2,1)S(1)}, bf16[152,1536]{1,0:T(8,128)(2,1)S(1)}, u32[]{:S(2)}, u32[]{:S(2)}) %collective-permute-start.13) | collective-permute-done | bytes 466976 | tf_op jit(solution)/shard_map/ppermute | solution.py:231
  44.9 0.2 place_r.1.refs_4_
  45.1 0.0 copy-start.1
  45.1 1.6 %collective-permute-done.14.refs_1_.refs_3_ = bf16[152,1536]{1,0:T(8,128)(2,1)S(1)} collective-permute-done((bf16[152,1536]{1,0:T(8,128)(2,1)S(1)}, bf16[152,1536]{1,0:T(8,128)(2,1)S(1)}, u32[]{:S(2)}, u32[]{:S(2)}) %collective-permute-start.14) | collective-permute-done | bytes 466976 | tf_op jit(solution)/shard_map/ppermute | solution.py:232
  46.7 0.1 opposite.1
  46.9 5.1 %finish.1 = (bf16[1024,1536]{1,0:T(8,128)(2,1)}, bf16[1024,896]{1,0:T(8,128)(2,1)}) custom-call(f32[1024,1536]{1,0:T(8,128)S(1)} %lower.1.so_far, bf16[1024,1536]{1,0:T(8,128)(2,1)S(1)} %copy-done, bf16[256,1536]{1,0:T(8,128)(2,1)S(1)} %get-tuple-element.6.window, bf16[896,1536]{1,0:T(8,128)(2,1)S(1)} %get-tuple-element.7.panel, bf16[1024,896]{1,0:T(8,128)(2,1)S(1)} %copy-done.1), custom_call_target="tpu_custom_call" | custom-call | flops 3623878656 | bytes 19005440 | tf_op jit(solution)/shard_map/finish/pallas_call | solution.py:208
  (8 shorter events, 0.0 us)
Async XLA Ops:
  1.7 37.1 %copy-start = (bf16[1024,1536]{1,0:T(8,128)(2,1)S(1)}, bf16[1024,1536]{1,0:T(8,128)(2,1)}, u32[]{:S(2)}) copy-start(bf16[1024,1536]{1,0:T(8,128)(2,1)} %column.3) | copy-start | bytes 9437188
  1.7 3.2 %collective-permute-start = (bf16[152,1536]{1,0:T(8,128)(2,1)S(1)}, bf16[152,1536]{1,0:T(8,128)(2,1)S(1)}, u32[]{:S(2)}, u32[]{:S(2)}) collective-permute-start(bf16[152,1536]{1,0:T(8,128)(2,1)S(1)} %load.1.refs_0_), channel_id=1, source_target_pairs={{0,1},{1,0},{2,3},{3,2},{4,5},{5,4},{6,7},{7,6},{8,9},{9,8},{10,11... | collective-permute-start | bytes 1400840 | tf_op jit(solution)/shard_map/ppermute | solution.py:232
  2.2 9.1 %collective-permute-start.1 = (bf16[152,1536]{1,0:T(8,128)(2,1)S(1)}, bf16[152,1536]{1,0:T(8,128)(2,1)S(1)}, u32[]{:S(2)}, u32[]{:S(2)}) collective-permute-start(bf16[152,1536]{1,0:T(8,128)(2,1)S(1)} %load.1.refs_0_), channel_id=1, source_target_pairs={{0,4},{4,8},{8,12},{12,14},{14,10},{10,6},{6,2},{2,0},{5,1},{9,5},... | collective-permute-start | bytes 1400840 | tf_op jit(solution)/shard_map/ppermute | solution.py:231
  4.8 11.5 %collective-permute-start.3 = (bf16[152,1536]{1,0:T(8,128)(2,1)S(1)}, bf16[152,1536]{1,0:T(8,128)(2,1)S(1)}, u32[]{:S(2)}, u32[]{:S(2)}) collective-permute-start(bf16[152,1536]{1,0:T(8,128)(2,1)S(1)} %collective-permute-done.refs_1_), channel_id=1, source_target_pairs={{0,4},{4,8},{8,12},{12,14},{14,10},{10,6},{6,2},{2,0},{5,1},{9,5},... | collective-permute-start | bytes 1400840 | tf_op jit(solution)/shard_map/ppermute | solution.py:231
  11.3 10.0 %collective-permute-start.5 = (bf16[152,1536]{1,0:T(8,128)(2,1)S(1)}, bf16[152,1536]{1,0:T(8,128)(2,1)S(1)}, u32[]{:S(2)}, u32[]{:S(2)}) collective-permute-start(bf16[152,1536]{1,0:T(8,128)(2,1)S(1)} %collective-permute-done.1.refs_2_), channel_id=1, source_target_pairs={{0,4},{4,8},{8,12},{12,14},{14,10},{10,6},{6,2},{2,0},{5,1},{9,5},... | collective-permute-start | bytes 1400840 | tf_op jit(solution)/shard_map/ppermute | solution.py:231
  16.3 10.0 %collective-permute-start.7 = (bf16[152,1536]{1,0:T(8,128)(2,1)S(1)}, bf16[152,1536]{1,0:T(8,128)(2,1)S(1)}, u32[]{:S(2)}, u32[]{:S(2)}) collective-permute-start(bf16[152,1536]{1,0:T(8,128)(2,1)S(1)} %collective-permute-done.3.refs_4_), channel_id=1, source_target_pairs={{0,4},{4,8},{8,12},{12,14},{14,10},{10,6},{6,2},{2,0},{5,1},{9,5},... | collective-permute-start | bytes 1400840 | tf_op jit(solution)/shard_map/ppermute | solution.py:231
  18.4 10.5 %collective-permute-start.2 = (bf16[152,1536]{1,0:T(8,128)(2,1)S(1)}, bf16[152,1536]{1,0:T(8,128)(2,1)S(1)}, u32[]{:S(2)}, u32[]{:S(2)}) collective-permute-start(bf16[152,1536]{1,0:T(8,128)(2,1)S(1)} %collective-permute-done.1.refs_2_), channel_id=1, source_target_pairs={{0,1},{1,0},{2,3},{3,2},{4,5},{5,4},{6,7},{7,6},{8,9},{9,8},{10,11... | collective-permute-start | bytes 1400840 | tf_op jit(solution)/shard_map/ppermute | solution.py:232
  21.3 10.0 %collective-permute-start.9 = (bf16[152,1536]{1,0:T(8,128)(2,1)S(1)}, bf16[152,1536]{1,0:T(8,128)(2,1)S(1)}, u32[]{:S(2)}, u32[]{:S(2)}) collective-permute-start(bf16[152,1536]{1,0:T(8,128)(2,1)S(1)} %collective-permute-done.5.refs_6_), channel_id=1, source_target_pairs={{0,4},{4,8},{8,12},{12,14},{14,10},{10,6},{6,2},{2,0},{5,1},{9,5},... | collective-permute-start | bytes 1400840 | tf_op jit(solution)/shard_map/ppermute | solution.py:231
  26.3 10.0 %collective-permute-start.11 = (bf16[152,1536]{1,0:T(8,128)(2,1)S(1)}, bf16[152,1536]{1,0:T(8,128)(2,1)S(1)}, u32[]{:S(2)}, u32[]{:S(2)}) collective-permute-start(bf16[152,1536]{1,0:T(8,128)(2,1)S(1)} %collective-permute-done.7.refs_8_), channel_id=1, source_target_pairs={{0,4},{4,8},{8,12},{12,14},{14,10},{10,6},{6,2},{2,0},{5,1},{9,5},... | collective-permute-start | bytes 1400840 | tf_op jit(solution)/shard_map/ppermute | solution.py:231
  28.4 7.9 %collective-permute-start.6 = (bf16[152,1536]{1,0:T(8,128)(2,1)S(1)}, bf16[152,1536]{1,0:T(8,128)(2,1)S(1)}, u32[]{:S(2)}, u32[]{:S(2)}) collective-permute-start(bf16[152,1536]{1,0:T(8,128)(2,1)S(1)} %collective-permute-done.5.refs_6_), channel_id=1, source_target_pairs={{0,1},{1,0},{2,3},{3,2},{4,5},{5,4},{6,7},{7,6},{8,9},{9,8},{10,11... | collective-permute-start | bytes 1400840 | tf_op jit(solution)/shard_map/ppermute | solution.py:232
  28.4 10.0 %collective-permute-start.4 = (bf16[152,1536]{1,0:T(8,128)(2,1)S(1)}, bf16[152,1536]{1,0:T(8,128)(2,1)S(1)}, u32[]{:S(2)}, u32[]{:S(2)}) collective-permute-start(bf16[152,1536]{1,0:T(8,128)(2,1)S(1)} %collective-permute-done.3.refs_4_), channel_id=1, source_target_pairs={{0,1},{1,0},{2,3},{3,2},{4,5},{5,4},{6,7},{7,6},{8,9},{9,8},{10,11... | collective-permute-start | bytes 1400840 | tf_op jit(solution)/shard_map/ppermute | solution.py:232
  28.9 9.5 %collective-permute-start.8 = (bf16[152,1536]{1,0:T(8,128)(2,1)S(1)}, bf16[152,1536]{1,0:T(8,128)(2,1)S(1)}, u32[]{:S(2)}, u32[]{:S(2)}) collective-permute-start(bf16[152,1536]{1,0:T(8,128)(2,1)S(1)} %collective-permute-done.7.refs_8_), channel_id=1, source_target_pairs={{0,1},{1,0},{2,3},{3,2},{4,5},{5,4},{6,7},{7,6},{8,9},{9,8},{10,11... | collective-permute-start | bytes 1400840 | tf_op jit(solution)/shard_map/ppermute | solution.py:232
  31.3 7.1 %collective-permute-start.10 = (bf16[152,1536]{1,0:T(8,128)(2,1)S(1)}, bf16[152,1536]{1,0:T(8,128)(2,1)S(1)}, u32[]{:S(2)}, u32[]{:S(2)}) collective-permute-start(bf16[152,1536]{1,0:T(8,128)(2,1)S(1)} %collective-permute-done.9.refs_10_), channel_id=1, source_target_pairs={{0,1},{1,0},{2,3},{3,2},{4,5},{5,4},{6,7},{7,6},{8,9},{9,8},{10,11... | collective-permute-start | bytes 1400840 | tf_op jit(solution)/shard_map/ppermute | solution.py:232
  36.3 2.1 %collective-permute-start.12 = (bf16[152,1536]{1,0:T(8,128)(2,1)S(1)}, bf16[152,1536]{1,0:T(8,128)(2,1)S(1)}, u32[]{:S(2)}, u32[]{:S(2)}) collective-permute-start(bf16[152,1536]{1,0:T(8,128)(2,1)S(1)} %collective-permute-done.11.refs_12_), channel_id=1, source_target_pairs={{0,1},{1,0},{2,3},{3,2},{4,5},{5,4},{6,7},{7,6},{8,9},{9,8},{10,11... | collective-permute-start | bytes 1400840 | tf_op jit(solution)/shard_map/ppermute | solution.py:232
  36.3 8.6 %collective-permute-start.13 = (bf16[152,1536]{1,0:T(8,128)(2,1)S(1)}, bf16[152,1536]{1,0:T(8,128)(2,1)S(1)}, u32[]{:S(2)}, u32[]{:S(2)}) collective-permute-start(bf16[152,1536]{1,0:T(8,128)(2,1)S(1)} %collective-permute-done.9.refs_10_), channel_id=1, source_target_pairs={{0,4},{4,8},{8,12},{12,14},{14,10},{10,6},{6,2},{2,0},{5,1},{9,5},... | collective-permute-start | bytes 1400840 | tf_op jit(solution)/shard_map/ppermute | solution.py:231
  44.9 1.8 %collective-permute-start.14 = (bf16[152,1536]{1,0:T(8,128)(2,1)S(1)}, bf16[152,1536]{1,0:T(8,128)(2,1)S(1)}, u32[]{:S(2)}, u32[]{:S(2)}) collective-permute-start(bf16[152,1536]{1,0:T(8,128)(2,1)S(1)} %collective-permute-done.13.refs_0_.refs_2_), channel_id=1, source_target_pairs={{0,1},{1,0},{2,3},{3,2},{4,5},{5,4},{6,7},{7,6},{8,9},{9,8},{10,11... | collective-permute-start | bytes 1400840 | tf_op jit(solution)/shard_map/ppermute | solution.py:232
  45.1 1.8 %copy-start.1 = (bf16[1024,896]{1,0:T(8,128)(2,1)S(1)}, bf16[1024,896]{1,0:T(8,128)(2,1)}, u32[]{:S(2)}) copy-start(bf16[1024,896]{1,0:T(8,128)(2,1)} %coupling.1) | copy-start | bytes 5505028
